TPU v7x, 32 devices: a whole 2x2x4 slice. The times are simulated.
32 devices in a mesh: groups: 2 (over x), seq: 16 (over z, y, core).
Axes of the slice: x: 2, y: 2, z: 4, core: 2. Of those that a mesh axis runs over, the one named last changes fastest.
Arguments:
- features: bfloat16 [3, 4096, 4096], P(None, ('groups', 'seq')), parts along dimension 1, may hold values from -6 to 6
- kernel: float32 [3, 3, 4096], replicated, may hold values from -3.5 to 3.5
- skip: float32 [4096], replicated, may hold values from -4 to 4
- residues: float32 [2, 16, 4096], replicated, may hold values from -3 to 3
- decay: float32 [16, 4096], replicated, may hold values from 9.765625e-05 to 0.041666667
- freq: float32 [16, 4096], replicated, may hold values from 0.001 to 0.5
- lengths: int32 [12], P('groups'), parts along dimension 0, may hold values from 1 to 1024, 2048 in all
Outputs:
- mixed: bfloat16 [4096, 4096], P(('groups', 'seq')), parts along dimension 0
There are 2 independent parts, one for each index of `groups`. A program takes and returns all parts, laid end to end along the dimension named above; an argument that names none is the same for every part. Nothing has to cross between parts.
Inputs may be any that keep to these rules, and one draw needn't show every extreme that they name: The lengths sum to 2048; the longest is exactly 1024.
All inputs are finite; a program needn't handle non-finite values.
Results may differ from a plain program's by a relative error of at most 0.0065.
Values may be sent and summed in bfloat16 or wider, within the bound.
No kernel may reach another device: no remote copies, remote signals or barrier semaphores. Data moves between devices by JAX's collectives and lax.ppermute only.
A program may use at most 192 MiB of HBM per device.

v0:
```python
import jax
import jax.numpy as jnp
from jax import lax
from jax.sharding import PartitionSpec as P

BLK = 16


def from_behind(block, axis, distance):
    devices = range(lax.axis_size(axis))
    route = [(i - distance, i) for i in devices if i - distance in devices]
    return lax.ppermute(block, axis, route)


def entering(part, axis, combine, identity):
    place = lax.axis_index(axis)
    gathered = jax.tree.map(lambda a: lax.all_gather(a, axis), part)
    state = jax.tree.map(lambda a, e: jnp.zeros_like(a) + jnp.asarray(e, a.dtype), part, identity)

    def one(lap, state):
        return combine(
            state, jax.tree.map(lambda a: lax.dynamic_index_in_dim(a, lap, 0, False), gathered)
        )

    return lax.fori_loop(0, place, one, state)


def segment_ids(lengths, index):
    starts = jnp.cumsum(lengths, dtype=jnp.int32) - lengths
    return jnp.sum((starts[None, :] <= index[:, None]).astype(jnp.int32), axis=1) - 1


def short_conv(extended, seg_ext, kernel):
    values = extended.astype(jnp.float32)
    mask_one = (seg_ext[2:] == seg_ext[1:-1]).astype(jnp.float32)[None, :, None]
    mask_two = (seg_ext[2:] == seg_ext[:-2]).astype(jnp.float32)[None, :, None]
    conv = kernel[:, 0][:, None, :] * values[:, 2:]
    conv = conv + kernel[:, 1][:, None, :] * values[:, 1:-1] * mask_one
    conv = conv + kernel[:, 2][:, None, :] * values[:, :-2] * mask_two
    return ((conv[0] * conv[2]).astype(jnp.bfloat16), conv[1])


def mode_tables(decay, freq, residues):
    block_len = BLK
    steps = jnp.arange(block_len + 1, dtype=jnp.float32)[:, None, None]
    magnitude = jnp.exp(-decay[None] * steps)
    angle = freq[None] * steps
    pow_re = magnitude * jnp.cos(angle)
    pow_im = magnitude * jnp.sin(angle)
    scale = jnp.sqrt(-jnp.expm1(-2.0 * decay))
    coef_re = residues[0] * scale
    coef_im = residues[1] * scale
    filt = jnp.sum(
        coef_re[None] * pow_re[:block_len] - coef_im[None] * pow_im[:block_len], axis=1
    ).astype(jnp.bfloat16)
    lag = (
        jnp.arange(block_len, dtype=jnp.int32)[:, None]
        - jnp.arange(block_len, dtype=jnp.int32)[None, :]
    )
    toeplitz = jnp.where(
        (lag >= 0)[:, :, None], filt[jnp.clip(lag, 0, block_len - 1)], jnp.zeros((), jnp.bfloat16)
    )
    return (pow_re, pow_im, coef_re, coef_im, toeplitz)


def local_blocks(gated, seg_with_prev, tables):
    pow_re, pow_im, coef_re, coef_im, toeplitz = tables
    block_len = BLK
    count = gated.shape[0] // block_len
    blocks = gated.reshape(count, block_len, gated.shape[1])
    seg_blocks = seg_with_prev[1:].reshape(count, block_len)
    seg_before = seg_with_prev[:-1].reshape(count, block_len)[:, 0]
    toe_wide = toeplitz.astype(jnp.float32)

    def one_block(pair):
        values, segs = pair
        same = (segs[:, None] == segs[None, :]).astype(jnp.float32)
        return jnp.sum(toe_wide * same[:, :, None] * values.astype(jnp.float32)[None], axis=1)

    intra = lax.map(one_block, (blocks, seg_blocks))
    last_mask = (seg_blocks == seg_blocks[:, -1:]).astype(jnp.float32)
    weighted = blocks.astype(jnp.float32) * last_mask[:, :, None]
    e_re = jnp.sum(pow_re[:block_len][::-1][None] * weighted[:, :, None, :], axis=1)
    e_im = jnp.sum(pow_im[:block_len][::-1][None] * weighted[:, :, None, :], axis=1)
    flags = (seg_blocks[:, -1] == seg_before).astype(jnp.float32)
    first_mask = (seg_blocks == seg_before[:, None]).astype(jnp.float32)
    return (intra, e_re, e_im, first_mask, flags)


def run_chain(start_re, start_im, flags, gate_re, gate_im, e_re, e_im):

    def advance(carry, item):
        s_re, s_im = carry
        flag, b_re, b_im = item
        a_re = flag * gate_re
        a_im = flag * gate_im
        n_re = a_re * s_re - a_im * s_im + b_re
        n_im = a_re * s_im + a_im * s_re + b_im
        return ((n_re, n_im), (s_re, s_im))

    final, states = lax.scan(advance, (start_re, start_im), (flags, e_re, e_im))
    return (states[0], states[1], final[0], final[1])


def finish(intra, states_re, states_im, tables, first_mask, gated, other, skip):
    pow_re, pow_im, coef_re, coef_im, toeplitz = tables
    amp_re = coef_re[None] * states_re - coef_im[None] * states_im
    amp_im = coef_re[None] * states_im + coef_im[None] * states_re
    carried = jnp.sum(
        pow_re[1:][None] * amp_re[:, None] - pow_im[1:][None] * amp_im[:, None], axis=2
    )
    total = intra + carried * first_mask[:, :, None]
    total = total.reshape(gated.shape)
    return (other * (total + skip[None, :] * gated.astype(jnp.float32))).astype(jnp.bfloat16)


def combine_gates(earlier, later):
    ge_re, ge_im, be_re, be_im = earlier
    gl_re, gl_im, bl_re, bl_im = later
    g_re = gl_re * ge_re - gl_im * ge_im
    g_im = gl_re * ge_im + gl_im * ge_re
    b_re = bl_re + gl_re * be_re - gl_im * be_im
    b_im = bl_im + gl_re * be_im + gl_im * be_re
    return (g_re, g_im, b_re, b_im)


def per_device(features, kernel, skip, residues, decay, freq, lengths):
    tokens_here = features.shape[1]
    modes, width = decay.shape
    base = lax.axis_index("seq") * tokens_here
    rims = from_behind(features[:, tokens_here - 2 :, :], "seq", 1)
    extended = jnp.concatenate([rims, features], axis=1)
    index = base - 2 + jnp.arange(tokens_here + 2, dtype=jnp.int32)
    seg_ext = segment_ids(lengths, index)
    gated, other = short_conv(extended, seg_ext, kernel)
    tables = mode_tables(decay, freq, residues)
    pow_re, pow_im = (tables[0], tables[1])
    intra, e_re, e_im, first_mask, flags = local_blocks(gated, seg_ext[1:], tables)
    zero = jnp.zeros((modes, width), jnp.float32)
    gate_re = pow_re[-1]
    gate_im = pow_im[-1]
    _, _, end_re, end_im = run_chain(zero, zero, flags, gate_re, gate_im, e_re, e_im)
    flag_dev = jnp.prod(flags)
    span_f = jnp.asarray(tokens_here, jnp.float32)
    magnitude = flag_dev * jnp.exp(-decay * span_f)
    prod_re = magnitude * jnp.cos(freq * span_f)
    prod_im = magnitude * jnp.sin(freq * span_f)
    unity = jnp.ones((modes, width), jnp.float32)
    prefix = entering(
        (prod_re, prod_im, end_re, end_im), "seq", combine_gates, (unity, zero, zero, zero)
    )
    start_re = prefix[2]
    start_im = prefix[3]
    states_re, states_im, _, _ = run_chain(start_re, start_im, flags, gate_re, gate_im, e_re, e_im)
    return finish(intra, states_re, states_im, tables, first_mask, gated, other, skip)


def solution(mesh):
    return jax.shard_map(
        per_device,
        mesh=mesh,
        in_specs=(P(None, ("groups", "seq"), None), P(), P(), P(), P(), P(), P("groups")),
        out_specs=P(("groups", "seq"), None),
        check_vma=False,
    )
```

profile of v0, /device:TPU:29, one launch (start us, length us, event | category | flops | bytes accessed | tf_op | source)
XLA Modules:
  0.0 293.9 jit_solution(12465605578945067810)
XLA Ops:
  9.2 3.6 %sine_multiply_fusion.1 = (f32[16,4096]{1,0:T(8,128)}, f32[16,4096]{1,0:T(8,128)}, f32[16,4096]{1,0:T(8,128)S(1)}, f32[16,4096]{1,0:T(8,128)S(1)}, f32[16,4096]{1,0:T(8,128)S(1)}) fusion(f32[16,4096]{1,0:T(8,128)} %param.20, f32[]{:T(128)} %get-tuple-element.296, f32[16,4096]{1,0:T(8,128)} %param.19, f32[2,16,4096]{2,1,0:T(8,128)} %param.18), kind=kLoop, calls=%fused_computation.53 | loop fusion | flops 655360 | bytes 2359300 | tf_op jit(solution)/shard_map/mul | solution.py:147
  15.4 17.0 %cosine_multiply_fusion = (f32[17,16,4096]{2,1,0:T(8,128)S(1)}, f32[17,16,4096]{2,1,0:T(8,128)S(1)}) fusion(f32[16,4096]{1,0:T(8,128)} %param.20, f32[16,4096]{1,0:T(8,128)S(1)} %get-tuple-element.319), kind=kLoop, calls=%fused_computation.32 | loop fusion | flops 4456448 | bytes 9437184 | tf_op jit(solution)/shard_map/mul | solution.py:48
  32.7 6.4 %fusion.13 = (f32[16,16,4096]{2,1,0:T(8,128)}, bf16[16,4096]{1,0:T(8,128)(2,1)S(1)}, f32[16,16,4096]{2,1,0:T(8,128)}, f32[16,16,4096]{2,1,0:T(8,128)}, f32[16,16,4096]{2,1,0:T(8,128)}) fusion(f32[17,16,4096]{2,1,0:T(8,128)S(1)} %get-tuple-element.317, f32[17,16,4096]{2,1,0:T(8,128)S(1)} %get-tuple-element.318, f32[16,4096]{1,0:T(8,128)S(1)} %get-tuple-element.320, ...), kind=kLoop, calls=%fused_computation.75 | loop fusion | flops 4128768 | bytes 34209792 | tf_op jit(solution)/shard_map/slice | solution.py:110
  39.2 4.7 %rev.6 = f32[16,16,4096]{2,1,0:T(8,128)} reverse(f32[16,16,4096]{2,1,0:T(8,128)} %get-tuple-element.312), dimensions={0} | reverse | bytes 8388608 | tf_op jit(solution)/shard_map/rev | solution.py:83
  43.9 4.7 %rev.7 = f32[16,16,4096]{2,1,0:T(8,128)} reverse(f32[16,16,4096]{2,1,0:T(8,128)} %get-tuple-element.311), dimensions={0} | reverse | bytes 8388608 | tf_op jit(solution)/shard_map/rev | solution.py:84
  48.7 2.9 maximum_convert_fusion
  59.5 9.2 %multiply_reduce_fusion.1 = (f32[8,16,4096]{2,1,0:T(8,128)S(1)}, f32[8,16,4096]{2,1,0:T(8,128)}) fusion(f32[16,16,4096]{2,1,0:T(8,128)} %rev.7, f32[8,16,4096]{2,1,0:T(8,128)S(1)} %convert_multiply_fusion.1, f32[16,16,4096]{2,1,0:T(8,128)S(1)} %copy-done.1), kind=kLoop, calls=%fused_computation.22 | loop fusion | flops 32505856 | bytes 14680064 | tf_op jit(solution)/shard_map/reduce_sum | solution.py:84
  68.7 19.5 %while.57 = (s32[]{:T(128)}, f32[16,4096]{1,0:T(8,128)S(1)}, f32[16,4096]{1,0:T(8,128)S(1)}, f32[8]{0:T(128)S(1)}, f32[16,4096]{1,0:T(8,128)S(1)}, /*index=5*/f3...) while((s32[]{:T(128)}, f32[16,4096]{1,0:T(8,128)S(1)}, ...), condition=%wide.region_10.11_spmd.clone, body=%wide.region_9.10_spmd.clone.sunk | while | flops 786435 | bytes 2097283 | solution.py:101
  89.1 3.2 %gather_fusion = bf16[256,4096]{1,0:T(8,128)(2,1)} fusion(bf16[16,4096]{1,0:T(8,128)(2,1)S(1)} %get-tuple-element.309, s32[1024]{0:T(1024)S(1)} %pad_clamp_fusion), kind=kCustom, calls=%fused_computation | custom fusion | bytes 4195328 | tf_op jit(solution)/shard_map/gather | solution.py:61
  92.3 4.1 %select_convert_fusion = f32[16,16,4096]{2,1,0:T(8,128)} fusion(bf16[16,16,4096]{2,1,0:T(8,128)(2,1)} %bitcast.104, pred[16,16]{1,0:T(8,128)(4,1)S(1)} %subtract_compare_fusion), kind=kLoop, calls=%fused_computation.48 | loop fusion | flops 2097152 | bytes 6291712 | tf_op jit(solution)/shard_map/convert_element_type | solution.py:73
  98.0 40.2 %while.54 = (s32[]{:T(128)}, f32[8,16,4096]{2,1,0:T(8,128)}, s32[8,16]{1,0:T(8,128)S(1)}, f32[16,16,4096]{2,1,0:T(8,128)}, bf16[8,16,4096]{2,1,0:T(8,128)(2,1)}, /*index=5*/s32[]{:T(128)}) while((s32[]{:T(128)}, f32[8,16,4096]{2,1,0:T(8,128)}, s32[8,16]{1,0:T(8,128)S(1)}, f32[16,16,4096]{2,1,0:T(8,128)}, bf16[8,16,4096]{2,1,0:T(8,128)(2,1)}, ...), condition=%wide.region_5.6_spmd, body=%wide.region_3.5_spmd.sunk | while | flops 3146242 | bytes 5638925 | solution.py:80
  99.0 3.3 %multiply_reduce_fusion.4 = f32[16,4096]{1,0:T(8,128)S(1)} fusion(f32[16,16,4096]{2,1,0:T(8,128)} %get-tuple-element.557, f32[16,4096]{1,0:T(8,128)S(1)} %bitcast_convert_fusion.2, f32[16,16]{1,0:T(8,128)S(1)} %compare_convert_fusion.8), kind=kLoop, calls=%fused_computation.1.clone.1 | loop fusion | flops 3080192 | bytes 4719616 | tf_op jit(solution)/shard_map/while/body/eval_jaxpr/reduce_sum | solution.py:78
  104.0 3.4 %multiply_reduce_fusion.4 = f32[16,4096]{1,0:T(8,128)S(1)} fusion(f32[16,16,4096]{2,1,0:T(8,128)} %get-tuple-element.557, f32[16,4096]{1,0:T(8,128)S(1)} %bitcast_convert_fusion.2, f32[16,16]{1,0:T(8,128)S(1)} %compare_convert_fusion.8), kind=kLoop, calls=%fused_computation.1.clone.1 | loop fusion | flops 3080192 | bytes 4719616 | tf_op jit(solution)/shard_map/while/body/eval_jaxpr/reduce_sum | solution.py:78
  109.1 3.3 %multiply_reduce_fusion.4 = f32[16,4096]{1,0:T(8,128)S(1)} fusion(f32[16,16,4096]{2,1,0:T(8,128)} %get-tuple-element.557, f32[16,4096]{1,0:T(8,128)S(1)} %bitcast_convert_fusion.2, f32[16,16]{1,0:T(8,128)S(1)} %compare_convert_fusion.8), kind=kLoop, calls=%fused_computation.1.clone.1 | loop fusion | flops 3080192 | bytes 4719616 | tf_op jit(solution)/shard_map/while/body/eval_jaxpr/reduce_sum | solution.py:78
  114.2 3.2 %multiply_reduce_fusion.4 = f32[16,4096]{1,0:T(8,128)S(1)} fusion(f32[16,16,4096]{2,1,0:T(8,128)} %get-tuple-element.557, f32[16,4096]{1,0:T(8,128)S(1)} %bitcast_convert_fusion.2, f32[16,16]{1,0:T(8,128)S(1)} %compare_convert_fusion.8), kind=kLoop, calls=%fused_computation.1.clone.1 | loop fusion | flops 3080192 | bytes 4719616 | tf_op jit(solution)/shard_map/while/body/eval_jaxpr/reduce_sum | solution.py:78
  119.2 3.2 %multiply_reduce_fusion.4 = f32[16,4096]{1,0:T(8,128)S(1)} fusion(f32[16,16,4096]{2,1,0:T(8,128)} %get-tuple-element.557, f32[16,4096]{1,0:T(8,128)S(1)} %bitcast_convert_fusion.2, f32[16,16]{1,0:T(8,128)S(1)} %compare_convert_fusion.8), kind=kLoop, calls=%fused_computation.1.clone.1 | loop fusion | flops 3080192 | bytes 4719616 | tf_op jit(solution)/shard_map/while/body/eval_jaxpr/reduce_sum | solution.py:78
  124.1 3.4 %multiply_reduce_fusion.4 = f32[16,4096]{1,0:T(8,128)S(1)} fusion(f32[16,16,4096]{2,1,0:T(8,128)} %get-tuple-element.557, f32[16,4096]{1,0:T(8,128)S(1)} %bitcast_convert_fusion.2, f32[16,16]{1,0:T(8,128)S(1)} %compare_convert_fusion.8), kind=kLoop, calls=%fused_computation.1.clone.1 | loop fusion | flops 3080192 | bytes 4719616 | tf_op jit(solution)/shard_map/while/body/eval_jaxpr/reduce_sum | solution.py:78
  129.2 3.3 %multiply_reduce_fusion.4 = f32[16,4096]{1,0:T(8,128)S(1)} fusion(f32[16,16,4096]{2,1,0:T(8,128)} %get-tuple-element.557, f32[16,4096]{1,0:T(8,128)S(1)} %bitcast_convert_fusion.2, f32[16,16]{1,0:T(8,128)S(1)} %compare_convert_fusion.8), kind=kLoop, calls=%fused_computation.1.clone.1 | loop fusion | flops 3080192 | bytes 4719616 | tf_op jit(solution)/shard_map/while/body/eval_jaxpr/reduce_sum | solution.py:78
  134.2 3.2 %multiply_reduce_fusion.4 = f32[16,4096]{1,0:T(8,128)S(1)} fusion(f32[16,16,4096]{2,1,0:T(8,128)} %get-tuple-element.557, f32[16,4096]{1,0:T(8,128)S(1)} %bitcast_convert_fusion.2, f32[16,16]{1,0:T(8,128)S(1)} %compare_convert_fusion.8), kind=kLoop, calls=%fused_computation.1.clone.1 | loop fusion | flops 3080192 | bytes 4719616 | tf_op jit(solution)/shard_map/while/body/eval_jaxpr/reduce_sum | solution.py:78
  138.2 27.2 %all-gather.9.cloned.1.call-done = f32[256,4096]{1,0:T(8,128)} async-done(((f32[16,4096]{1,0:T(8,128)}), f32[256,4096]{1,0:T(8,128)}) %all-gather.9.cloned.1.call-update) | async-done | bytes 4194320 | tf_op jit(solution)/shard_map/all_gather | solution.py:17
  165.4 51.1 %all-gather.15.cloned.1.call-done = f32[256,4096]{1,0:T(8,128)} async-done(((f32[16,4096]{1,0:T(8,128)}), f32[256,4096]{1,0:T(8,128)}) %all-gather.15.cloned.1.call-update) | async-done | bytes 4194320 | tf_op jit(solution)/shard_map/all_gather | solution.py:17
  216.5 22.2 %while.55 = (s32[]{:T(128)}, f32[16,4096]{1,0:T(8,128)S(1)}, f32[16,4096]{1,0:T(8,128)S(1)}, s32[]{:T(128)}, f32[16,16,4096]{2,1,0:T(8,128)}, /*index=5*/f32[16,...) while((s32[]{:T(128)}, f32[16,4096]{1,0:T(8,128)S(1)}, ...), condition=%wide.region_12.13_spmd, body=%wide.region_11.12_spmd.sunk | while | flops 524293 | bytes 2097299 | solution.py:25
  241.8 26.0 %while.56 = (s32[]{:T(128)}, f32[16,4096]{1,0:T(8,128)S(1)}, f32[16,4096]{1,0:T(8,128)S(1)}, f32[8,16,4096]{2,1,0:T(8,128)}, f32[8,16,4096]{2,1,0:T(8,128)}, /*i...) while((s32[]{:T(128)}, f32[16,4096]{1,0:T(8,128)S(1)}, ...), condition=%wide.region_14.15_spmd, body=%wide.region_13.14_spmd.sunk | while | flops 655362 | bytes 3146369 | solution.py:101
  272.7 11.0 %subtract_reduce_fusion = f32[8,16,4096]{2,1,0:T(8,128)S(1)} fusion(f32[8,16,4096]{2,1,0:T(8,128)S(1)} %get-tuple-element.307, f32[16,16,4096]{2,1,0:T(8,128)S(1)} %copy-done.3, f32[8,16,4096]{2,1,0:T(8,128)S(1)} %get-tuple-element.306, f32[16,16,4096]{2,1,0:T(8,128)S(1)} %copy-done.2), kind=kLoop, calls=%fused_computation.21 | loop fusion | flops 33030144 | bytes 14680064 | tf_op jit(solution)/shard_map/reduce_sum | solution.py:109
  (163 shorter events, 108.3 us)
Async XLA Ops:
  6.5 131.7 %all-gather.11.cloned.1.call-start = ((), (), s32[]{:S(2)}) async-start(), calls=%async_computation.1 | async-start | bytes 4456448 | tf_op jit(solution)/shard_map/all_gather | solution.py:17
  12.8 19.8 %copy-start.7 = (f32[16,4096]{1,0:T(8,128)}, f32[16,4096]{1,0:T(8,128)S(1)}, u32[]{:S(2)}) copy-start(f32[16,4096]{1,0:T(8,128)S(1)} %get-tuple-element.320) | copy-start | bytes 786436
  12.8 19.9 %copy-start.9 = (f32[16,4096]{1,0:T(8,128)}, f32[16,4096]{1,0:T(8,128)S(1)}, u32[]{:S(2)}) copy-start(f32[16,4096]{1,0:T(8,128)S(1)} %get-tuple-element.321) | copy-start | bytes 786436
  12.8 125.4 %all-gather.13.cloned.1.call-start = ((), (), s32[]{:S(2)}) async-start(), calls=%async_computation.2 | async-start | bytes 4456448 | tf_op jit(solution)/shard_map/all_gather | solution.py:17
  14.0 34.7 %collective-permute-start = (bf16[3,2,4096]{2,1,0:T(2,128)(2,1)S(1)}, bf16[3,2,4096]{2,1,0:T(2,128)(2,1)S(1)}, u32[]{:S(2)}, u32[]{:S(2)}) collective-permute-start(bf16[3,2,4096]{2,1,0:T(2,128)(2,1)S(1)} %slice.79), channel_id=1, source_target_pairs={{0,1},{1,2},{2,3},{3,4},{4,5},{5,6},{6,7},{7,8},{8,9},{9,10},{10,1... | collective-permute-start | bytes 147464 | tf_op jit(solution)/shard_map/ppermute | solution.py:12
  15.3 150.1 %all-gather.9.cloned.1.call-start = ((), (), s32[]{:S(2)}) async-start(), calls=%async_computation | async-start | bytes 4456448 | tf_op jit(solution)/shard_map/all_gather | solution.py:17
  15.4 17.0 %copy-start.10 = (f32[3,3,4096]{2,1,0:T(4,128)S(1)}, f32[3,3,4096]{2,1,0:T(4,128)}, u32[]{:S(2)}) copy-start(f32[3,3,4096]{2,1,0:T(4,128)} %param.16) | copy-start | bytes 442372
  54.2 2.7 copy-start
  56.8 2.7 copy-start.1
  57.1 1.0 copy-start.6
  88.2 0.7 copy-start.4
  88.3 4.1 %copy-start.5 = (f32[16,4096]{1,0:T(8,128)}, f32[16,4096]{1,0:T(8,128)S(1)}, u32[]{:S(2)}) copy-start(f32[16,4096]{1,0:T(8,128)S(1)} %get-tuple-element.200) | copy-start | bytes 786436
  89.0 127.5 %all-gather.15.cloned.1.call-start = ((), (), s32[]{:S(2)}) async-start(), calls=%async_computation.3 | async-start | bytes 4456448 | tf_op jit(solution)/shard_map/all_gather | solution.py:17
  241.8 26.0 %copy-start.8 = (f32[16,4096]{1,0:T(8,128)S(1)}, f32[16,4096]{1,0:T(8,128)}, u32[]{:S(2)}) copy-start(f32[16,4096]{1,0:T(8,128)} %copy-done.7) | copy-start | bytes 786436
  267.9 3.5 %copy-start.2 = (f32[16,16,4096]{2,1,0:T(8,128)S(1)}, f32[16,16,4096]{2,1,0:T(8,128)}, u32[]{:S(2)}) copy-start(f32[16,16,4096]{2,1,0:T(8,128)} %get-tuple-element.308) | copy-start | bytes 12582916
  267.9 4.8 %copy-start.3 = (f32[16,16,4096]{2,1,0:T(8,128)S(1)}, f32[16,16,4096]{2,1,0:T(8,128)}, u32[]{:S(2)}) copy-start(f32[16,16,4096]{2,1,0:T(8,128)} %get-tuple-element.310) | copy-start | bytes 12582916
  270.7 15.0 %slice-start = ((s8[6291456]{0:T(1024)(128)(4,1)}), s8[4194304]{0:T(1024)(128)(4,1)S(1)}, s32[]{:S(2)}) async-start(s8[6291456]{0:T(1024)(128)(4,1)} %bitcast.102), calls=%async_computation.4 | async-start | bytes 8388608
  272.7 13.0 %slice-start.1 = ((s8[6291456]{0:T(1024)(128)(4,1)}), s8[2097152]{0:T(1024)(128)(4,1)S(1)}, s32[]{:S(2)}) async-start(s8[6291456]{0:T(1024)(128)(4,1)} %bitcast.102), calls=%async_computation.5 | async-start | bytes 4194304
  283.8 2.0 copy-start.11
Sparse Core Ops, SparseCore 0:
  12.9 49.6 all-gather.10
  64.8 49.2 all-gather.12
  116.3 49.0 all-gather.8
  167.4 49.0 all-gather.14
where the time goes:
time: 296 us; the launch traced here: 294 us
  other arithmetic  151 us (51%)
  waiting for transfers between devices  78.3 us (26%)
  local copies, waits for them, and re-layouts  48.8 us (16%)
  between operations  13.4 us (5%)
    all_gather x4, waiting for transfers between devices, entering(): gathered = jax.tree.map(lambda a: lax.all_gather(a, axis), part)  78.3 us
    add x16, other arithmetic, advance(): n_im = a_re * s_im + a_im * s_re + b_im  29 us
    reduce_sum x8, other arithmetic, one_block(): jnp.sum(toe_wide * same[:, :, None] * values.astype(jnp.float32)[None], a...  26.2 us
    add x15, other arithmetic, combine_gates(): b_im = bl_im + gl_re * be_im + gl_im * be_re  21.9 us
    mul x1, other arithmetic, mode_tables(): pow_re = magnitude * jnp.cos(angle)  17 us
    dynamic_update_slice x16, local copies, waits for them, and re-layouts, local_blocks(): intra = lax.map(one_block, (blocks, seg_blocks))  12.6 us
    reduce_sum x1, other arithmetic, finish(): jnp.sum(pow_re[1:][None] * amp_re[:, None] - pow_im[1:][None] * amp_im[:,...  11 us
    dynamic_slice x16, local copies, waits for them, and re-layouts, run_chain(): final, states = lax.scan(advance, (start_re, start_im), (flags, e_re, e_im))  9.53 us
  transfers between devices with their start and end apart: 5, of which 2 were waited for; matrix products, arithmetic and copies ran while one was open for 40% of the time, Pallas kernels for 0%

commit v1 on v0

v1 whole, which is shorter than its diff:
```python
import jax
import jax.numpy as jnp
from jax import lax
from jax.experimental import pallas as pl
from jax.experimental.pallas import tpu as pltpu
from jax.sharding import PartitionSpec as P

BLK = 16
LANE = 128
SUB = 8
TILE = 512
F32 = jnp.float32
BF16 = jnp.bfloat16


def exchange(block, distance):
    devices = range(lax.axis_size("seq"))
    return lax.ppermute(block, "seq", [(i, i ^ distance) for i in devices])


def row_iota(rows):
    return lax.broadcasted_iota(jnp.int32, (rows, LANE), 0)


def short_filter(rows, halo, taps, pad, mask_one, mask_two):
    tokens = rows.shape[0]
    values = rows.astype(F32)
    pad[pl.ds(SUB, tokens), :] = values
    pad[pl.ds(SUB - 2, 2), :] = halo.astype(F32)
    conv = taps[0:1, :] * values
    conv = conv + taps[1:2, :] * pad[pl.ds(SUB - 1, tokens), :] * mask_one
    return conv + taps[2:3, :] * pad[pl.ds(SUB - 2, tokens), :] * mask_two


def tap_masks(starts_ref, tokens):
    t = row_iota(tokens)
    here = jnp.zeros((tokens, LANE), jnp.bool_)
    before = jnp.zeros((tokens, LANE), jnp.bool_)
    for i in range(starts_ref.shape[0]):
        here = here | (t == starts_ref[i])
        before = before | (t - 1 == starts_ref[i])
    mask_one = jnp.where(here, 0.0, 1.0)
    return mask_one, jnp.where(here | before, 0.0, 1.0)


def block_flags(starts_ref, count):
    flags = []
    for b in range(count):
        hit = jnp.int32(0)
        for i in range(starts_ref.shape[0]):
            s = starts_ref[i]
            hit = hit | ((s >= b * BLK) & (s < (b + 1) * BLK)).astype(jnp.int32)
        flags.append((1 - hit).astype(F32))
    return flags


def cmul(a_re, a_im, b_re, b_im):
    return a_re * b_re - a_im * b_im, a_re * b_im + a_im * b_re


def column_sums(parts):
    row = lax.broadcasted_iota(jnp.int32, (SUB, LANE), 0)
    low = row < 4
    level = []
    for b in range(4):
        keep = jnp.where(low, parts[b], parts[b + 4])
        move = jnp.where(low, parts[b + 4], parts[b])
        level.append(keep + pltpu.roll(move, 4, 0))
    for step in (2, 1):
        clear = (row & step) == 0
        level = [
            jnp.where(
                clear,
                level[b] + pltpu.roll(level[b], SUB - step, 0),
                level[b + step] + pltpu.roll(level[b + step], step, 0),
            )
            for b in range(step)
        ]
    return level[0]


def front_kernel(starts_ref, f0_ref, f2_ref, halo_ref, taps_ref, pre_ref, pim_ref,
                 z_ref, e_ref, end_ref, one_s, two_s, last_s, pad_s, z_s):
    tokens, width = z_ref.shape
    count = tokens // BLK
    modes = pre_ref.shape[0]
    halves = modes // SUB

    @pl.when(pl.program_id(0) == 0)
    def _():
        mask_one, mask_two = tap_masks(starts_ref, tokens)
        one_s[...] = mask_one
        two_s[...] = mask_two
        t = row_iota(tokens)
        last = jnp.full((tokens, LANE), -1, jnp.int32)
        for i in range(starts_ref.shape[0]):
            s = starts_ref[i]
            last = jnp.maximum(last, jnp.where(s <= (t | (BLK - 1)), s, -1))
        last_s[...] = jnp.where(t >= last, 1.0, 0.0)

    flags = block_flags(starts_ref, count)

    @pl.loop(0, width // LANE)
    def _(tile):
        lanes = pl.ds(pl.multiple_of(tile * LANE, LANE), LANE)
        mask_one, mask_two = one_s[...], two_s[...]
        conv0 = short_filter(f0_ref[0, :, lanes], halo_ref[0, :, lanes], taps_ref[0, :, lanes],
                             pad_s.at[0], mask_one, mask_two)
        conv2 = short_filter(f2_ref[0, :, lanes], halo_ref[2, :, lanes], taps_ref[2, :, lanes],
                             pad_s.at[1], mask_one, mask_two)
        z = (conv0 * conv2).astype(BF16)
        z_ref[:, lanes] = z
        z_s[...] = z.astype(F32) * last_s[...]
        p_re = [pre_ref[pl.ds(h * SUB, SUB), lanes] for h in range(halves)]
        p_im = [pim_ref[pl.ds(h * SUB, SUB), lanes] for h in range(halves)]
        pow_re, pow_im = list(p_re), list(p_im)
        e_re, e_im = [], []
        for b in range(count):
            here = z_s[pl.ds(b * BLK + BLK - 1, SUB, stride=0), :]
            prev = z_s[pl.ds(b * BLK + BLK - 2, SUB, stride=0), :]
            e_re.append([here + p_re[h] * prev for h in range(halves)])
            e_im.append([p_im[h] * prev for h in range(halves)])
        for k in range(2, BLK):
            for h in range(halves):
                pow_re[h], pow_im[h] = cmul(pow_re[h], pow_im[h], p_re[h], p_im[h])
            for b in range(count):
                here = z_s[pl.ds(b * BLK + BLK - 1 - k, SUB, stride=0), :]
                for h in range(halves):
                    e_re[b][h] = e_re[b][h] + pow_re[h] * here
                    e_im[b][h] = e_im[b][h] + pow_im[h] * here
        for h in range(halves):
            g_re, g_im = cmul(pow_re[h], pow_im[h], p_re[h], p_im[h])
            end_re, end_im = e_re[0][h], e_im[0][h]
            for b in range(count):
                if b:
                    move_re, move_im = cmul(g_re, g_im, end_re, end_im)
                    end_re = flags[b] * move_re + e_re[b][h]
                    end_im = flags[b] * move_im + e_im[b][h]
                e_ref[b, pl.ds(h * SUB, SUB), lanes] = e_re[b][h]
                e_ref[b, pl.ds(modes + h * SUB, SUB), lanes] = e_im[b][h]
            end_ref[0, pl.ds(h * SUB, SUB), lanes] = end_re.astype(BF16)
            end_ref[0, pl.ds(modes + h * SUB, SUB), lanes] = end_im.astype(BF16)


def middle_kernel(starts_ref, f1_ref, halo_ref, taps_ref, z_ref, skip_ref, pre_ref, pim_ref,
                  cre_ref, cim_ref, base_ref, gain_ref,
                  one_s, two_s, first_s, part_s, pad_s, z_s, filt_s, acc_s):
    tokens, width = z_ref.shape
    count = tokens // BLK
    modes = pre_ref.shape[0]
    halves = modes // SUB
    nseq = starts_ref.shape[0]

    @pl.when(pl.program_id(0) == 0)
    def _():
        mask_one, mask_two = tap_masks(starts_ref, tokens)
        one_s[...] = mask_one
        two_s[...] = mask_two
        t = row_iota(tokens)
        t0 = t & (-BLK)
        piece = jnp.zeros((tokens, LANE), jnp.int32)
        opened = jnp.zeros((tokens, LANE), jnp.bool_)
        for i in range(nseq):
            s = starts_ref[i]
            piece = piece + jnp.where((s > t0) & (s <= t), 1, 0)
            opened = opened | ((s >= t0) & (s <= t))
        part_s[...] = piece.astype(F32)
        first_s[...] = jnp.where(opened, 0.0, 1.0)

    pieces = jnp.int32(1)
    for b in range(count):
        inside = jnp.int32(1)
        for i in range(nseq):
            s = starts_ref[i]
            inside = inside + ((s > b * BLK) & (s < (b + 1) * BLK)).astype(jnp.int32)
        pieces = jnp.maximum(pieces, inside)

    @pl.loop(0, width // LANE)
    def _(tile):
        lanes = pl.ds(pl.multiple_of(tile * LANE, LANE), LANE)
        q_re = [cre_ref[pl.ds(h * SUB, SUB), lanes] for h in range(halves)]
        q_im = [cim_ref[pl.ds(h * SUB, SUB), lanes] for h in range(halves)]
        p_re = [pre_ref[pl.ds(h * SUB, SUB), lanes] for h in range(halves)]
        p_im = [pim_ref[pl.ds(h * SUB, SUB), lanes] for h in range(halves)]
        filt_s[pl.ds(0, BLK), :] = jnp.zeros((BLK, LANE), F32)
        for group in range(BLK // SUB):
            parts = []
            for k in range(SUB):
                parts.append(sum(q_re[1:], q_re[0]))
                for h in range(halves):
                    q_re[h], q_im[h] = cmul(q_re[h], q_im[h], p_re[h], p_im[h])
            filt_s[pl.ds(BLK + group * SUB, SUB), :] = column_sums(parts).astype(BF16).astype(F32)
        z = z_ref[:, lanes].astype(F32)
        acc_s[...] = skip_ref[:, lanes] * z

        def one_piece(q, carry):
            mask = jnp.where(part_s[...] == q.astype(F32), 1.0, 0.0)
            z_s[...] = z_ref[:, lanes].astype(F32) * mask
            sums = [[None] * 2 for _ in range(count)]
            for s in range(BLK):
                for r in range(BLK // SUB):
                    if s >= (r + 1) * SUB:
                        continue
                    column = filt_s[pl.ds(BLK - s + r * SUB, SUB), :]
                    for b in range(count):
                        term = column * z_s[pl.ds(b * BLK + s, SUB, stride=0), :]
                        sums[b][r] = term if s == 0 else sums[b][r] + term
            for b in range(count):
                for r in range(BLK // SUB):
                    rows = pl.ds(b * BLK + r * SUB, SUB)
                    here = jnp.where(part_s[rows, :] == q.astype(F32), sums[b][r], 0.0)
                    acc_s[rows, :] = acc_s[rows, :] + here
            return carry

        lax.fori_loop(0, pieces, one_piece, 0)
        conv1 = short_filter(f1_ref[0, :, lanes], halo_ref[1, :, lanes], taps_ref[1, :, lanes],
                             pad_s, one_s[...], two_s[...])
        base_ref[:, lanes] = conv1 * acc_s[...]
        gain_ref[:, lanes] = conv1 * first_s[...]


def back_kernel(starts_ref, core_ref, own_ref, other_ref, e_ref, pre_ref, pim_ref, cre_ref, cim_ref,
                base_ref, gain_ref, out_ref, y_s):
    tokens, width = out_ref.shape
    count = tokens // BLK
    modes = pre_ref.shape[0]
    halves = modes // SUB
    flags = block_flags(starts_ref, count)
    mine = (pl.program_id(0) * 2 >= pl.num_programs(0)).astype(jnp.int32) == core_ref[0]

    @pl.loop(0, width // LANE)
    def _(tile):
        lanes = pl.ds(pl.multiple_of(tile * LANE, LANE), LANE)

        def rows(ref, h):
            return ref[pl.ds(h * SUB, SUB), lanes]

        entry = [
            jnp.where(mine, rows(own_ref, h).astype(F32), rows(other_ref, h).astype(F32))
            for h in range(2 * halves)
        ]
        p_re = [rows(pre_ref, h) for h in range(halves)]
        p_im = [rows(pim_ref, h) for h in range(halves)]
        q_re = [rows(cre_ref, h) for h in range(halves)]
        q_im = [rows(cim_ref, h) for h in range(halves)]
        s_re, s_im = [entry[:halves]], [entry[halves:]]
        gate = [(p_re[h], p_im[h]) for h in range(halves)]
        for _ in range(4):
            gate = [cmul(*g, *g) for g in gate]
        for b in range(count - 1):
            new_re, new_im = [], []
            for h in range(halves):
                move_re, move_im = cmul(*gate[h], s_re[b][h], s_im[b][h])
                new_re.append(flags[b] * move_re + e_ref[b, pl.ds(h * SUB, SUB), lanes])
                new_im.append(flags[b] * move_im + e_ref[b, pl.ds(modes + h * SUB, SUB), lanes])
            s_re.append(new_re)
            s_im.append(new_im)
        for k in range(BLK):
            for h in range(halves):
                q_re[h], q_im[h] = cmul(q_re[h], q_im[h], p_re[h], p_im[h])
            parts = []
            for b in range(count):
                part = q_re[0] * s_re[b][0] - q_im[0] * s_im[b][0]
                for h in range(1, halves):
                    part = part + q_re[h] * s_re[b][h] - q_im[h] * s_im[b][h]
                parts.append(part)
            y_s[pl.ds(k, SUB, stride=BLK), :] = column_sums(parts)
        out_ref[:, lanes] = (base_ref[:, lanes] + gain_ref[:, lanes] * y_s[...]).astype(BF16)


def per_device(features, kernel, skip, residues, decay, freq, lengths):
    tokens = features.shape[1]
    modes, width = decay.shape
    half = width // 2
    count = tokens // BLK
    n = lax.axis_size("seq")
    place = lax.axis_index("seq")
    core = place % 2
    tiles = width // TILE

    rim = features[:, tokens - 2 :, :]
    inner = exchange(rim, 1)
    link = [(i, i + 1) for i in range(1, n - 1, 2)]
    outer = lax.ppermute(rim, "seq", link + [(b, a) for a, b in link])
    halo = jnp.where(core == 1, inner, outer)

    order = jnp.arange(lengths.shape[0])
    starts = jnp.sum(jnp.where(order[None, :] < order[:, None], lengths[None, :], 0), axis=1)
    base = place * tokens
    local_starts = (starts - base).astype(jnp.int32)

    def same(first, last):
        hit = (starts >= first * tokens) & (starts < (last + 1) * tokens)
        return jnp.where(jnp.any(hit), 0.0, 1.0).astype(F32)

    magnitude = jnp.exp(-decay)
    p_re = magnitude * jnp.cos(freq)
    p_im = magnitude * jnp.sin(freq)
    scale = jnp.sqrt(-jnp.expm1(-2.0 * decay))
    c_re = residues[0] * scale
    c_im = residues[1] * scale

    def smem(shape):
        return pl.BlockSpec(shape, lambda *_: (0,) * len(shape), memory_space=pltpu.SMEM)

    def stream(r):
        return pl.BlockSpec((1, tokens, TILE), lambda i, *_: (r, 0, i))

    def columns(*lead):
        return pl.BlockSpec((*lead, TILE), lambda i, *_: (0,) * len(lead) + (i,))

    params = pltpu.CompilerParams(
        dimension_semantics=("arbitrary",), vmem_limit_bytes=32 * 1024 * 1024
    )
    table = columns(modes)
    plane = pltpu.VMEM((tokens, LANE), F32)
    pad = pltpu.VMEM((tokens + SUB, LANE), F32)
    z, e, end = pl.pallas_call(
        front_kernel,
        grid_spec=pltpu.PrefetchScalarGridSpec(
            num_scalar_prefetch=1,
            grid=(tiles,),
            in_specs=[stream(0), stream(2), columns(3, 2), columns(3, 3), table, table],
            out_specs=[
                columns(tokens),
                columns(count, 2 * modes),
                pl.BlockSpec((1, 2 * modes, TILE), lambda i, *_: (i * 2 // tiles, 0, i % (tiles // 2))),
            ],
            scratch_shapes=[plane, plane, plane, pltpu.VMEM((2, tokens + SUB, LANE), F32), plane],
        ),
        out_shape=[
            jax.ShapeDtypeStruct((tokens, width), BF16),
            jax.ShapeDtypeStruct((count, 2 * modes, width), F32),
            jax.ShapeDtypeStruct((2, 2 * modes, half), BF16),
        ],
        compiler_params=params,
        name="front",
    )(local_starts, features, features, halo, kernel, p_re, p_im)

    base_out, gain = pl.pallas_call(
        middle_kernel,
        grid_spec=pltpu.PrefetchScalarGridSpec(
            num_scalar_prefetch=1,
            grid=(tiles,),
            in_specs=[stream(1), columns(3, 2), columns(3, 3), columns(tokens), columns(1),
                      table, table, table, table],
            out_specs=[columns(tokens), columns(tokens)],
            scratch_shapes=[plane, plane, plane, plane, pad, plane,
                            pltpu.VMEM((2 * BLK, LANE), F32), plane],
        ),
        out_shape=[jax.ShapeDtypeStruct((tokens, width), F32)] * 2,
        compiler_params=params,
        cost_estimate=pl.CostEstimate(flops=10 * 1000 * 1000, bytes_accessed=8 << 20, transcendentals=0),
        name="middle",
    )(local_starts, features, halo, kernel, z, skip[None], p_re, p_im, c_re, c_im)

    span = lax.dynamic_slice_in_dim(decay, core * half, half, 1) * float(tokens)
    turn = lax.dynamic_slice_in_dim(freq, core * half, half, 1) * float(tokens)
    fade = jnp.exp(-span)
    one = (fade * jnp.cos(turn), fade * jnp.sin(turn))

    def split(packed):
        return packed[:modes].astype(F32), packed[modes:].astype(F32)

    def pack(pair):
        return jnp.concatenate([pair[0].astype(BF16), pair[1].astype(BF16)], axis=0)

    def advance(gate, flag, state, addend):
        re, im = cmul(*gate, *state)
        return addend[0] + flag * re, addend[1] + flag * im

    def choose(flag, a, b):
        return tuple(jnp.where(flag, x, y) for x, y in zip(a, b))

    kept = split(lax.dynamic_index_in_dim(end, core, 0, False))
    came = split(exchange(lax.dynamic_index_in_dim(end, 1 - core, 0, False), 1))
    odd = core == 1
    even_end, odd_end = choose(odd, came, kept), choose(odd, kept, came)
    even = place - core
    total = advance(one, same(even + 1, even + 1), even_end, odd_end)
    zero = jnp.zeros((modes, half), F32)
    prefix = (zero, zero)
    before = (zero + 1.0, zero)
    power = cmul(*one, *one)
    distance = 2
    while distance < n:
        upper = (place & distance) != 0
        group = place - place % distance
        met = split(exchange(pack(total), distance))
        added = advance(before, same(group, even - 1), met, prefix)
        prefix = choose(upper, added, prefix)
        early, late = choose(upper, met, total), choose(upper, total, met)
        later = group | distance
        total = advance(power, same(later, later + distance - 1), early, late)
        before = choose(upper, cmul(*before, *power), before)
        power = cmul(*power, *power)
        distance *= 2
    beyond = advance(one, same(even, even), prefix, even_end)
    own = pack(choose(odd, beyond, prefix))
    other = exchange(pack(choose(odd, prefix, beyond)), 1)

    entry = pl.BlockSpec((2 * modes, TILE), lambda i, *_: (0, i % (tiles // 2)))
    return pl.pallas_call(
        back_kernel,
        grid_spec=pltpu.PrefetchScalarGridSpec(
            num_scalar_prefetch=2,
            grid=(tiles,),
            in_specs=[entry, entry, columns(count, 2 * modes), table, table, table, table,
                      columns(tokens), columns(tokens)],
            out_specs=columns(tokens),
            scratch_shapes=[plane],
        ),
        out_shape=jax.ShapeDtypeStruct((tokens, width), BF16),
        compiler_params=params,
        name="back",
    )(local_starts, core[None].astype(jnp.int32), own, other, e, p_re, p_im, c_re, c_im, base_out, gain)


def solution(mesh):
    return jax.shard_map(
        per_device,
        mesh=mesh,
        in_specs=(P(None, ("groups", "seq"), None), P(), P(), P(), P(), P(), P("groups")),
        out_specs=P(("groups", "seq"), None),
        check_vma=False,
    )
```

time: 296 us -> 90.7 us (0.31)
  the two profiles are of different devices: /device:TPU:29 before, /device:TPU:1 now
where the time goes in v1:
time: 90.7 us; the launch traced here: 90.2 us
  Pallas kernels  30.3 us (33%)
  other arithmetic  18.7 us (21%)
  local copies, waits for them, and re-layouts  15.1 us (17%)
  starting transfers between devices  14.7 us (16%)
  waiting for transfers between devices  6.55 us (7%)
  between operations  4.87 us (5%)
    unnamed x56, local copies, waits for them, and re-layouts  13.4 us
    convert_element_type x9, other arithmetic, pack(): return jnp.concatenate([pair[0].astype(BF16), pair[1].astype(BF16)], axis=0)  12.2 us
    pallas_call x1, Pallas kernels, per_device(): pl.pallas_call(back_kernel, grid_spec=pltpu.PrefetchScalarGridSpec(num_sc...  11.5 us
    pallas_call x1, Pallas kernels, per_device(): pl.pallas_call(front_kernel, grid_spec=pltpu.PrefetchScalarGridSpec(num_s...  10.7 us
    ppermute x6, starting transfers between devices, exchange(): return lax.ppermute(block, 'seq', [(i, i ^ distance) for i in devices])  10.2 us
    pallas_call x1, Pallas kernels, per_device(): pl.pallas_call(middle_kernel, grid_spec=pltpu.PrefetchScalarGridSpec(num_...  8.15 us
    ppermute x6, waiting for transfers between devices, exchange(): return lax.ppermute(block, 'seq', [(i, i ^ distance) for i in devices])  6.55 us
    ppermute x1, starting transfers between devices, per_device(): outer = lax.ppermute(rim, 'seq', link + [(b, a) for a, b in link])  4.54 us
  transfers between devices with their start and end apart: 7, of which 3 were waited for; matrix products, arithmetic and copies ran while one was open for 5% of the time, Pallas kernels for 9%

profile of v1, /device:TPU:1, one launch (start us, length us, event | category | flops | bytes accessed | tf_op | source)
XLA Modules:
  0.0 90.2 jit_solution(13975960878326063310)
XLA Ops:
  0.0 1.0 %slice.41 = bf16[3,2,4096]{2,1,0:T(2,128)(2,1)S(1)} slice(bf16[3,128,4096]{2,1,0:T(8,128)(2,1)} %f1_ref.1), slice={[0:3], [126:128], [0:4096]} | slice | bytes 98304 | tf_op jit(solution)/shard_map/slice | solution.py:281
  1.0 4.5 %collective-permute-start.1 = (bf16[3,2,4096]{2,1,0:T(2,128)(2,1)S(1)}, bf16[3,2,4096]{2,1,0:T(2,128)(2,1)S(1)}, u32[]{:S(2)}, u32[]{:S(2)}) collective-permute-start(bf16[3,2,4096]{2,1,0:T(2,128)(2,1)S(1)} %slice.41), channel_id=1, source_target_pairs={{1,2},{3,4},{5,6},{7,8},{9,10},{11,12},{13,14},{2,1},{4,3},{6,5},{... | collective-permute-start | bytes 147464 | tf_op jit(solution)/shard_map/ppermute | solution.py:284
  6.4 2.9 %bitcast_multiply_fusion = (f32[16,4096]{1,0:T(8,128)}, f32[16,4096]{1,0:T(8,128)}, f32[16,4096]{1,0:T(8,128)S(1)}, f32[16,4096]{1,0:T(8,128)S(1)}) fusion(f32[2,16,4096]{2,1,0:T(8,128)} %param.10, f32[16,4096]{1,0:T(8,128)} %param.11, f32[16,4096]{1,0:T(8,128)} %param.12), kind=kLoop, calls=%fused_computation | loop fusion | flops 458752 | bytes 2097152 | tf_op jit(solution)/shard_map/mul | solution.py:301
  9.4 1.9 %copy-done = bf16[3,128,4096]{2,1,0:T(8,128)(2,1)S(1)} copy-done((bf16[3,128,4096]{2,1,0:T(8,128)(2,1)S(1)}, bf16[3,128,4096]{2,1,0:T(8,128)(2,1)}, u32[]{:S(2)}) %copy-start) | copy-done | bytes 3145752
  12.2 10.7 %front.1 = (bf16[128,4096]{1,0:T(8,128)(2,1)S(1)}, f32[8,32,4096]{2,1,0:T(8,128)S(1)}, bf16[2,32,2048]{2,1,0:T(8,128)(2,1)S(1)}) custom-call(s32[6]{0:T(128)S(1)} %broadcast_subtract_fusion.starts_ref, bf16[3,128,4096]{2,1,0:T(8,128)(2,1)S(1)} %copy-done, bf16[3,128,4096]{2,1,0:T(8,128)(2,1)S(1)} %copy-done, ...), custom_call_target="tpu_custom_call" | custom-call | tf_op jit(solution)/shard_map/front/pallas_call | solution.py:318
  22.9 1.9 %copy-done.5 = f32[8,32,4096]{2,1,0:T(8,128)} copy-done((f32[8,32,4096]{2,1,0:T(8,128)}, f32[8,32,4096]{2,1,0:T(8,128)S(1)}, u32[]{:S(2)}) %copy-start.5) | copy-done | bytes 4194328
  24.8 1.0 %copy-done.11 = bf16[128,4096]{1,0:T(8,128)(2,1)} copy-done((bf16[128,4096]{1,0:T(8,128)(2,1)}, bf16[128,4096]{1,0:T(8,128)(2,1)S(1)}, u32[]{:S(2)}) %copy-start.11) | copy-done | bytes 1048600
  29.3 2.3 %fusion.24 = (bf16[16,2048]{1,0:T(8,128)(2,1)S(1)}, f32[16,2048]{1,0:T(8,128)}, f32[16,2048]{1,0:T(8,128)S(1)}, f32[16,2048]{1,0:T(8,128)S(1)}) fusion(bf16[2,32,2048]{2,1,0:T(8,128)(2,1)} %copy-done.9, s32[]{:T(128)S(6)} %select_n.182, s32[]{:T(128)S(6)} %add.165, bf16[32,2048]{1,0:T(8,128)(2,1)} %collective-permute-done.2, f32[]{:T(128)S(6)} %select_n.191, ...), kind=kLoop, calls=%fused_computation.94 | loop fusion | flops 589824 | bytes 983057 | tf_op jit(solution)/shard_map/convert_element_type | solution.py:366
  32.2 1.6 %fusion.26 = (bf16[16,2048]{1,0:T(8,128)(2,1)S(1)}, f32[16,2048]{1,0:T(8,128)}) fusion(f32[16,2048]{1,0:T(8,128)S(1)} %get-tuple-element.40, bf16[2,32,2048]{2,1,0:T(8,128)(2,1)} %copy-done.9, s32[]{:T(128)S(6)} %select_n.182, bf16[32,2048]{1,0:T(8,128)(2,1)} %collective-permute-done.2, f32[16,2048]{1,0:T(8,128)S(1)} %get-tuple-element.39, ...), kind=kLoop, calls=%fused_computation.95 | loop fusion | flops 425984 | bytes 720909 | tf_op jit(solution)/shard_map/convert_element_type | solution.py:366
  34.5 1.2 %collective-permute-start.3 = (bf16[32,2048]{1,0:T(8,128)(2,1)}, bf16[32,2048]{1,0:T(8,128)(2,1)}, u32[]{:S(2)}, u32[]{:S(2)}) collective-permute-start(bf16[32,2048]{1,0:T(8,128)(2,1)} %pad_maximum_fusion), channel_id=1, source_target_pairs={{0,2},{1,3},{2,0},{3,1},{4,6},{5,7},{6,4},{7,5},{8,10},{9,11},{10,... | collective-permute-start | bytes 393224 | tf_op jit(solution)/shard_map/ppermute | solution.py:18
  36.4 3.4 %collective-permute-done.3 = bf16[32,2048]{1,0:T(8,128)(2,1)} collective-permute-done((bf16[32,2048]{1,0:T(8,128)(2,1)}, bf16[32,2048]{1,0:T(8,128)(2,1)}, u32[]{:S(2)}, u32[]{:S(2)}) %collective-permute-start.3) | collective-permute-done | bytes 131104 | tf_op jit(solution)/shard_map/ppermute | solution.py:18
  39.8 1.9 %fusion.20 = (bf16[16,2048]{1,0:T(8,128)(2,1)S(1)}, f32[16,2048]{1,0:T(8,128)}, f32[16,2048]{1,0:T(8,128)S(1)}, f32[16,2048]{1,0:T(8,128)S(1)}) fusion(f32[16,2048]{1,0:T(8,128)} %get-tuple-element.42, bf16[32,2048]{1,0:T(8,128)(2,1)} %collective-permute-done.3, f32[16,2048]{1,0:T(8,128)} %get-tuple-element.38, f32[]{:T(128)S(6)} %select_n.199, pred[]{:T(512)S(6)} %ne.28, ...), kind=kLoop, calls=%fused_computation.92 | loop fusion | flops 524288 | bytes 1114117 | tf_op jit(solution)/shard_map/convert_element_type | solution.py:366
  42.4 1.8 %fusion.22 = (bf16[16,2048]{1,0:T(8,128)(2,1)S(1)}, f32[16,2048]{1,0:T(8,128)}) fusion(f32[16,2048]{1,0:T(8,128)S(1)} %get-tuple-element.34, f32[16,2048]{1,0:T(8,128)} %get-tuple-element.38, bf16[32,2048]{1,0:T(8,128)(2,1)} %collective-permute-done.3, f32[16,2048]{1,0:T(8,128)S(1)} %get-tuple-element.33, f32[16,2048]{1,0:T(8,128)} %get-tuple-element.42, ...), kind=kLoop, calls=%fused_computation.93 | loop fusion | flops 360448 | bytes 851973 | tf_op jit(solution)/shard_map/convert_element_type | solution.py:366
  44.8 1.3 %collective-permute-start.4 = (bf16[32,2048]{1,0:T(8,128)(2,1)}, bf16[32,2048]{1,0:T(8,128)(2,1)}, u32[]{:S(2)}, u32[]{:S(2)}) collective-permute-start(bf16[32,2048]{1,0:T(8,128)(2,1)} %pad_maximum_fusion.1), channel_id=1, source_target_pairs={{0,4},{1,5},{2,6},{3,7},{4,0},{5,1},{6,2},{7,3},{8,12},{9,13},{10,... | collective-permute-start | bytes 393224 | tf_op jit(solution)/shard_map/ppermute | solution.py:18
  46.7 2.2 %collective-permute-done.4 = bf16[32,2048]{1,0:T(8,128)(2,1)} collective-permute-done((bf16[32,2048]{1,0:T(8,128)(2,1)}, bf16[32,2048]{1,0:T(8,128)(2,1)}, u32[]{:S(2)}, u32[]{:S(2)}) %collective-permute-start.4) | collective-permute-done | bytes 131104 | tf_op jit(solution)/shard_map/ppermute | solution.py:18
  48.9 1.2 %fusion.15 = (bf16[16,2048]{1,0:T(8,128)(2,1)S(1)}, f32[16,2048]{1,0:T(8,128)S(1)}, f32[16,2048]{1,0:T(8,128)S(1)}) fusion(f32[16,2048]{1,0:T(8,128)} %get-tuple-element.32, f32[16,2048]{1,0:T(8,128)} %get-tuple-element.36, f32[]{:T(128)S(6)} %select_n.209, pred[]{:T(512)S(6)} %ne.27, bf16[32,2048]{1,0:T(8,128)(2,1)} %collective-permute-done.4, ...), kind=kLoop, calls=%fused_computation.49 | loop fusion | flops 524288 | bytes 983045 | tf_op jit(solution)/shard_map/convert_element_type | solution.py:366
  50.8 1.1 %fusion.19 = bf16[16,2048]{1,0:T(8,128)(2,1)S(1)} fusion(f32[16,2048]{1,0:T(8,128)} %get-tuple-element.36, f32[16,2048]{1,0:T(8,128)S(1)} %get-tuple-element.29, f32[16,2048]{1,0:T(8,128)S(1)} %get-tuple-element.30, f32[16,2048]{1,0:T(8,128)} %get-tuple-element.32, f32[]{:T(128)S(6)} %select_n.209, pred[]{:T(512)S(6)} %ne.27, ...), kind=kLoop, calls=%fused_computation.53 | loop fusion | flops 360448 | bytes 720901 | tf_op jit(solution)/shard_map/convert_element_type | solution.py:366
  52.5 2.3 %collective-permute-start.5 = (bf16[32,2048]{1,0:T(8,128)(2,1)}, bf16[32,2048]{1,0:T(8,128)(2,1)}, u32[]{:S(2)}, u32[]{:S(2)}) collective-permute-start(bf16[32,2048]{1,0:T(8,128)(2,1)} %pad_maximum_fusion.2), channel_id=1, source_target_pairs={{0,8},{1,9},{2,10},{3,11},{4,12},{5,13},{6,14},{7,15},{8,0},{9,1},... | collective-permute-start | bytes 393224 | tf_op jit(solution)/shard_map/ppermute | solution.py:18
  60.2 1.2 %copy-done.12 = bf16[128,4096]{1,0:T(8,128)(2,1)S(1)} copy-done((bf16[128,4096]{1,0:T(8,128)(2,1)S(1)}, bf16[128,4096]{1,0:T(8,128)(2,1)}, u32[]{:S(2)}) %copy-start.12) | copy-done | bytes 1048600
  62.4 8.1 %middle.1 = (f32[128,4096]{1,0:T(8,128)S(1)}, f32[128,4096]{1,0:T(8,128)S(1)}) custom-call(s32[6]{0:T(128)S(1)} %broadcast_subtract_fusion.starts_ref, bf16[3,128,4096]{2,1,0:T(8,128)(2,1)S(1)} %copy-done.1, bf16[3,2,4096]{2,1,0:T(2,128)(2,1)S(1)} %broadcast_select_fusion.halo_ref, f32[3,3,4096]{2,1,0:T(4,128)S(1)} %copy-done.14, ...), custom_call_target="tpu_custom_call" | custom-call | flops 10000000 | bytes 8388608 | tf_op jit(solution)/shard_map/middle/pallas_call | solution.py:340
  70.7 1.3 %select_convert_fusion.1 = (bf16[16,2048]{1,0:T(8,128)(2,1)S(1)}, bf16[16,2048]{1,0:T(8,128)(2,1)S(1)}, f32[16,2048]{1,0:T(8,128)S(1)}, f32[16,2048]{1,0:T(8,128)S(1)}) fusion(pred[]{:T(512)S(6)} %eq.9, f32[16,2048]{1,0:T(8,128)S(1)} %copy-done.19, f32[16,2048]{1,0:T(8,128)S(1)} %copy-done.17, f32[]{:T(128)S(6)} %select_n.184, ...), kind=kLoop, calls=%fused_computation.62 | loop fusion | flops 2031616 | bytes 1703960 | tf_op jit(solution)/shard_map/convert_element_type | solution.py:366
  73.0 4.8 %collective-permute-start.6 = (bf16[32,2048]{1,0:T(8,128)(2,1)S(1)}, bf16[32,2048]{1,0:T(8,128)(2,1)S(1)}, u32[]{:S(2)}, u32[]{:S(2)}) collective-permute-start(bf16[32,2048]{1,0:T(8,128)(2,1)S(1)} %pad_maximum_fusion.4), channel_id=1, source_target_pairs={{0,1},{1,0},{2,3},{3,2},{4,5},{5,4},{6,7},{7,6},{8,9},{9,8},{10,11... | collective-permute-start | bytes 393224 | tf_op jit(solution)/shard_map/ppermute | solution.py:18
  77.8 1.0 %collective-permute-done.6.other_ref = bf16[32,2048]{1,0:T(8,128)(2,1)S(1)} collective-permute-done((bf16[32,2048]{1,0:T(8,128)(2,1)S(1)}, bf16[32,2048]{1,0:T(8,128)(2,1)S(1)}, u32[]{:S(2)}, u32[]{:S(2)}) %collective-permute-start.6) | collective-permute-done | bytes 131104 | tf_op jit(solution)/shard_map/ppermute | solution.py:18
  78.7 11.5 %back.1 = bf16[128,4096]{1,0:T(8,128)(2,1)} custom-call(s32[6]{0:T(128)S(1)} %broadcast_subtract_fusion.starts_ref, s32[1]{0:T(128)} %bitcast.core_ref, bf16[32,2048]{1,0:T(8,128)(2,1)S(1)} %pad_maximum_fusion.3.own_ref, bf16[32,2048]{1,0:T(8,128)(2,1)S(1)} %collective-permute-done.6.other_ref, f32[8,32,4096]{2,1,0:T(8,128)S(1)} %copy-done.6, ...), custom_call_target="tpu_custom_call" | custom-call | tf_op jit(solution)/shard_map/back/pallas_call | solution.py:403
  (70 shorter events, 13.2 us)
Async XLA Ops:
  1.0 8.3 %collective-permute-start.1 = (bf16[3,2,4096]{2,1,0:T(2,128)(2,1)S(1)}, bf16[3,2,4096]{2,1,0:T(2,128)(2,1)S(1)}, u32[]{:S(2)}, u32[]{:S(2)}) collective-permute-start(bf16[3,2,4096]{2,1,0:T(2,128)(2,1)S(1)} %slice.41), channel_id=1, source_target_pairs={{1,2},{3,4},{5,6},{7,8},{9,10},{11,12},{13,14},{2,1},{4,3},{6,5},{... | collective-permute-start | bytes 147464 | tf_op jit(solution)/shard_map/ppermute | solution.py:284
  5.5 3.8 %collective-permute-start = (bf16[3,2,4096]{2,1,0:T(2,128)(2,1)S(1)}, bf16[3,2,4096]{2,1,0:T(2,128)(2,1)S(1)}, u32[]{:S(2)}, u32[]{:S(2)}) collective-permute-start(bf16[3,2,4096]{2,1,0:T(2,128)(2,1)S(1)} %slice.41), channel_id=1, source_target_pairs={{0,1},{1,0},{2,3},{3,2},{4,5},{5,4},{6,7},{7,6},{8,9},{9,8},{10,11... | collective-permute-start | bytes 147464 | tf_op jit(solution)/shard_map/ppermute | solution.py:18
  9.3 13.6 %copy-start.2 = (f32[16,4096]{1,0:T(8,128)}, f32[16,4096]{1,0:T(8,128)S(1)}, u32[]{:S(2)}) copy-start(f32[16,4096]{1,0:T(8,128)S(1)} %get-tuple-element.48.pim_ref) | copy-start | bytes 786436
  9.4 1.9 %copy-start = (bf16[3,128,4096]{2,1,0:T(8,128)(2,1)S(1)}, bf16[3,128,4096]{2,1,0:T(8,128)(2,1)}, u32[]{:S(2)}) copy-start(bf16[3,128,4096]{2,1,0:T(8,128)(2,1)} %f1_ref.1) | copy-start | bytes 9437188
  22.9 1.9 %copy-start.5 = (f32[8,32,4096]{2,1,0:T(8,128)}, f32[8,32,4096]{2,1,0:T(8,128)S(1)}, u32[]{:S(2)}) copy-start(f32[8,32,4096]{2,1,0:T(8,128)S(1)} %get-tuple-element.11.e_ref) | copy-start | bytes 12582916
  27.2 2.0 %collective-permute-start.2 = (bf16[32,2048]{1,0:T(8,128)(2,1)}, bf16[32,2048]{1,0:T(8,128)(2,1)}, u32[]{:S(2)}, u32[]{:S(2)}) collective-permute-start(bf16[32,2048]{1,0:T(8,128)(2,1)} %dynamic-slice_bitcast_fusion), channel_id=1, source_target_pairs={{0,1},{1,0},{2,3},{3,2},{4,5},{5,4},{6,7},{7,6},{8,9},{9,8},{10,11... | collective-permute-start | bytes 393224 | tf_op jit(solution)/shard_map/ppermute | solution.py:18
  27.7 29.7 %copy-start.1 = (bf16[3,128,4096]{2,1,0:T(8,128)(2,1)S(1)}, bf16[3,128,4096]{2,1,0:T(8,128)(2,1)}, u32[]{:S(2)}) copy-start(bf16[3,128,4096]{2,1,0:T(8,128)(2,1)} %f1_ref.1) | copy-start | bytes 9437188
  27.7 29.7 %copy-start.15 = (f32[4096]{0:T(1024)S(1)}, f32[4096]{0:T(1024)}, u32[]{:S(2)}) copy-start(f32[4096]{0:T(1024)} %param.9) | copy-start | bytes 49156
  31.6 2.3 %copy-start.18 = (f32[16,2048]{1,0:T(8,128)}, f32[16,2048]{1,0:T(8,128)S(1)}, u32[]{:S(2)}) copy-start(f32[16,2048]{1,0:T(8,128)S(1)} %get-tuple-element.40) | copy-start | bytes 393220
  34.5 5.3 %collective-permute-start.3 = (bf16[32,2048]{1,0:T(8,128)(2,1)}, bf16[32,2048]{1,0:T(8,128)(2,1)}, u32[]{:S(2)}, u32[]{:S(2)}) collective-permute-start(bf16[32,2048]{1,0:T(8,128)(2,1)} %pad_maximum_fusion), channel_id=1, source_target_pairs={{0,2},{1,3},{2,0},{3,1},{4,6},{5,7},{6,4},{7,5},{8,10},{9,11},{10,... | collective-permute-start | bytes 393224 | tf_op jit(solution)/shard_map/ppermute | solution.py:18
  41.7 2.4 %copy-start.22 = (f32[16,2048]{1,0:T(8,128)}, f32[16,2048]{1,0:T(8,128)S(1)}, u32[]{:S(2)}) copy-start(f32[16,2048]{1,0:T(8,128)S(1)} %get-tuple-element.34) | copy-start | bytes 393220
  44.8 4.1 %collective-permute-start.4 = (bf16[32,2048]{1,0:T(8,128)(2,1)}, bf16[32,2048]{1,0:T(8,128)(2,1)}, u32[]{:S(2)}, u32[]{:S(2)}) collective-permute-start(bf16[32,2048]{1,0:T(8,128)(2,1)} %pad_maximum_fusion.1), channel_id=1, source_target_pairs={{0,4},{1,5},{2,6},{3,7},{4,0},{5,1},{6,2},{7,3},{8,12},{9,13},{10,... | collective-permute-start | bytes 393224 | tf_op jit(solution)/shard_map/ppermute | solution.py:18
  50.1 1.7 %copy-start.26 = (f32[16,2048]{1,0:T(8,128)}, f32[16,2048]{1,0:T(8,128)S(1)}, u32[]{:S(2)}) copy-start(f32[16,2048]{1,0:T(8,128)S(1)} %get-tuple-element.30) | copy-start | bytes 393220
  52.5 18.1 %collective-permute-start.5 = (bf16[32,2048]{1,0:T(8,128)(2,1)}, bf16[32,2048]{1,0:T(8,128)(2,1)}, u32[]{:S(2)}, u32[]{:S(2)}) collective-permute-start(bf16[32,2048]{1,0:T(8,128)(2,1)} %pad_maximum_fusion.2), channel_id=1, source_target_pairs={{0,8},{1,9},{2,10},{3,11},{4,12},{5,13},{6,14},{7,15},{8,0},{9,1},... | collective-permute-start | bytes 393224 | tf_op jit(solution)/shard_map/ppermute | solution.py:18
  62.4 8.2 %copy-start.10 = (bf16[2,32,2048]{2,1,0:T(8,128)(2,1)S(1)}, bf16[2,32,2048]{2,1,0:T(8,128)(2,1)}, u32[]{:S(2)}) copy-start(bf16[2,32,2048]{2,1,0:T(8,128)(2,1)} %copy-done.9) | copy-start | bytes 786436
  62.4 8.2 %copy-start.17 = (f32[16,2048]{1,0:T(8,128)S(1)}, f32[16,2048]{1,0:T(8,128)}, u32[]{:S(2)}) copy-start(f32[16,2048]{1,0:T(8,128)} %copy-done.16) | copy-start | bytes 393220
  62.4 8.2 %copy-start.19 = (f32[16,2048]{1,0:T(8,128)S(1)}, f32[16,2048]{1,0:T(8,128)}, u32[]{:S(2)}) copy-start(f32[16,2048]{1,0:T(8,128)} %copy-done.18) | copy-start | bytes 393220
  62.4 8.3 %copy-start.21 = (f32[16,2048]{1,0:T(8,128)S(1)}, f32[16,2048]{1,0:T(8,128)}, u32[]{:S(2)}) copy-start(f32[16,2048]{1,0:T(8,128)} %copy-done.20) | copy-start | bytes 393220
  62.4 8.3 %copy-start.23 = (f32[16,2048]{1,0:T(8,128)S(1)}, f32[16,2048]{1,0:T(8,128)}, u32[]{:S(2)}) copy-start(f32[16,2048]{1,0:T(8,128)} %copy-done.22) | copy-start | bytes 393220
  62.4 8.3 %copy-start.25 = (f32[16,2048]{1,0:T(8,128)S(1)}, f32[16,2048]{1,0:T(8,128)}, u32[]{:S(2)}) copy-start(f32[16,2048]{1,0:T(8,128)} %copy-done.24) | copy-start | bytes 393220
  62.4 8.3 %copy-start.27 = (f32[16,2048]{1,0:T(8,128)S(1)}, f32[16,2048]{1,0:T(8,128)}, u32[]{:S(2)}) copy-start(f32[16,2048]{1,0:T(8,128)} %copy-done.26) | copy-start | bytes 393220
  62.4 16.3 %copy-start.4 = (f32[16,4096]{1,0:T(8,128)S(1)}, f32[16,4096]{1,0:T(8,128)}, u32[]{:S(2)}) copy-start(f32[16,4096]{1,0:T(8,128)} %copy-done.2) | copy-start | bytes 786436
  62.4 16.3 %copy-start.6 = (f32[8,32,4096]{2,1,0:T(8,128)S(1)}, f32[8,32,4096]{2,1,0:T(8,128)}, u32[]{:S(2)}) copy-start(f32[8,32,4096]{2,1,0:T(8,128)} %copy-done.5) | copy-start | bytes 12582916
  73.0 5.8 %collective-permute-start.6 = (bf16[32,2048]{1,0:T(8,128)(2,1)S(1)}, bf16[32,2048]{1,0:T(8,128)(2,1)S(1)}, u32[]{:S(2)}, u32[]{:S(2)}) collective-permute-start(bf16[32,2048]{1,0:T(8,128)(2,1)S(1)} %pad_maximum_fusion.4), channel_id=1, source_target_pairs={{0,1},{1,0},{2,3},{3,2},{4,5},{5,4},{6,7},{7,6},{8,9},{9,8},{10,11... | collective-permute-start | bytes 393224 | tf_op jit(solution)/shard_map/ppermute | solution.py:18
  (11 other events, 9.6 us)

commit v2 on v1

v2 whole, which is shorter than its diff:
```python
import functools

import jax
import jax.numpy as jnp
from jax import lax
from jax.experimental import pallas as pl
from jax.experimental.pallas import tpu as pltpu
from jax.sharding import PartitionSpec as P

BLK = 16
LANE = 128
SUB = 8
TILE = 512
F32 = jnp.float32
BF16 = jnp.bfloat16


def exchange(block, distance):
    devices = range(lax.axis_size("seq"))
    return lax.ppermute(block, "seq", [(i, i ^ distance) for i in devices])


def row_iota(rows):
    return lax.broadcasted_iota(jnp.int32, (rows, LANE), 0)


def starts_of(lengths_ref, origin):
    starts, at = [], -origin
    for i in range(lengths_ref.shape[0]):
        starts.append(at)
        at = at + lengths_ref[i]
    return starts


def none_in(starts, first, beyond):
    hit = jnp.int32(0)
    for s in starts:
        hit = hit | ((s >= first) & (s < beyond)).astype(jnp.int32)
    return (1 - hit).astype(F32)


def block_flags(starts, count):
    return [none_in(starts, b * BLK, (b + 1) * BLK) for b in range(count)]


def tap_masks(starts, tokens):
    t = row_iota(tokens)
    here = jnp.zeros((tokens, LANE), jnp.bool_)
    before = jnp.zeros((tokens, LANE), jnp.bool_)
    for s in starts:
        here = here | (t == s)
        before = before | (t - 1 == s)
    mask_one = jnp.where(here, 0.0, 1.0)
    return mask_one, jnp.where(here | before, 0.0, 1.0)


def short_filter(rows, halo, taps, mask_one, mask_two):
    values = rows.astype(F32)
    edge = halo.astype(F32)
    first, second = edge[0:1, :], edge[1:2, :]
    row = row_iota(values.shape[0])
    behind = jnp.where(row == 0, second, pltpu.roll(values, 1, 0))
    further = jnp.where(row == 0, first, jnp.where(row == 1, second, pltpu.roll(values, 2, 0)))
    conv = taps[0:1, :] * values
    conv = conv + taps[1:2, :] * behind * mask_one
    return conv + taps[2:3, :] * further * mask_two


def lane_tile(tile):
    return pl.ds(pl.multiple_of(tile * LANE, LANE), LANE)


def cmul(a_re, a_im, b_re, b_im):
    return a_re * b_re - a_im * b_im, a_re * b_im + a_im * b_re


def column_sums(parts):
    row = lax.broadcasted_iota(jnp.int32, (SUB, LANE), 0)
    low = row < 4
    level = []
    for b in range(4):
        keep = jnp.where(low, parts[b], parts[b + 4])
        move = jnp.where(low, parts[b + 4], parts[b])
        level.append(keep + pltpu.roll(move, 4, 0))
    for step in (2, 1):
        clear = (row & step) == 0
        level = [
            jnp.where(
                clear,
                level[b] + pltpu.roll(level[b], SUB - step, 0),
                level[b + step] + pltpu.roll(level[b + step], step, 0),
            )
            for b in range(step)
        ]
    return level[0]


def rows_of(ref, h, lanes):
    return ref[pl.ds(h * SUB, SUB), lanes]


def tables_kernel(place_ref, decay_ref, freq_ref, residues_ref, pole_ref, coef_ref, gate_ref, before_ref,
                  *, tokens):
    modes, width = decay_ref.shape
    half = width // 2
    place = place_ref[0]
    rounds = gate_ref.shape[0]

    @pl.loop(0, width // LANE)
    def _(tile):
        lanes = lane_tile(tile)
        decay, x = decay_ref[:, lanes], freq_ref[:, lanes]
        fade = jnp.exp(-decay)
        s = x * x
        sine = x * (1 + s * (-1 / 6 + s * (1 / 120 + s * (-1 / 5040 + s * (1 / 362880)))))
        cosine = 1 + s * (-1 / 2 + s * (1 / 24 + s * (-1 / 720 + s * (1 / 40320 - s * (1 / 3628800)))))
        pole_ref[0:modes, lanes] = fade * cosine
        pole_ref[modes : 2 * modes, lanes] = fade * sine
        d = 2 * decay
        scale = jnp.sqrt(d * (1 - d * (1 / 2 - d * (1 / 6 - d * (1 / 24 - d * (1 / 120 - d * (1 / 720)))))))
        coef_ref[0:modes, lanes] = residues_ref[0, :, lanes] * scale
        coef_ref[modes : 2 * modes, lanes] = residues_ref[1, :, lanes] * scale

    @pl.loop(0, half // LANE)
    def _(tile):
        lanes = lane_tile(tile)
        from_lane = pl.ds(pl.multiple_of((place & 1) * half + tile * LANE, LANE), LANE)
        gate = pole_ref[0:modes, from_lane], pole_ref[modes : 2 * modes, from_lane]
        reach = 1
        while reach < tokens:
            gate = cmul(*gate, *gate)
            reach *= 2
        before = jnp.ones_like(gate[0]), jnp.zeros_like(gate[0])
        for k in range(rounds):
            gate_ref[k, 0:modes, lanes], gate_ref[k, modes : 2 * modes, lanes] = gate
            before_ref[k, 0:modes, lanes], before_ref[k, modes : 2 * modes, lanes] = before
            if k:
                upper = (place & (1 << k)) != 0
                moved = cmul(*before, *gate)
                before = tuple(jnp.where(upper, a, b) for a, b in zip(moved, before))
            gate = cmul(*gate, *gate)


def front_kernel(lengths_ref, place_ref, f0_ref, f2_ref, halo_ref, taps_ref, pole_ref,
                 z_ref, e_ref, end_ref, one_s, two_s, last_s, z_s):
    tokens, width = z_ref.shape
    count = tokens // BLK
    modes = pole_ref.shape[0] // 2
    halves = modes // SUB
    starts = starts_of(lengths_ref, place_ref[0] * tokens)

    @pl.when(pl.program_id(0) == 0)
    def _():
        mask_one, mask_two = tap_masks(starts, tokens)
        one_s[...] = mask_one
        two_s[...] = mask_two
        t = row_iota(tokens)
        last = jnp.full((tokens, LANE), -1, jnp.int32)
        for s in starts:
            last = jnp.maximum(last, jnp.where(s <= (t | (BLK - 1)), s, -1))
        last_s[...] = jnp.where(t >= last, 1.0, 0.0)

    flags = block_flags(starts, count)

    @pl.loop(0, width // LANE)
    def _(tile):
        lanes = lane_tile(tile)
        mask_one, mask_two = one_s[...], two_s[...]
        conv0 = short_filter(f0_ref[0, :, lanes], halo_ref[0, :, lanes], taps_ref[0, :, lanes], mask_one, mask_two)
        conv2 = short_filter(f2_ref[0, :, lanes], halo_ref[2, :, lanes], taps_ref[2, :, lanes], mask_one, mask_two)
        z = (conv0 * conv2).astype(BF16)
        z_ref[:, lanes] = z
        z_s[...] = z.astype(F32) * last_s[...]
        p_re = [rows_of(pole_ref, h, lanes) for h in range(halves)]
        p_im = [rows_of(pole_ref, halves + h, lanes) for h in range(halves)]
        pow_re, pow_im = list(p_re), list(p_im)
        e_re, e_im = [], []
        for b in range(count):
            here = z_s[pl.ds(b * BLK + BLK - 1, SUB, stride=0), :]
            prev = z_s[pl.ds(b * BLK + BLK - 2, SUB, stride=0), :]
            e_re.append([here + p_re[h] * prev for h in range(halves)])
            e_im.append([p_im[h] * prev for h in range(halves)])
        for k in range(2, BLK):
            for h in range(halves):
                pow_re[h], pow_im[h] = cmul(pow_re[h], pow_im[h], p_re[h], p_im[h])
            for b in range(count):
                here = z_s[pl.ds(b * BLK + BLK - 1 - k, SUB, stride=0), :]
                for h in range(halves):
                    e_re[b][h] = e_re[b][h] + pow_re[h] * here
                    e_im[b][h] = e_im[b][h] + pow_im[h] * here
        for h in range(halves):
            g_re, g_im = cmul(pow_re[h], pow_im[h], p_re[h], p_im[h])
            end_re, end_im = e_re[0][h], e_im[0][h]
            for b in range(count):
                if b:
                    move_re, move_im = cmul(g_re, g_im, end_re, end_im)
                    end_re = flags[b] * move_re + e_re[b][h]
                    end_im = flags[b] * move_im + e_im[b][h]
                e_ref[b, pl.ds(h * SUB, SUB), lanes] = e_re[b][h]
                e_ref[b, pl.ds(modes + h * SUB, SUB), lanes] = e_im[b][h]
            end_ref[pl.ds(h * SUB, SUB), lanes] = end_re.astype(BF16)
            end_ref[pl.ds(modes + h * SUB, SUB), lanes] = end_im.astype(BF16)


def middle_kernel(lengths_ref, place_ref, f1_ref, halo_ref, taps_ref, z_ref, skip_ref, pole_ref, coef_ref,
                  base_ref, gain_ref, one_s, two_s, first_s, part_s, z_s, filt_s, acc_s):
    tokens, width = z_ref.shape
    count = tokens // BLK
    modes = pole_ref.shape[0] // 2
    halves = modes // SUB
    starts = starts_of(lengths_ref, place_ref[0] * tokens)

    @pl.when(pl.program_id(0) == 0)
    def _():
        mask_one, mask_two = tap_masks(starts, tokens)
        one_s[...] = mask_one
        two_s[...] = mask_two
        t = row_iota(tokens)
        t0 = t & (-BLK)
        piece = jnp.zeros((tokens, LANE), jnp.int32)
        opened = jnp.zeros((tokens, LANE), jnp.bool_)
        for s in starts:
            piece = piece + jnp.where((s > t0) & (s <= t), 1, 0)
            opened = opened | ((s >= t0) & (s <= t))
        part_s[...] = piece.astype(F32)
        first_s[...] = jnp.where(opened, 0.0, 1.0)

    pieces = jnp.int32(1)
    for b in range(count):
        inside = jnp.int32(1)
        for s in starts:
            inside = inside + ((s > b * BLK) & (s < (b + 1) * BLK)).astype(jnp.int32)
        pieces = jnp.maximum(pieces, inside)

    @pl.loop(0, width // LANE)
    def _(tile):
        lanes = lane_tile(tile)
        p_re = [rows_of(pole_ref, h, lanes) for h in range(halves)]
        p_im = [rows_of(pole_ref, halves + h, lanes) for h in range(halves)]
        q_re = [rows_of(coef_ref, h, lanes) for h in range(halves)]
        q_im = [rows_of(coef_ref, halves + h, lanes) for h in range(halves)]
        filt_s[pl.ds(0, BLK), :] = jnp.zeros((BLK, LANE), F32)
        for group in range(BLK // SUB):
            parts = []
            for k in range(SUB):
                parts.append(sum(q_re[1:], q_re[0]))
                for h in range(halves):
                    q_re[h], q_im[h] = cmul(q_re[h], q_im[h], p_re[h], p_im[h])
            filt_s[pl.ds(BLK + group * SUB, SUB), :] = column_sums(parts).astype(BF16).astype(F32)
        acc_s[...] = skip_ref[:, lanes] * z_ref[:, lanes].astype(F32)

        def one_piece(q, carry):
            mask = jnp.where(part_s[...] == q.astype(F32), 1.0, 0.0)
            z_s[...] = z_ref[:, lanes].astype(F32) * mask
            sums = [[None] * 2 for _ in range(count)]
            for s in range(BLK):
                for r in range(BLK // SUB):
                    if s >= (r + 1) * SUB:
                        continue
                    column = filt_s[pl.ds(BLK - s + r * SUB, SUB), :]
                    for b in range(count):
                        term = column * z_s[pl.ds(b * BLK + s, SUB, stride=0), :]
                        sums[b][r] = term if s == 0 else sums[b][r] + term
            for b in range(count):
                for r in range(BLK // SUB):
                    rows = pl.ds(b * BLK + r * SUB, SUB)
                    here = jnp.where(part_s[rows, :] == q.astype(F32), sums[b][r], 0.0)
                    acc_s[rows, :] = acc_s[rows, :] + here
            return carry

        lax.fori_loop(0, pieces, one_piece, 0)
        conv1 = short_filter(f1_ref[0, :, lanes], halo_ref[1, :, lanes], taps_ref[1, :, lanes], one_s[...], two_s[...])
        base_ref[:, lanes] = conv1 * acc_s[...]
        gain_ref[:, lanes] = conv1 * first_s[...]


def split(ref, lanes, *lead):
    modes = ref.shape[-2] // 2
    packed = ref[(*lead, slice(None), lanes)].astype(F32)
    return packed[:modes], packed[modes:]


def store(ref, lanes, pair):
    modes = ref.shape[-2] // 2
    ref[0:modes, lanes] = pair[0].astype(ref.dtype)
    ref[modes : 2 * modes, lanes] = pair[1].astype(ref.dtype)


def advance(gate, flag, state, addend):
    re, im = cmul(*gate, *state)
    return addend[0] + flag * re, addend[1] + flag * im


def choose(flag, a, b):
    return tuple(jnp.where(flag, x, y) for x, y in zip(a, b))


def first_kernel(lengths_ref, place_ref, kept_ref, came_ref, gate_ref, total_ref, send_ref, *, tokens):
    starts = starts_of(lengths_ref, 0)
    place = place_ref[0]
    odd = (place & 1) == 1
    second = place | 1
    flag = none_in(starts, second * tokens, (second + 1) * tokens)

    @pl.loop(0, kept_ref.shape[1] // LANE)
    def _(tile):
        lanes = lane_tile(tile)
        kept, came = split(kept_ref, lanes), split(came_ref, lanes)
        total = advance(split(gate_ref, lanes, 0), flag, choose(odd, came, kept), choose(odd, kept, came))
        store(total_ref, lanes, total)
        store(send_ref, lanes, total)


def round_kernel(lengths_ref, place_ref, total_ref, met_ref, prefix_ref, gate_ref, before_ref, *refs,
                 tokens, k, last):
    starts = starts_of(lengths_ref, 0)
    place = place_ref[0]
    distance = 1 << k
    upper = (place & distance) != 0
    group = (place >> k) << k
    even = (place >> 1) << 1
    later = group | distance
    enter = none_in(starts, group * tokens, even * tokens)
    enter = jnp.where(upper, enter, 0.0)
    whole = none_in(starts, later * tokens, (later + distance) * tokens)

    @pl.loop(0, met_ref.shape[1] // LANE)
    def _(tile):
        lanes = lane_tile(tile)
        met, total = split(met_ref, lanes), split(total_ref, lanes)
        prefix = split(prefix_ref, lanes) if k > 1 else (jnp.zeros_like(met[0]),) * 2
        prefix = advance(split(before_ref, lanes, k), enter, met, prefix)
        if not last:
            total_out, send_ref, prefix_out = refs
            total = advance(split(gate_ref, lanes, k), whole, choose(upper, met, total), choose(upper, total, met))
            store(total_out, lanes, total)
            store(send_ref, lanes, total)
            store(prefix_out, lanes, prefix)
        else:
            kept_ref, came_ref, own_ref, send_ref = refs
            odd = (place & 1) == 1
            kept, came = split(kept_ref, lanes), split(came_ref, lanes)
            flag = none_in(starts, even * tokens, (even + 1) * tokens)
            beyond = advance(split(gate_ref, lanes, 0), flag, prefix, choose(odd, came, kept))
            store(own_ref, lanes, choose(odd, beyond, prefix))
            store(send_ref, lanes, choose(odd, prefix, beyond))


def back_kernel(lengths_ref, place_ref, entry_ref, e_ref, pole_ref, coef_ref, base_ref, gain_ref, *refs):
    out_ref, y_s = refs[-2:]
    tokens, width = out_ref.shape
    count = tokens // BLK
    modes = pole_ref.shape[0] // 2
    halves = modes // SUB
    flags = block_flags(starts_of(lengths_ref, place_ref[0] * tokens), count)

    @pl.loop(0, width // LANE)
    def _(tile):
        lanes = lane_tile(tile)
        entry = [rows_of(entry_ref, h, lanes) for h in range(2 * halves)] if entry_ref.dtype == F32 else None
        if entry is None:
            packed = entry_ref[:, lanes].astype(F32)
            entry = [packed[h * SUB : (h + 1) * SUB] for h in range(2 * halves)]
        p_re = [rows_of(pole_ref, h, lanes) for h in range(halves)]
        p_im = [rows_of(pole_ref, halves + h, lanes) for h in range(halves)]
        q_re = [rows_of(coef_ref, h, lanes) for h in range(halves)]
        q_im = [rows_of(coef_ref, halves + h, lanes) for h in range(halves)]
        s_re, s_im = [entry[:halves]], [entry[halves:]]
        gate = [(p_re[h], p_im[h]) for h in range(halves)]
        for _ in range(BLK.bit_length() - 1):
            gate = [cmul(*g, *g) for g in gate]
        for b in range(count - 1):
            new_re, new_im = [], []
            for h in range(halves):
                move_re, move_im = cmul(*gate[h], s_re[b][h], s_im[b][h])
                new_re.append(flags[b] * move_re + e_ref[b, pl.ds(h * SUB, SUB), lanes])
                new_im.append(flags[b] * move_im + e_ref[b, pl.ds(modes + h * SUB, SUB), lanes])
            s_re.append(new_re)
            s_im.append(new_im)
        for k in range(BLK):
            for h in range(halves):
                q_re[h], q_im[h] = cmul(q_re[h], q_im[h], p_re[h], p_im[h])
            parts = []
            for b in range(count):
                part = q_re[0] * s_re[b][0] - q_im[0] * s_im[b][0]
                for h in range(1, halves):
                    part = part + q_re[h] * s_re[b][h] - q_im[h] * s_im[b][h]
                parts.append(part)
            y_s[pl.ds(k, SUB, stride=BLK), :] = column_sums(parts)
        out_ref[:, lanes] = (base_ref[:, lanes] + gain_ref[:, lanes] * y_s[...]).astype(BF16)


def per_device(features, kernel, skip, residues, decay, freq, lengths):
    tokens = features.shape[1]
    modes, width = decay.shape
    half = width // 2
    count = tokens // BLK
    n = lax.axis_size("seq")
    place = lax.axis_index("seq")
    core = place % 2
    tiles = half // TILE
    rounds = n.bit_length() - 1
    where = place.astype(jnp.int32)[None]

    rim = features[:, tokens - 2 :, :]
    inner = exchange(rim, 1)
    link = [(i, i + 1) for i in range(1, n - 1, 2)]
    outer = lax.ppermute(rim, "seq", link + [(b, a) for a, b in link])
    halo = jnp.where(core == 1, inner, outer)

    params = pltpu.CompilerParams(vmem_limit_bytes=12 * 1024 * 1024)
    plane = pltpu.VMEM((tokens, LANE), F32)
    whole = pl.BlockSpec(memory_space=pltpu.VMEM)

    def simple(body, prefetch, args, outs, name, aliases={}):
        return pl.pallas_call(
            body,
            grid_spec=pltpu.PrefetchScalarGridSpec(
                num_scalar_prefetch=len(prefetch), grid=(),
                in_specs=[whole] * len(args), out_specs=[whole] * len(outs),
            ),
            out_shape=[jax.ShapeDtypeStruct(*o) for o in outs],
            compiler_params=params, name=name,
        )(*prefetch, *args)

    packed = 2 * modes
    state, sent = ((packed, half), F32), ((packed, half), BF16)
    pole, coef, gates, befores = simple(
        functools.partial(tables_kernel, tokens=tokens), (where,), (decay, freq, residues),
        (((packed, width), F32), ((packed, width), F32), ((rounds, packed, half), F32), ((rounds, packed, half), F32)),
        "tables",
    )

    def half_of(mine, place_ref):
        core = place_ref[0] & 1
        return core if mine else 1 - core

    def call(body, mine, name, args, specs, outs, scratch, cost, aliases={}):
        return pl.pallas_call(
            body,
            grid_spec=pltpu.PrefetchScalarGridSpec(
                num_scalar_prefetch=2, grid=(tiles,), in_specs=specs,
                out_specs=[o[2] for o in outs], scratch_shapes=scratch,
            ),
            out_shape=[jax.ShapeDtypeStruct(o[0], o[1]) for o in outs],
            input_output_aliases=aliases,
            compiler_params=params, name=name,
            cost_estimate=pl.CostEstimate(flops=cost, bytes_accessed=1 << 20, transcendentals=0),
        )(lengths, where, *args)

    def columns(mine, *lead):
        zeros = (0,) * len(lead)
        return pl.BlockSpec((*lead, TILE), lambda i, n_ref, w_ref: (*zeros, half_of(mine, w_ref) * tiles + i))

    def stream(mine, r):
        return pl.BlockSpec((1, tokens, TILE), lambda i, n_ref, w_ref: (r, 0, half_of(mine, w_ref) * tiles + i))

    def local(*lead):
        zeros = (0,) * len(lead)
        return pl.BlockSpec((*lead, TILE), lambda i, *_: (*zeros, i))

    def front(mine):
        return call(
            front_kernel, mine, "front", (features, features, halo, kernel, pole),
            [stream(mine, 0), stream(mine, 2), columns(mine, 3, 2), columns(mine, 3, 3), columns(mine, packed)],
            [((tokens, half), BF16, local(tokens)), ((count, packed, half), F32, local(count, packed)),
             ((packed, half), BF16, local(packed))],
            [plane] * 4, 5_000_000,
        )

    def middle(mine, z):
        return call(
            middle_kernel, mine, "middle", (features, halo, kernel, z, skip[None], pole, coef),
            [stream(mine, 1), columns(mine, 3, 2), columns(mine, 3, 3), local(tokens), columns(mine, 1),
             columns(mine, packed), columns(mine, packed)],
            [((tokens, half), F32, local(tokens))] * 2,
            [plane] * 5 + [pltpu.VMEM((2 * BLK, LANE), F32), plane], 5_000_000,
        )

    def back(mine, entry, e, base, gain, out):
        args = (entry, e, pole, coef, base, gain)
        specs = [local(packed), local(count, packed), columns(mine, packed), columns(mine, packed),
                 local(tokens), local(tokens)]
        if out is not None:
            args, specs = args + (out,), specs + [pl.BlockSpec(memory_space=pl.ANY)]
        return call(
            back_kernel, mine, "back", args, specs, [((tokens, width), BF16, columns(mine, tokens))],
            [plane], 5_000_000, {} if out is None else {len(args) + 1: 0},
        )[0]

    z_other, e_other, end_other = front(False)
    came_start = exchange(end_other, 1)
    z_own, e_own, end_own = front(True)
    came = came_start
    total, send = simple(
        functools.partial(first_kernel, tokens=tokens), (lengths, where), (end_own, came, gates), (state, sent), "first"
    )
    prefix = total
    fillers = {1: lambda: middle(True, z_own), 2: lambda: middle(False, z_other)}
    filled = {}
    for k in range(1, rounds):
        met = exchange(send, 1 << k)
        if k in fillers:
            filled[k] = fillers[k]()
            met, filled[k] = lax.optimization_barrier((met, filled[k]))
        last = k == rounds - 1
        body = functools.partial(round_kernel, tokens=tokens, k=k, last=last)
        args = (total, met, prefix, gates, befores)
        if last:
            own, send = simple(body, (lengths, where), args + (end_own, came), (state, sent), "round")
        else:
            total, send, prefix = simple(body, (lengths, where), args, (state, sent, state), "round")
    other = exchange(send, 1)
    out = back(True, own, e_own, *filled[1], None)
    return back(False, other, e_other, *filled[2], out)


def solution(mesh):
    return jax.shard_map(
        per_device,
        mesh=mesh,
        in_specs=(P(None, ("groups", "seq"), None), P(), P(), P(), P(), P(), P("groups")),
        out_specs=P(("groups", "seq"), None),
        check_vma=False,
    )
```

time: 90.7 us -> 63.4 us (0.70)
  other arithmetic: 18.7 us -> 0.06 us
  Pallas kernels: 30.3 us -> 39.8 us
  local copies, waits for them, and re-layouts: 15.1 us -> 7.39 us
  starting transfers between devices: 14.7 us -> 7.68 us
  between operations: 4.87 us -> 0.19 us
  waiting for transfers between devices: 6.55 us -> 8.52 us
    convert_element_type x9 -> x0, other arithmetic: 12.2 us -> none  [pack(): return jnp.concatenate([pair[0].astype(BF16), pair[1].astype(BF16)], axis=0)]
    pallas_call x3 -> x11, Pallas kernels: 30.3 us -> 39.8 us  [the longest x6 35.2 us: call(): pl.pallas_call(body, grid_spec=pltpu.PrefetchScalarGridSpec(num_scalar_pr...]
    ppermute x6, starting transfers between devices: 10.2 us -> 3.14 us  [exchange(): return lax.ppermute(block, 'seq', [(i, i ^ distance) for i in devices])]
    unnamed x56 -> x18, local copies, waits for them, and re-layouts: 13.4 us -> 6.42 us
    mul x1 -> x0, other arithmetic: 2.92 us -> none  [per_device(): c_im = residues[1] * scale]
    concatenate x5 -> x0, other arithmetic: 2 us -> none  [pack(): return jnp.concatenate([pair[0].astype(BF16), pair[1].astype(BF16)], axis=0)]
    ppermute x6, waiting for transfers between devices: 6.55 us -> 8.52 us  [exchange(): return lax.ppermute(block, 'seq', [(i, i ^ distance) for i in devices])]
  transfers between devices with their start and end apart: 7 -> 7, of which waited for: 3 -> 1; matrix products, arithmetic and copies ran while one was open for 5% -> 0% of each run, Pallas kernels for 9% -> 39%
where the time goes in v2:
time: 63.4 us; the launch traced here: 63.6 us
  Pallas kernels  39.8 us (63%)
  waiting for transfers between devices  8.52 us (13%)
  starting transfers between devices  7.68 us (12%)
  local copies, waits for them, and re-layouts  7.39 us (12%)
    pallas_call x6, Pallas kernels, call(): pl.pallas_call(body, grid_spec=pltpu.PrefetchScalarGridSpec(num_scalar_pr...  35.2 us
    ppermute x6, waiting for transfers between devices, exchange(): return lax.ppermute(block, 'seq', [(i, i ^ distance) for i in devices])  8.52 us
    unnamed x18, local copies, waits for them, and re-layouts  6.42 us
    pallas_call x5, Pallas kernels, simple(): pl.pallas_call(body, grid_spec=pltpu.PrefetchScalarGridSpec(num_scalar_pr...  4.59 us
    ppermute x1, starting transfers between devices, per_device(): outer = lax.ppermute(rim, 'seq', link + [(b, a) for a, b in link])  4.54 us
    ppermute x6, starting transfers between devices, exchange(): return lax.ppermute(block, 'seq', [(i, i ^ distance) for i in devices])  3.14 us
  transfers between devices with their start and end apart: 7, of which 1 were waited for; matrix products, arithmetic and copies ran while one was open for 0% of the time, Pallas kernels for 39%

profile of v2, /device:TPU:1, one launch (start us, length us, event | category | flops | bytes accessed | tf_op | source)
XLA Modules:
  0.0 63.6 jit_solution(17659861575624332610)
XLA Ops:
  0.0 1.0 %slice.3 = bf16[3,2,4096]{2,1,0:T(2,128)(2,1)S(1)} slice(bf16[3,128,4096]{2,1,0:T(8,128)(2,1)} %f1_ref.3), slice={[0:3], [126:128], [0:4096]} | slice | bytes 98304 | tf_op jit(solution)/shard_map/slice | solution.py:405
  1.0 4.5 %collective-permute-start.1 = (bf16[3,2,4096]{2,1,0:T(2,128)(2,1)S(1)}, bf16[3,2,4096]{2,1,0:T(2,128)(2,1)S(1)}, u32[]{:S(2)}, u32[]{:S(2)}) collective-permute-start(bf16[3,2,4096]{2,1,0:T(2,128)(2,1)S(1)} %slice.3), channel_id=1, source_target_pairs={{1,2},{3,4},{5,6},{7,8},{9,10},{11,12},{13,14},{2,1},{4,3},{6,5},{... | collective-permute-start | bytes 147464 | tf_op jit(solution)/shard_map/ppermute | solution.py:408
  5.6 1.0 %copy-done.3 = f32[2,16,4096]{2,1,0:T(8,128)S(1)} copy-done((f32[2,16,4096]{2,1,0:T(8,128)S(1)}, f32[2,16,4096]{2,1,0:T(8,128)}, u32[]{:S(2)}) %copy-start.3) | copy-done | bytes 524312
  6.7 0.9 %copy-done.4 = f32[16,4096]{1,0:T(8,128)S(1)} copy-done((f32[16,4096]{1,0:T(8,128)S(1)}, f32[16,4096]{1,0:T(8,128)}, u32[]{:S(2)}) %copy-start.4) | copy-done | bytes 262168
  7.6 0.9 %copy-done.5 = f32[16,4096]{1,0:T(8,128)S(1)} copy-done((f32[16,4096]{1,0:T(8,128)S(1)}, f32[16,4096]{1,0:T(8,128)}, u32[]{:S(2)}) %copy-start.5) | copy-done | bytes 262168
  8.6 1.3 %tables.1 = (f32[32,4096]{1,0:T(8,128)S(1)}, f32[32,4096]{1,0:T(8,128)S(1)}, f32[4,32,2048]{2,1,0:T(8,128)S(1)}, f32[4,32,2048]{2,1,0:T(8,128)S(1)}) custom-call(s32[1]{0:T(128)} %bitcast.place_ref, f32[16,4096]{1,0:T(8,128)S(1)} %copy-done.4, f32[16,4096]{1,0:T(8,128)S(1)} %copy-done.5, f32[2,16,4096]{2,1,0:T(8,128)S(1)} %copy-done.3), custom_call_target="tpu_custom_call" | custom-call | tf_op jit(solution)/shard_map/tables/pallas_call | solution.py:416
  9.9 1.9 %copy-done = bf16[3,128,4096]{2,1,0:T(8,128)(2,1)S(1)} copy-done((bf16[3,128,4096]{2,1,0:T(8,128)(2,1)S(1)}, bf16[3,128,4096]{2,1,0:T(8,128)(2,1)}, u32[]{:S(2)}) %copy-start) | copy-done | bytes 3145752
  11.8 0.9 %copy-done.2 = f32[3,3,4096]{2,1,0:T(4,128)S(1)} copy-done((f32[3,3,4096]{2,1,0:T(4,128)S(1)}, f32[3,3,4096]{2,1,0:T(4,128)}, u32[]{:S(2)}) %copy-start.2) | copy-done | bytes 147480
  12.8 0.7 %copy-done.7 = s32[6]{0:T(128)S(1)} copy-done((s32[6]{0:T(128)S(1)}, s32[6]{0:T(128)}, u32[]{:S(2)}) %copy-start.7) | copy-done | bytes 48
  13.4 5.7 %front.3 = (bf16[128,2048]{1,0:T(8,128)(2,1)S(1)}, f32[8,32,2048]{2,1,0:T(8,128)S(1)}, bf16[32,2048]{1,0:T(8,128)(2,1)S(1)}) custom-call(s32[6]{0:T(128)S(1)} %copy-done.7, s32[1]{0:T(128)} %bitcast.place_ref, bf16[3,128,4096]{2,1,0:T(8,128)(2,1)S(1)} %copy-done, bf16[3,128,4096]{2,1,0:T(8,128)(2,1)S(1)} %copy-done, ...), custom_call_target="tpu_custom_call" | custom-call | flops 5000000 | bytes 1048576 | tf_op jit(solution)/shard_map/front/pallas_call | solution.py:439
  19.2 0.5 collective-permute-start.2
  19.7 5.7 %front.2 = (bf16[128,2048]{1,0:T(8,128)(2,1)S(1)}, f32[8,32,2048]{2,1,0:T(8,128)S(1)}, bf16[32,2048]{1,0:T(8,128)(2,1)S(1)}) custom-call(s32[6]{0:T(128)S(1)} %copy-done.8, s32[1]{0:T(128)} %bitcast.place_ref, bf16[3,128,4096]{2,1,0:T(8,128)(2,1)S(1)} %copy-done, bf16[3,128,4096]{2,1,0:T(8,128)(2,1)S(1)} %copy-done, ...), custom_call_target="tpu_custom_call" | custom-call | flops 5000000 | bytes 1048576 | tf_op jit(solution)/shard_map/front/pallas_call | solution.py:439
  25.5 0.8 %first.1 = (f32[32,2048]{1,0:T(8,128)S(1)}, bf16[32,2048]{1,0:T(8,128)(2,1)S(1)}) custom-call(s32[6]{0:T(128)S(1)} %copy-done.8, s32[1]{0:T(128)} %bitcast.place_ref, bf16[32,2048]{1,0:T(8,128)(2,1)S(1)} %get-tuple-element.36.kept_ref.refs_0_, bf16[32,2048]{1,0:T(8,128)(2,1)S(1)} %collective-permute-done.2.came_ref.refs_1_, ...), custom_call_target="tpu_custom_call" | custom-call | tf_op jit(solution)/shard_map/first/pallas_call | solution.py:416
  26.3 1.3 %collective-permute-start.3 = (bf16[32,2048]{1,0:T(8,128)(2,1)S(1)}, bf16[32,2048]{1,0:T(8,128)(2,1)S(1)}, u32[]{:S(2)}, u32[]{:S(2)}) collective-permute-start(bf16[32,2048]{1,0:T(8,128)(2,1)S(1)} %get-tuple-element.40), channel_id=1, source_target_pairs={{0,2},{1,3},{2,0},{3,1},{4,6},{5,7},{6,4},{7,5},{8,10},{9,11},{10,... | collective-permute-start | bytes 393224 | tf_op jit(solution)/shard_map/ppermute | solution.py:20
  27.6 5.6 %middle.2 = (f32[128,2048]{1,0:T(8,128)S(1)}, f32[128,2048]{1,0:T(8,128)S(1)}) custom-call(s32[6]{0:T(128)S(1)} %copy-done.8, s32[1]{0:T(128)} %bitcast.place_ref, bf16[3,128,4096]{2,1,0:T(8,128)(2,1)S(1)} %copy-done.1, bf16[3,2,4096]{2,1,0:T(2,128)(2,1)S(1)} %broadcast_select_fusion.halo_ref, f32[3,3,4096]{2,1,0:T(4,128)S(1)} %copy-done.2, ...), custom_call_target="tpu_custom_call" | custom-call | flops 5000000 | bytes 1048576 | tf_op jit(solution)/shard_map/middle/pallas_call | solution.py:439
  33.2 0.8 %round.3 = (f32[32,2048]{1,0:T(8,128)S(1)}, bf16[32,2048]{1,0:T(8,128)(2,1)S(1)}, f32[32,2048]{1,0:T(8,128)S(1)}) custom-call(s32[6]{0:T(128)S(1)} %copy-done.8, s32[1]{0:T(128)} %bitcast.place_ref, f32[32,2048]{1,0:T(8,128)S(1)} %get-tuple-element.39.total_ref.prefix_ref, bf16[32,2048]{1,0:T(8,128)(2,1)S(1)} %collective-permute-done.3.met_ref, ...), custom_call_target="tpu_custom_call" | custom-call | tf_op jit(solution)/shard_map/round/pallas_call | solution.py:416
  34.2 5.6 %middle.3 = (f32[128,2048]{1,0:T(8,128)S(1)}, f32[128,2048]{1,0:T(8,128)S(1)}) custom-call(s32[6]{0:T(128)S(1)} %copy-done.8, s32[1]{0:T(128)} %bitcast.place_ref, bf16[3,128,4096]{2,1,0:T(8,128)(2,1)S(1)} %copy-done.1, bf16[3,2,4096]{2,1,0:T(2,128)(2,1)S(1)} %broadcast_select_fusion.halo_ref, f32[3,3,4096]{2,1,0:T(4,128)S(1)} %copy-done.2, ...), custom_call_target="tpu_custom_call" | custom-call | flops 5000000 | bytes 1048576 | tf_op jit(solution)/shard_map/middle/pallas_call | solution.py:439
  39.9 0.8 %round.4 = (f32[32,2048]{1,0:T(8,128)S(1)}, bf16[32,2048]{1,0:T(8,128)(2,1)S(1)}, f32[32,2048]{1,0:T(8,128)S(1)}) custom-call(s32[6]{0:T(128)S(1)} %copy-done.8, s32[1]{0:T(128)} %bitcast.place_ref, f32[32,2048]{1,0:T(8,128)S(1)} %get-tuple-element.47.total_ref, bf16[32,2048]{1,0:T(8,128)(2,1)S(1)} %collective-permute-done.4.met_ref, ...), custom_call_target="tpu_custom_call" | custom-call | tf_op jit(solution)/shard_map/round/pallas_call | solution.py:416
  40.7 0.6 collective-permute-start.5
  41.3 8.5 %collective-permute-done.5.met_ref = bf16[32,2048]{1,0:T(8,128)(2,1)S(1)} collective-permute-done((bf16[32,2048]{1,0:T(8,128)(2,1)S(1)}, bf16[32,2048]{1,0:T(8,128)(2,1)S(1)}, u32[]{:S(2)}, u32[]{:S(2)}) %collective-permute-start.5) | collective-permute-done | bytes 131104 | tf_op jit(solution)/shard_map/ppermute | solution.py:20
  49.8 0.9 %round.5 = (f32[32,2048]{1,0:T(8,128)S(1)}, bf16[32,2048]{1,0:T(8,128)(2,1)S(1)}) custom-call(s32[6]{0:T(128)S(1)} %copy-done.8, s32[1]{0:T(128)} %bitcast.place_ref, f32[32,2048]{1,0:T(8,128)S(1)} %get-tuple-element.54.total_ref, bf16[32,2048]{1,0:T(8,128)(2,1)S(1)} %collective-permute-done.5.met_ref, f32[32,2048]{1,0:T(8,128)S(1)} %get-tuple-element.56.prefix_ref, ...), custom_call_target="tpu_custom_call" | custom-call | tf_op jit(solution)/shard_map/round/pallas_call | solution.py:416
  50.7 0.5 collective-permute-start.6
  51.2 6.2 %back.2.refs_0_ = bf16[128,4096]{1,0:T(8,128)(2,1)} custom-call(s32[6]{0:T(128)S(1)} %copy-done.8, s32[1]{0:T(128)} %bitcast.place_ref, f32[32,2048]{1,0:T(8,128)S(1)} %get-tuple-element.61.entry_ref, f32[8,32,2048]{2,1,0:T(8,128)S(1)} %get-tuple-element.62.e_ref, f32[32,4096]{1,0:T(8,128)S(1)} %get-tuple-element.35.pole_ref, ...), custom_call_target="tpu_custom_call" | custom-call | flops 5000000 | bytes 1048576 | tf_op jit(solution)/shard_map/back/pallas_call | solution.py:439
  57.4 6.3 %back.3 = bf16[128,4096]{1,0:T(8,128)(2,1)} custom-call(s32[6]{0:T(128)S(1)} %copy-done.8, s32[1]{0:T(128)} %bitcast.place_ref, bf16[32,2048]{1,0:T(8,128)(2,1)S(1)} %collective-permute-done.6.entry_ref, f32[8,32,2048]{2,1,0:T(8,128)S(1)} %get-tuple-element.58.e_ref, f32[32,4096]{1,0:T(8,128)S(1)} %get-tuple-element.35.pole_ref, ...), custom_call_target="tpu_custom_call", output_to_operand_aliasing={{}: (8, {})} | custom-call | flops 5000000 | bytes 1048576 | tf_op jit(solution)/shard_map/back/pallas_call | solution.py:439
  (21 shorter events, 0.4 us)
Async XLA Ops:
  1.0 8.9 %collective-permute-start.1 = (bf16[3,2,4096]{2,1,0:T(2,128)(2,1)S(1)}, bf16[3,2,4096]{2,1,0:T(2,128)(2,1)S(1)}, u32[]{:S(2)}, u32[]{:S(2)}) collective-permute-start(bf16[3,2,4096]{2,1,0:T(2,128)(2,1)S(1)} %slice.3), channel_id=1, source_target_pairs={{1,2},{3,4},{5,6},{7,8},{9,10},{11,12},{13,14},{2,1},{4,3},{6,5},{... | collective-permute-start | bytes 147464 | tf_op jit(solution)/shard_map/ppermute | solution.py:408
  5.5 4.3 %collective-permute-start = (bf16[3,2,4096]{2,1,0:T(2,128)(2,1)S(1)}, bf16[3,2,4096]{2,1,0:T(2,128)(2,1)S(1)}, u32[]{:S(2)}, u32[]{:S(2)}) collective-permute-start(bf16[3,2,4096]{2,1,0:T(2,128)(2,1)S(1)} %slice.3), channel_id=1, source_target_pairs={{0,1},{1,0},{2,3},{3,2},{4,5},{5,4},{6,7},{7,6},{8,9},{9,8},{10,11... | collective-permute-start | bytes 147464 | tf_op jit(solution)/shard_map/ppermute | solution.py:20
  5.6 1.0 %copy-start.3 = (f32[2,16,4096]{2,1,0:T(8,128)S(1)}, f32[2,16,4096]{2,1,0:T(8,128)}, u32[]{:S(2)}) copy-start(f32[2,16,4096]{2,1,0:T(8,128)} %residues_ref.1) | copy-start | bytes 1572868
  6.7 0.9 %copy-start.4 = (f32[16,4096]{1,0:T(8,128)S(1)}, f32[16,4096]{1,0:T(8,128)}, u32[]{:S(2)}) copy-start(f32[16,4096]{1,0:T(8,128)} %decay_ref.1) | copy-start | bytes 786436
  7.6 0.9 %copy-start.5 = (f32[16,4096]{1,0:T(8,128)S(1)}, f32[16,4096]{1,0:T(8,128)}, u32[]{:S(2)}) copy-start(f32[16,4096]{1,0:T(8,128)} %freq_ref.1) | copy-start | bytes 786436
  9.9 1.9 %copy-start = (bf16[3,128,4096]{2,1,0:T(8,128)(2,1)S(1)}, bf16[3,128,4096]{2,1,0:T(8,128)(2,1)}, u32[]{:S(2)}) copy-start(bf16[3,128,4096]{2,1,0:T(8,128)(2,1)} %f1_ref.3) | copy-start | bytes 9437188
  11.8 0.9 %copy-start.2 = (f32[3,3,4096]{2,1,0:T(4,128)S(1)}, f32[3,3,4096]{2,1,0:T(4,128)}, u32[]{:S(2)}) copy-start(f32[3,3,4096]{2,1,0:T(4,128)} %taps_ref.7) | copy-start | bytes 442372
  12.8 0.7 %copy-start.7 = (s32[6]{0:T(128)S(1)}, s32[6]{0:T(128)}, u32[]{:S(2)}) copy-start(s32[6]{0:T(128)} %lengths_ref.19) | copy-start | bytes 76
  13.4 6.3 %copy-start.8 = (s32[6]{0:T(128)S(1)}, s32[6]{0:T(128)}, u32[]{:S(2)}) copy-start(s32[6]{0:T(128)} %lengths_ref.19) | copy-start | bytes 76
  19.1 8.4 %copy-start.6 = (f32[4096]{0:T(1024)S(1)}, f32[4096]{0:T(1024)}, u32[]{:S(2)}) copy-start(f32[4096]{0:T(1024)} %param.9) | copy-start | bytes 49156
  19.2 6.3 %collective-permute-start.2 = (bf16[32,2048]{1,0:T(8,128)(2,1)S(1)}, bf16[32,2048]{1,0:T(8,128)(2,1)S(1)}, u32[]{:S(2)}, u32[]{:S(2)}) collective-permute-start(bf16[32,2048]{1,0:T(8,128)(2,1)S(1)} %get-tuple-element.37), channel_id=1, source_target_pairs={{0,1},{1,0},{2,3},{3,2},{4,5},{5,4},{6,7},{7,6},{8,9},{9,8},{10,11... | collective-permute-start | bytes 393224 | tf_op jit(solution)/shard_map/ppermute | solution.py:20
  19.7 7.9 %copy-start.1 = (bf16[3,128,4096]{2,1,0:T(8,128)(2,1)S(1)}, bf16[3,128,4096]{2,1,0:T(8,128)(2,1)}, u32[]{:S(2)}) copy-start(bf16[3,128,4096]{2,1,0:T(8,128)(2,1)} %f1_ref.3) | copy-start | bytes 9437188
  26.3 6.9 %collective-permute-start.3 = (bf16[32,2048]{1,0:T(8,128)(2,1)S(1)}, bf16[32,2048]{1,0:T(8,128)(2,1)S(1)}, u32[]{:S(2)}, u32[]{:S(2)}) collective-permute-start(bf16[32,2048]{1,0:T(8,128)(2,1)S(1)} %get-tuple-element.40), channel_id=1, source_target_pairs={{0,2},{1,3},{2,0},{3,1},{4,6},{5,7},{6,4},{7,5},{8,10},{9,11},{10,... | collective-permute-start | bytes 393224 | tf_op jit(solution)/shard_map/ppermute | solution.py:20
  34.0 5.8 %collective-permute-start.4 = (bf16[32,2048]{1,0:T(8,128)(2,1)S(1)}, bf16[32,2048]{1,0:T(8,128)(2,1)S(1)}, u32[]{:S(2)}, u32[]{:S(2)}) collective-permute-start(bf16[32,2048]{1,0:T(8,128)(2,1)S(1)} %get-tuple-element.48), channel_id=1, source_target_pairs={{0,4},{1,5},{2,6},{3,7},{4,0},{5,1},{6,2},{7,3},{8,12},{9,13},{10,... | collective-permute-start | bytes 393224 | tf_op jit(solution)/shard_map/ppermute | solution.py:20
  40.7 9.1 %collective-permute-start.5 = (bf16[32,2048]{1,0:T(8,128)(2,1)S(1)}, bf16[32,2048]{1,0:T(8,128)(2,1)S(1)}, u32[]{:S(2)}, u32[]{:S(2)}) collective-permute-start(bf16[32,2048]{1,0:T(8,128)(2,1)S(1)} %get-tuple-element.55), channel_id=1, source_target_pairs={{0,8},{1,9},{2,10},{3,11},{4,12},{5,13},{6,14},{7,15},{8,0},{9,1},... | collective-permute-start | bytes 393224 | tf_op jit(solution)/shard_map/ppermute | solution.py:20
  50.7 6.7 %collective-permute-start.6 = (bf16[32,2048]{1,0:T(8,128)(2,1)S(1)}, bf16[32,2048]{1,0:T(8,128)(2,1)S(1)}, u32[]{:S(2)}, u32[]{:S(2)}) collective-permute-start(bf16[32,2048]{1,0:T(8,128)(2,1)S(1)} %get-tuple-element.57), channel_id=1, source_target_pairs={{0,1},{1,0},{2,3},{3,2},{4,5},{5,4},{6,7},{7,6},{8,9},{9,8},{10,11... | collective-permute-start | bytes 393224 | tf_op jit(solution)/shard_map/ppermute | solution.py:20

commit v3 on v2

v3 whole, which is shorter than its diff:
```python
import functools

import jax
import jax.numpy as jnp
from jax import lax
from jax.experimental import pallas as pl
from jax.experimental.pallas import tpu as pltpu
from jax.sharding import PartitionSpec as P

BLK = 16
LANE = 128
SUB = 8
TILE = 512
PITCH = 40
ROOM = 49
F32 = jnp.float32
BF16 = jnp.bfloat16


def exchange(block, distance):
    devices = range(lax.axis_size("seq"))
    return lax.ppermute(block, "seq", [(i, i ^ distance) for i in devices])


def row_iota(rows):
    return lax.broadcasted_iota(jnp.int32, (rows, LANE), 0)


def starts_of(lengths_ref, origin):
    starts, at = [], -origin
    for i in range(lengths_ref.shape[0]):
        starts.append(at)
        at = at + lengths_ref[i]
    return starts


def none_in(starts, first, beyond):
    hit = jnp.int32(0)
    for s in starts:
        hit = hit | ((s >= first) & (s < beyond)).astype(jnp.int32)
    return (1 - hit).astype(F32)


def block_flags(starts, count):
    return [none_in(starts, b * BLK, (b + 1) * BLK) for b in range(count)]


def shift_matrix(starts, tokens):
    t = lax.broadcasted_iota(jnp.int32, (tokens, tokens), 0)
    u = lax.broadcasted_iota(jnp.int32, (tokens, tokens), 1)
    here = jnp.zeros((tokens, tokens), jnp.bool_)
    before = jnp.zeros((tokens, tokens), jnp.bool_)
    for s in starts:
        here = here | (t == s)
        before = before | (t - 1 == s)
    one = jnp.where((u == t - 1) & ~here, 1.0, 0.0)
    two = jnp.where((u == t - 2) & ~(here | before), 1.0, 0.0)
    return jnp.concatenate([one, two], axis=0).astype(BF16)


def edge_flags(starts):
    return none_in(starts, 0, 1), none_in(starts, -1, 1), none_in(starts, 0, 2)


def short_filter(rows, halo, taps, shift_ref, edges):
    tokens, width = rows.shape
    moved = jnp.dot(shift_ref[...], rows, preferred_element_type=F32)
    behind, further = moved[:tokens], moved[tokens:]
    edge = halo.astype(F32)
    far, near = edge[0:1, :], edge[1:2, :]
    row = lax.broadcasted_iota(jnp.int32, (SUB, width), 0)
    top = behind[:SUB] + jnp.where(row == 0, near * edges[0], 0.0)
    behind = jnp.concatenate([top, behind[SUB:]], axis=0)
    top = further[:SUB] + jnp.where(row == 0, far * edges[1], jnp.where(row == 1, near * edges[2], 0.0))
    further = jnp.concatenate([top, further[SUB:]], axis=0)
    return taps[0:1, :] * rows.astype(F32) + taps[1:2, :] * behind + taps[2:3, :] * further


def lane_tile(tile):
    return pl.ds(pl.multiple_of(tile * LANE, LANE), LANE)


def cmul(a_re, a_im, b_re, b_im):
    return a_re * b_re - a_im * b_im, a_re * b_im + a_im * b_re


def column_sums(parts):
    row = lax.broadcasted_iota(jnp.int32, (SUB, LANE), 0)
    low = row < 4
    level = []
    for b in range(4):
        keep = jnp.where(low, parts[b], parts[b + 4])
        move = jnp.where(low, parts[b + 4], parts[b])
        level.append(keep + pltpu.roll(move, 4, 0))
    for step in (2, 1):
        clear = (row & step) == 0
        level = [
            jnp.where(
                clear,
                level[b] + pltpu.roll(level[b], SUB - step, 0),
                level[b + step] + pltpu.roll(level[b + step], step, 0),
            )
            for b in range(step)
        ]
    return level[0]


def rows_of(ref, h, lanes):
    return ref[pl.ds(h * SUB, SUB), lanes]


def half_lanes(place_ref, mine, half, offset, size):
    core = place_ref[0] & 1
    core = core if mine else 1 - core
    return pl.ds(pl.multiple_of(core * half + offset, LANE), size)


def front_kernel(lengths_ref, place_ref, f0_ref, f2_ref, halo_ref, taps_ref, pole_ref,
                 z_ref, e_ref, end_ref, last_s, shift_s, z_s):
    tokens = z_ref.shape[0]
    width = f0_ref.shape[2]
    count = tokens // BLK
    modes = pole_ref.shape[0] // 2
    halves = modes // SUB
    origin = pl.program_id(0) * width
    wide = z_s.shape[0] * LANE
    starts = starts_of(lengths_ref, place_ref[0] * tokens)
    edges = edge_flags(starts)

    @pl.when(pl.program_id(0) == 0)
    def _():
        t = row_iota(tokens)
        last = jnp.full((tokens, LANE), -1, jnp.int32)
        for s in starts:
            last = jnp.maximum(last, jnp.where(s <= (t | (BLK - 1)), s, -1))
        last_s[...] = jnp.where(t >= last, 1.0, 0.0)
        shift_s[...] = shift_matrix(starts, tokens)

    @pl.loop(0, width // wide)
    def _(part):
        lanes = pl.ds(pl.multiple_of(part * wide, LANE), wide)
        conv0, conv2 = (
            short_filter(ref[0, :, lanes], halo_ref[r, :, lanes], taps_ref[r, :, lanes], shift_s, edges)
            for r, ref in ((0, f0_ref), (2, f2_ref))
        )
        z = (conv0 * conv2).astype(BF16)
        z_ref[:, pl.ds(pl.multiple_of(origin + part * wide, LANE), wide)] = z
        for i in range(wide // LANE):
            z_s[i] = z[:, i * LANE : (i + 1) * LANE].astype(F32) * last_s[...]
        for i in range(wide // LANE):
            z_i = z_s.at[i]
            from_lane = pl.ds(pl.multiple_of(part * wide + i * LANE, LANE), LANE)
            to_lane = pl.ds(pl.multiple_of(origin + part * wide + i * LANE, LANE), LANE)
            p_re = [rows_of(pole_ref, h, from_lane) for h in range(halves)]
            p_im = [rows_of(pole_ref, halves + h, from_lane) for h in range(halves)]
            pow_re, pow_im = list(p_re), list(p_im)
            e_re, e_im = [], []
            for b in range(count):
                now = z_i[pl.ds(b * BLK + BLK - 1, SUB, stride=0), :]
                prev = z_i[pl.ds(b * BLK + BLK - 2, SUB, stride=0), :]
                e_re.append([now + p_re[h] * prev for h in range(halves)])
                e_im.append([p_im[h] * prev for h in range(halves)])
            for k in range(2, BLK):
                for h in range(halves):
                    pow_re[h], pow_im[h] = cmul(pow_re[h], pow_im[h], p_re[h], p_im[h])
                for b in range(count):
                    now = z_i[pl.ds(b * BLK + BLK - 1 - k, SUB, stride=0), :]
                    for h in range(halves):
                        e_re[b][h] = e_re[b][h] + pow_re[h] * now
                        e_im[b][h] = e_im[b][h] + pow_im[h] * now
            for h in range(halves):
                rows, rows_im = pl.ds(h * SUB, SUB), pl.ds(modes + h * SUB, SUB)
                for b in range(count):
                    e_ref[b, rows, to_lane] = e_re[b][h]
                    e_ref[b, rows_im, to_lane] = e_im[b][h]
                gate = cmul(pow_re[h], pow_im[h], p_re[h], p_im[h])
                level = [(e_re[b][h], e_im[b][h]) for b in range(count)]
                span = BLK
                while len(level) > 1:
                    joined = []
                    for i in range(0, len(level), 2):
                        flag = none_in(starts, (i + 1) * span, (i + 2) * span)
                        joined.append(advance(gate, flag, level[i], level[i + 1]))
                    level = joined
                    gate = cmul(*gate, *gate)
                    span *= 2
                end_ref[rows, to_lane] = level[0][0].astype(BF16)
                end_ref[rows_im, to_lane] = level[0][1].astype(BF16)


def middle_kernel(lengths_ref, place_ref, features_ref, halo_ref, taps_ref, z_ref, skip_ref, pole_ref,
                  coef_ref, base_ref, gain_ref, first_s, part_s, z_s, filt_s, acc_s, shift_s, piece_s, *, mine):
    tokens, half = z_ref.shape
    count = tokens // BLK
    modes = pole_ref.shape[0] // 2
    halves = modes // SUB
    starts = starts_of(lengths_ref, place_ref[0] * tokens)
    edges = edge_flags(starts)
    t = row_iota(tokens)
    t0 = t & (-BLK)
    piece = jnp.zeros((tokens, LANE), jnp.int32)
    opened = jnp.zeros((tokens, LANE), jnp.bool_)
    for s in starts:
        piece = piece + jnp.where((s > t0) & (s <= t), 1, 0)
        opened = opened | ((s >= t0) & (s <= t))
    part_s[...] = piece.astype(F32)
    first_s[...] = jnp.where(opened, 0.0, 1.0)
    shift_s[...] = shift_matrix(starts, tokens)

    pieces = []
    for b in range(count):
        inside = jnp.int32(1)
        for s in starts:
            inside = inside + ((s > b * BLK) & (s < (b + 1) * BLK)).astype(jnp.int32)
        pieces.append(inside)
    wide = TILE

    @pl.loop(0, half // wide)
    def _(part):
        here = pl.ds(pl.multiple_of(part * wide, LANE), wide)
        lanes = half_lanes(place_ref, mine, half, part * wide, wide)
        conv1 = short_filter(features_ref[1, :, lanes], halo_ref[1, :, lanes], taps_ref[1, :, lanes], shift_s, edges)
        base_ref[:, here] = conv1
        for i in range(wide // LANE):
            inner = pl.ds(pl.multiple_of(part * wide + i * LANE, LANE), LANE)
            gain_ref[:, inner] = conv1[:, i * LANE : (i + 1) * LANE] * first_s[...]

    @pl.loop(0, half // LANE)
    def _(tile):
        here = lane_tile(tile)
        lanes = half_lanes(place_ref, mine, half, tile * LANE, LANE)
        p_re = [rows_of(pole_ref, h, lanes) for h in range(halves)]
        p_im = [rows_of(pole_ref, halves + h, lanes) for h in range(halves)]
        q_re = [rows_of(coef_ref, h, lanes) for h in range(halves)]
        q_im = [rows_of(coef_ref, halves + h, lanes) for h in range(halves)]
        filt_s[pl.ds(0, BLK), :] = jnp.zeros((BLK, LANE), F32)
        for group in range(BLK // SUB):
            parts = []
            for k in range(SUB):
                parts.append(sum(q_re[1:], q_re[0]))
                for h in range(halves):
                    q_re[h], q_im[h] = cmul(q_re[h], q_im[h], p_re[h], p_im[h])
            filt_s[pl.ds(BLK + group * SUB, SUB), :] = column_sums(parts).astype(BF16).astype(F32)
        z = z_ref[:, here].astype(F32)
        z_s[...] = z
        acc = skip_ref[:, lanes] * z
        sums = [[acc[b * BLK + r * SUB : b * BLK + (r + 1) * SUB] for r in range(BLK // SUB)] for b in range(count)]
        for s in range(BLK):
            firsts = range(s // SUB, BLK // SUB)
            columns = {r: filt_s[pl.ds(BLK - s + r * SUB, SUB), :] for r in firsts}
            for b in range(count):
                value = z_s[pl.ds(b * BLK + s, SUB, stride=0), :]
                for r in firsts:
                    sums[b][r] = sums[b][r] + columns[r] * value
        for b in range(count):
            for r in range(BLK // SUB):
                acc_s[pl.ds(b * BLK + r * SUB, SUB), :] = sums[b][r]

        for b in range(count):
            @pl.when(pieces[b] > 1)
            def _(b=b):
                rows = pl.ds(b * BLK, BLK)
                acc_s[rows, :] = skip_ref[:, lanes] * z_s[rows, :]

                def one_piece(q, carry):
                    member = part_s[rows, :] == q.astype(F32)
                    piece_s[...] = jnp.where(member, z_s[rows, :], 0.0)
                    total = jnp.zeros((BLK, LANE), F32)
                    for s in range(BLK):
                        total = total + filt_s[pl.ds(BLK - s, BLK), :] * piece_s[pl.ds(s, 1), :]
                    acc_s[rows, :] = acc_s[rows, :] + jnp.where(member, total, 0.0)
                    return carry

                lax.fori_loop(0, pieces[b], one_piece, 0)

        base_ref[:, here] = base_ref[:, here] * acc_s[...]


def prepare_kernel(lengths_ref, place_ref, e_ref, pole_ref, coef_ref, table_ref, local_ref, reach_ref, turn_s, *, mine):
    count, packed, half = e_ref.shape
    modes = packed // 2
    halves = modes // SUB
    starts = starts_of(lengths_ref, place_ref[0] * count * BLK)
    flags = block_flags(starts, count)
    pitch = turn_s.shape[0] // BLK

    @pl.loop(0, half // LANE)
    def _(tile):
        here = lane_tile(tile)
        lanes = half_lanes(place_ref, mine, half, tile * LANE, LANE)
        for h in range(halves):
            rows, rows_im = pl.ds(h * SUB, SUB), pl.ds(modes + h * SUB, SUB)
            p = pole_ref[rows, lanes], pole_ref[rows_im, lanes]
            q = coef_ref[rows, lanes], coef_ref[rows_im, lanes]
            for k in range(BLK):
                q = cmul(*q, *p)
                turn_s[pl.ds(k * pitch + h * SUB, SUB), :] = q[0]
                turn_s[pl.ds(k * pitch + modes + h * SUB, SUB), :] = -q[1]
            gate = p
            for _ in range(BLK.bit_length() - 1):
                gate = cmul(*gate, *gate)
            zero = jnp.zeros((SUB, LANE), F32)
            state, reach = (zero, zero), (zero + 1.0, zero)
            for b in range(count):
                local_ref[b, rows, here], local_ref[b, rows_im, here] = state
                reach_ref[b, rows, here], reach_ref[b, rows_im, here] = reach
                if b < count - 1:
                    state = advance(gate, flags[b], state, (e_ref[b, rows, here], e_ref[b, rows_im, here]))
                    reach = tuple(flags[b] * x for x in cmul(*gate, *reach))
        for m in range(packed):
            for r in range(BLK // SUB):
                table_ref[m, pl.ds(r * SUB, SUB), here] = turn_s[pl.ds(r * SUB * pitch + m, SUB, stride=pitch), :]


def split(ref, lanes, *lead):
    modes = ref.shape[-2] // 2
    packed = ref[(*lead, slice(None), lanes)].astype(F32)
    return packed[:modes], packed[modes:]


def store(ref, lanes, pair):
    modes = ref.shape[-2] // 2
    ref[0:modes, lanes] = pair[0].astype(ref.dtype)
    ref[modes : 2 * modes, lanes] = pair[1].astype(ref.dtype)


def advance(gate, flag, state, addend):
    re, im = cmul(*gate, *state)
    return addend[0] + flag * re, addend[1] + flag * im


def choose(flag, a, b):
    return tuple(jnp.where(flag, x, y) for x, y in zip(a, b))


def first_kernel(lengths_ref, place_ref, kept_ref, came_ref, pole_ref, total_ref, send_ref, gate_ref, *, tokens):
    starts = starts_of(lengths_ref, 0)
    place = place_ref[0]
    odd = (place & 1) == 1
    second = place | 1
    flag = none_in(starts, second * tokens, (second + 1) * tokens)
    half = kept_ref.shape[1]

    @pl.loop(0, half // LANE)
    def _(tile):
        lanes = lane_tile(tile)
        kept, came = split(kept_ref, lanes), split(came_ref, lanes)
        gate = split(pole_ref, half_lanes(place_ref, True, half, tile * LANE, LANE))
        reach = 1
        while reach < tokens:
            gate = cmul(*gate, *gate)
            reach *= 2
        total = advance(gate, flag, choose(odd, came, kept), choose(odd, kept, came))
        store(total_ref, lanes, total)
        store(send_ref, lanes, total)
        store(gate_ref, lanes, gate)


def round_kernel(lengths_ref, place_ref, total_ref, met_ref, *refs, tokens, k, last):
    starts = starts_of(lengths_ref, 0)
    place = place_ref[0]
    distance = 1 << k
    upper = (place & distance) != 0
    group = (place >> k) << k
    even = (place >> 1) << 1
    later = group | distance
    enter = none_in(starts, group * tokens, even * tokens)
    enter = jnp.where(upper, enter, 0.0)
    whole = none_in(starts, later * tokens, (later + distance) * tokens)
    flag = none_in(starts, even * tokens, (even + 1) * tokens)

    @pl.loop(0, met_ref.shape[1] // LANE)
    def _(tile):
        lanes = lane_tile(tile)
        rest = list(refs)
        met, total = split(met_ref, lanes), split(total_ref, lanes)
        power = split(rest.pop(0), lanes)
        if k == 1:
            prefix = tuple(enter * x for x in met)
        else:
            before, prefix = split(rest.pop(0), lanes), split(rest.pop(0), lanes)
            prefix = advance(before, enter, met, prefix)
        if not last:
            total_out, send_ref, power_out, before_out, prefix_out = rest
            power = cmul(*power, *power)
            total = advance(power, whole, choose(upper, met, total), choose(upper, total, met))
            store(total_out, lanes, total)
            store(send_ref, lanes, total)
            store(prefix_out, lanes, prefix)
            store(power_out, lanes, power)
            if k == 1:
                before = choose(upper, power, (jnp.ones_like(met[0]), jnp.zeros_like(met[0])))
            else:
                before = choose(upper, cmul(*before, *power), before)
            store(before_out, lanes, before)
        else:
            gate_ref, kept_ref, came_ref, own_ref, send_ref = rest
            odd = (place & 1) == 1
            kept, came = split(kept_ref, lanes), split(came_ref, lanes)
            beyond = advance(split(gate_ref, lanes), flag, prefix, choose(odd, came, kept))
            store(own_ref, lanes, choose(odd, beyond, prefix))
            store(send_ref, lanes, choose(odd, prefix, beyond))


def back_kernel(place_ref, entry_ref, table_ref, local_ref, reach_ref, base_ref, gain_ref, *refs):
    out_ref, state_s = refs[-2:]
    tokens, width = out_ref.shape
    count, packed, _ = local_ref.shape
    modes = packed // 2
    halves = modes // SUB
    origin = pl.program_id(0) * width

    @pl.loop(0, width // LANE)
    def _(tile):
        lanes = lane_tile(tile)
        here = pl.ds(pl.multiple_of(origin + tile * LANE, LANE), LANE)
        entry = entry_ref[:, here].astype(F32)
        for h in range(halves):
            rows, rows_im = pl.ds(h * SUB, SUB), pl.ds(modes + h * SUB, SUB)
            first = entry[h * SUB : (h + 1) * SUB], entry[modes + h * SUB : modes + (h + 1) * SUB]
            for b in range(count):
                state = first
                if b:
                    state = cmul(reach_ref[b, rows, here], reach_ref[b, rows_im, here], *first)
                    state = state[0] + local_ref[b, rows, here], state[1] + local_ref[b, rows_im, here]
                state_s[pl.ds(b * packed + h * SUB, SUB), :] = state[0]
                state_s[pl.ds(b * packed + modes + h * SUB, SUB), :] = state[1]
        sums = [[None] * (BLK // SUB) for _ in range(count)]
        for m in range(packed):
            turn = [table_ref[m, pl.ds(r * SUB, SUB), here] for r in range(BLK // SUB)]
            for b in range(count):
                state = state_s[pl.ds(b * packed + m, SUB, stride=0), :]
                for r in range(BLK // SUB):
                    term = turn[r] * state
                    sums[b][r] = term if m == 0 else sums[b][r] + term
        for b in range(count):
            rows = pl.ds(b * BLK, BLK)
            carried = jnp.concatenate(sums[b], axis=0)
            out_ref[rows, lanes] = (base_ref[rows, here] + gain_ref[rows, here] * carried).astype(BF16)


def per_device(features, kernel, skip, residues, decay, freq, lengths):
    tokens = features.shape[1]
    modes, width = decay.shape
    half = width // 2
    count = tokens // BLK
    n = lax.axis_size("seq")
    place = lax.axis_index("seq")
    core = place % 2
    rounds = n.bit_length() - 1
    where = place.astype(jnp.int32)[None]

    rim = features[:, tokens - 2 :, :]
    inner = exchange(rim, 1)
    link = [(i, i + 1) for i in range(1, n - 1, 2)]
    outer = lax.ppermute(rim, "seq", link + [(b, a) for a, b in link])
    halo = jnp.where(core == 1, inner, outer)

    fade = jnp.exp(-decay)
    q = freq * freq
    sine = freq * (1 + q * (-1 / 6 + q * (1 / 120 + q * (-1 / 5040 + q * (1 / 362880)))))
    cosine = 1 + q * (-1 / 2 + q * (1 / 24 + q * (-1 / 720 + q * (1 / 40320 - q * (1 / 3628800)))))
    d = 2 * decay
    scale = jnp.sqrt(d * (1 - d * (1 / 2 - d * (1 / 6 - d * (1 / 24 - d * (1 / 120 - d * (1 / 720)))))))
    pole = jnp.stack([fade * cosine, fade * sine]).reshape(2 * modes, width)
    coef = (residues * scale[None]).reshape(2 * modes, width)

    params = pltpu.CompilerParams(vmem_limit_bytes=16 * 1024 * 1024)
    roomy = pltpu.CompilerParams(vmem_limit_bytes=ROOM * 1024 * 1024)
    plane = pltpu.VMEM((tokens, LANE), F32)
    shifts = pltpu.VMEM((2 * tokens, tokens), BF16)
    whole = pl.BlockSpec(memory_space=pltpu.VMEM)

    def call(body, args, outs, name, scratch=(), cost=0.8e9):
        return pl.pallas_call(
            body,
            grid_spec=pltpu.PrefetchScalarGridSpec(
                num_scalar_prefetch=2, grid=(), in_specs=[whole] * len(args), out_specs=[whole] * len(outs),
                scratch_shapes=scratch,
            ),
            out_shape=[jax.ShapeDtypeStruct(*o) for o in outs],
            compiler_params=params, name=name,
            cost_estimate=pl.CostEstimate(flops=int(cost), bytes_accessed=1 << 20, transcendentals=0),
        )(lengths, where, *args)

    packed = 2 * modes
    tiles = half // TILE
    state, sent = ((packed, half), F32), ((packed, half), BF16)
    blocks, plain = ((count, packed, half), F32), ((tokens, half), F32)

    def tile_of(mine, i, w_ref):
        core = w_ref[0] & 1
        return (core if mine else 1 - core) * tiles + i

    def front(mine):
        def columns(*lead):
            return pl.BlockSpec((*lead, TILE), lambda i, n_ref, w_ref: (*(0,) * len(lead), tile_of(mine, i, w_ref)))

        def stream(r):
            return pl.BlockSpec((1, tokens, TILE), lambda i, n_ref, w_ref: (r, 0, tile_of(mine, i, w_ref)))

        return pl.pallas_call(
            front_kernel,
            grid_spec=pltpu.PrefetchScalarGridSpec(
                num_scalar_prefetch=2, grid=(tiles,),
                in_specs=[stream(0), stream(2), columns(3, 2), columns(3, 3), columns(packed)],
                out_specs=[whole] * 3,
                scratch_shapes=[plane, shifts, pltpu.VMEM((TILE // LANE, tokens, LANE), F32)],
            ),
            out_shape=[jax.ShapeDtypeStruct((tokens, half), BF16), jax.ShapeDtypeStruct(*blocks),
                       jax.ShapeDtypeStruct(*sent)],
            compiler_params=roomy, name="front",
            cost_estimate=pl.CostEstimate(flops=5_000_000_000, bytes_accessed=4 << 20, transcendentals=0),
        )(lengths, where, features, features, halo, kernel, pole)

    def middle(mine, z):
        return call(
            functools.partial(middle_kernel, mine=mine), (features, halo, kernel, z, skip[None], pole, coef),
            (plain, plain), "middle", [plane, plane, plane, pltpu.VMEM((2 * BLK, LANE), F32), plane, shifts, pltpu.VMEM((BLK, LANE), F32)], cost=5e9,
        )

    def prepare(mine, e):
        return call(
            functools.partial(prepare_kernel, mine=mine), (e, pole, coef),
            (((packed, BLK, half), F32), blocks, blocks), "prepare", [pltpu.VMEM((BLK * PITCH, LANE), F32)], cost=4e9,
        )

    def back(mine, args, out):
        specs = [whole] * len(args)
        if out is not None:
            args, specs = args + (out,), specs + [pl.BlockSpec(memory_space=pl.ANY)]

        return pl.pallas_call(
            back_kernel,
            grid_spec=pltpu.PrefetchScalarGridSpec(
                num_scalar_prefetch=1, grid=(tiles,), in_specs=specs,
                out_specs=pl.BlockSpec((tokens, TILE), lambda i, w_ref: (0, tile_of(mine, i, w_ref))),
                scratch_shapes=[pltpu.VMEM((count * packed, LANE), F32)],
            ),
            out_shape=jax.ShapeDtypeStruct((tokens, width), BF16),
            input_output_aliases={} if out is None else {len(args): 0},
            compiler_params=params, name="back",
            cost_estimate=pl.CostEstimate(flops=3_500_000_000, bytes_accessed=1 << 20, transcendentals=0),
        )(where, *args)

    z_other, e_other, end_other = front(False)
    came = exchange(end_other, 1)
    z_own, e_own, end_own = front(True)
    total, send, gate = call(
        functools.partial(first_kernel, tokens=tokens), (end_own, came, pole), (state, sent, state), "first"
    )
    power, carry = gate, ()
    jobs = [lambda z: middle(True, z), lambda z: middle(False, z), lambda es: (*prepare(True, es[0]), *prepare(False, es[1]))]
    inputs = [z_own, z_other, (e_own, e_other)]
    ready = []
    for k in range(1, rounds):
        last = k == rounds - 1
        met = exchange(send, 1 << k)
        for job, operand in [(jobs.pop(0), inputs.pop(0)) for _ in range(len(jobs) if last else min(1, len(jobs)))]:
            operand, send = lax.optimization_barrier((operand, send))
            met, done = lax.optimization_barrier((met, job(operand)))
            ready.append(done)
        body = functools.partial(round_kernel, tokens=tokens, k=k, last=last)
        args = (total, met, power, *carry)
        if last:
            own, send = call(body, args + (gate, end_own, came), (state, sent), "round")
        else:
            total, send, power, *carry = call(body, args, (state, sent, state, state, state), "round")
    other = exchange(send, 1)
    out = back(True, (own, *ready[2][:3], *ready[0]), None)
    return back(False, (other, *ready[2][3:], *ready[1]), out)


def solution(mesh):
    return jax.shard_map(
        per_device,
        mesh=mesh,
        in_specs=(P(None, ("groups", "seq"), None), P(), P(), P(), P(), P(), P("groups")),
        out_specs=P(("groups", "seq"), None),
        check_vma=False,
    )
```

time: 63.4 us -> 54.6 us (0.86)
  waiting for transfers between devices: 8.52 us -> 1.98 us
  local copies, waits for them, and re-layouts: 7.39 us -> 1.04 us
  starting transfers between devices: 7.68 us -> 11.4 us
  Pallas kernels: 39.8 us -> 37.2 us
  other arithmetic: 0.06 us -> 2.59 us
    pallas_call x6 -> x8, Pallas kernels: 35.2 us -> 17.1 us  [call(): pl.pallas_call(body, grid_spec=pltpu.PrefetchScalarGridSpec(num_scalar_pr...]
    pallas_call x5 -> x4, Pallas kernels: 4.59 us -> 20.1 us  [the longest x2 12.8 us: front(): pl.pallas_call(front_kernel, grid_spec=pltpu.PrefetchScalarGridSpec(num_s...]
    ppermute x6, waiting for transfers between devices: 8.52 us -> 1.98 us  [exchange(): return lax.ppermute(block, 'seq', [(i, i ^ distance) for i in devices])]
    unnamed x18 -> x8, local copies, waits for them, and re-layouts: 6.42 us -> 0.02 us
    ppermute x6, starting transfers between devices: 3.14 us -> 6.88 us  [exchange(): return lax.ppermute(block, 'seq', [(i, i ^ distance) for i in devices])]
    another operation x0 -> x2, other arithmetic: none -> 2.53 us  [per_device(): pole = jnp.stack([fade * cosine, fade * sine]).reshape(2 * modes, width)]
  transfers between devices with their start and end apart: 7 -> 7, of which waited for: 1 -> 1; matrix products, arithmetic and copies ran while one was open for 0% -> 5% of each run, Pallas kernels for 39% -> 44%
where the time goes in v3:
time: 54.6 us; the launch traced here: 54.4 us
  Pallas kernels  37.2 us (68%)
  starting transfers between devices  11.4 us (21%)
  other arithmetic  2.59 us (5%)
  waiting for transfers between devices  1.98 us (4%)
  local copies, waits for them, and re-layouts  1.04 us (2%)
    pallas_call x8, Pallas kernels, call(): pl.pallas_call(body, grid_spec=pltpu.PrefetchScalarGridSpec(num_scalar_pr...  17.1 us
    pallas_call x2, Pallas kernels, front(): pl.pallas_call(front_kernel, grid_spec=pltpu.PrefetchScalarGridSpec(num_s...  12.8 us
    pallas_call x2, Pallas kernels, back(): pl.pallas_call(back_kernel, grid_spec=pltpu.PrefetchScalarGridSpec(num_sc...  7.28 us
    ppermute x6, starting transfers between devices, exchange(): return lax.ppermute(block, 'seq', [(i, i ^ distance) for i in devices])  6.88 us
    ppermute x1, starting transfers between devices, per_device(): outer = lax.ppermute(rim, 'seq', link + [(b, a) for a, b in link])  4.54 us
    another operation x2, other arithmetic, per_device(): pole = jnp.stack([fade * cosine, fade * sine]).reshape(2 * modes, width)  2.53 us
    ppermute x6, waiting for transfers between devices, exchange(): return lax.ppermute(block, 'seq', [(i, i ^ distance) for i in devices])  1.98 us
  transfers between devices with their start and end apart: 7, of which 1 were waited for; matrix products, arithmetic and copies ran while one was open for 5% of the time, Pallas kernels for 44%

profile of v3, /device:TPU:1, one launch (start us, length us, event | category | flops | bytes accessed | tf_op | source)
XLA Modules:
  0.0 54.4 jit_solution(17389944408687904962)
XLA Ops:
  0.0 1.0 %slice.3 = bf16[3,2,4096]{2,1,0:T(2,128)(2,1)S(1)} slice(bf16[3,128,4096]{2,1,0:T(8,128)(2,1)} %features_ref.3), slice={[0:3], [126:128], [0:4096]} | slice | bytes 98304 | tf_op jit(solution)/shard_map/slice | solution.py:453
  1.0 4.5 %collective-permute-start.1 = (bf16[3,2,4096]{2,1,0:T(2,128)(2,1)S(1)}, bf16[3,2,4096]{2,1,0:T(2,128)(2,1)S(1)}, u32[]{:S(2)}, u32[]{:S(2)}) collective-permute-start(bf16[3,2,4096]{2,1,0:T(2,128)(2,1)S(1)} %slice.3), channel_id=1, source_target_pairs={{1,2},{3,4},{5,6},{7,8},{9,10},{11,12},{13,14},{2,1},{4,3},{6,5},{... | collective-permute-start | bytes 147464 | tf_op jit(solution)/shard_map/ppermute | solution.py:456
  5.6 0.1 collective-permute-start
  5.7 1.4 %fusion.6 = (f32[1,16,4096]{2,1,0:T(8,128)S(1)}, f32[1,16,4096]{2,1,0:T(8,128)S(1)}, f32[16,4096]{1,0:T(8,128)S(1)}) fusion(f32[16,4096]{1,0:T(8,128)} %param.12, f32[16,4096]{1,0:T(8,128)} %param.11), kind=kLoop, calls=%fused_computation.17 | loop fusion | flops 2293760 | bytes 1310720 | tf_op jit(solution)/shard_map/stack | solution.py:465
  7.1 1.1 %pad_maximum_fusion = (f32[2,16,4096]{2,1,0:T(8,128)S(1)}, f32[2,16,4096]{2,1,0:T(8,128)S(1)}) fusion(f32[1,16,4096]{2,1,0:T(8,128)S(1)} %get-tuple-element.102, f32[1,16,4096]{2,1,0:T(8,128)S(1)} %get-tuple-element.101, f32[2,16,4096]{2,1,0:T(8,128)} %param.10, f32[16,4096]{1,0:T(8,128)S(1)} %get-tuple-element.103), kind=kLoop, calls=%fused_computation | loop fusion | flops 262144 | bytes 2359296 | tf_op jit(solution)/shard_map/stack | solution.py:465
  8.2 0.1 broadcast_select_fusion.halo_ref
  8.3 6.3 %front.3 = (bf16[128,2048]{1,0:T(8,128)(2,1)S(1)}, f32[8,32,2048]{2,1,0:T(8,128)S(1)}, bf16[32,2048]{1,0:T(8,128)(2,1)S(1)}) custom-call(s32[6]{0:T(128)S(1)} %copy-done.3, s32[1]{0:T(128)} %bitcast.place_ref, bf16[3,128,4096]{2,1,0:T(8,128)(2,1)} %features_ref.3, bf16[3,128,4096]{2,1,0:T(8,128)(2,1)} %features_ref.3, ...), custom_call_target="tpu_custom_call" | custom-call | flops 5000000000 | bytes 4194304 | tf_op jit(solution)/shard_map/front/pallas_call | solution.py:502
  14.6 0.6 %collective-permute-start.2 = (bf16[32,2048]{1,0:T(8,128)(2,1)S(1)}, bf16[32,2048]{1,0:T(8,128)(2,1)S(1)}, u32[]{:S(2)}, u32[]{:S(2)}) collective-permute-start(bf16[32,2048]{1,0:T(8,128)(2,1)S(1)} %get-tuple-element.54), channel_id=1, source_target_pairs={{0,1},{1,0},{2,3},{3,2},{4,5},{5,4},{6,7},{7,6},{8,9},{9,8},{10,11... | collective-permute-start | bytes 393224 | tf_op jit(solution)/shard_map/ppermute | solution.py:22
  15.1 6.5 %front.2 = (bf16[128,2048]{1,0:T(8,128)(2,1)S(1)}, f32[8,32,2048]{2,1,0:T(8,128)S(1)}, bf16[32,2048]{1,0:T(8,128)(2,1)S(1)}) custom-call(s32[6]{0:T(128)S(1)} %copy-done.3, s32[1]{0:T(128)} %bitcast.place_ref, bf16[3,128,4096]{2,1,0:T(8,128)(2,1)} %features_ref.3, bf16[3,128,4096]{2,1,0:T(8,128)(2,1)} %features_ref.3, ...), custom_call_target="tpu_custom_call" | custom-call | flops 5000000000 | bytes 4194304 | tf_op jit(solution)/shard_map/front/pallas_call | solution.py:502
  21.7 1.0 %first.1 = (f32[32,2048]{1,0:T(8,128)S(1)}, bf16[32,2048]{1,0:T(8,128)(2,1)S(1)}, f32[32,2048]{1,0:T(8,128)S(1)}) custom-call(s32[6]{0:T(128)S(1)} %copy-done.3, s32[1]{0:T(128)} %bitcast.place_ref, bf16[32,2048]{1,0:T(8,128)(2,1)S(1)} %get-tuple-element.53.kept_ref.refs_4_, bf16[32,2048]{1,0:T(8,128)(2,1)S(1)} %collective-permute-done.2.came_ref.refs_5_, ...), custom_call_target="tpu_custom_call" | custom-call | flops 800000000 | bytes 1048576 | tf_op jit(solution)/shard_map/first/pallas_call | solution.py:475
  22.7 1.3 %collective-permute-start.3 = (bf16[32,2048]{1,0:T(8,128)(2,1)S(1)}, bf16[32,2048]{1,0:T(8,128)(2,1)S(1)}, u32[]{:S(2)}, u32[]{:S(2)}) collective-permute-start(bf16[32,2048]{1,0:T(8,128)(2,1)S(1)} %get-tuple-element.56), channel_id=1, source_target_pairs={{0,2},{1,3},{2,0},{3,1},{4,6},{5,7},{6,4},{7,5},{8,10},{9,11},{10,... | collective-permute-start | bytes 393224 | tf_op jit(solution)/shard_map/ppermute | solution.py:22
  24.0 4.3 %middle.2 = (f32[128,2048]{1,0:T(8,128)S(1)}, f32[128,2048]{1,0:T(8,128)S(1)}) custom-call(s32[6]{0:T(128)S(1)} %copy-done.3, s32[1]{0:T(128)} %bitcast.place_ref, bf16[3,128,4096]{2,1,0:T(8,128)(2,1)S(1)} %copy-done, bf16[3,2,4096]{2,1,0:T(2,128)(2,1)S(1)} %broadcast_select_fusion.halo_ref, f32[3,3,4096]{2,1,0:T(4,128)S(1)} %copy-done.1, ...), custom_call_target="tpu_custom_call" | custom-call | flops 5000000000 | bytes 1048576 | tf_op jit(solution)/shard_map/middle/pallas_call | solution.py:475
  28.4 0.8 %round.3 = (f32[32,2048]{1,0:T(8,128)S(1)}, bf16[32,2048]{1,0:T(8,128)(2,1)S(1)}, f32[32,2048]{1,0:T(8,128)S(1)}, f32[32,2048]{1,0:T(8,128)S(1)}, f32[32,2048]{1,0:T(8,128)S(1)}) custom-call(s32[6]{0:T(128)S(1)} %copy-done.3, s32[1]{0:T(128)} %bitcast.place_ref, f32[32,2048]{1,0:T(8,128)S(1)} %get-tuple-element.55.total_ref, ...), custom_call_target="tpu_custom_call" | custom-call | flops 800000000 | bytes 1048576 | tf_op jit(solution)/shard_map/round/pallas_call | solution.py:475
  29.2 2.1 %collective-permute-start.4 = (bf16[32,2048]{1,0:T(8,128)(2,1)S(1)}, bf16[32,2048]{1,0:T(8,128)(2,1)S(1)}, u32[]{:S(2)}, u32[]{:S(2)}) collective-permute-start(bf16[32,2048]{1,0:T(8,128)(2,1)S(1)} %get-tuple-element.64), channel_id=1, source_target_pairs={{0,4},{1,5},{2,6},{3,7},{4,0},{5,1},{6,2},{7,3},{8,12},{9,13},{10,... | collective-permute-start | bytes 393224 | tf_op jit(solution)/shard_map/ppermute | solution.py:22
  31.3 4.3 %middle.3 = (f32[128,2048]{1,0:T(8,128)S(1)}, f32[128,2048]{1,0:T(8,128)S(1)}) custom-call(s32[6]{0:T(128)S(1)} %copy-done.3, s32[1]{0:T(128)} %bitcast.place_ref, bf16[3,128,4096]{2,1,0:T(8,128)(2,1)S(1)} %copy-done, bf16[3,2,4096]{2,1,0:T(2,128)(2,1)S(1)} %broadcast_select_fusion.halo_ref, f32[3,3,4096]{2,1,0:T(4,128)S(1)} %copy-done.1, ...), custom_call_target="tpu_custom_call" | custom-call | flops 5000000000 | bytes 1048576 | tf_op jit(solution)/shard_map/middle/pallas_call | solution.py:475
  35.6 0.9 %round.4 = (f32[32,2048]{1,0:T(8,128)S(1)}, bf16[32,2048]{1,0:T(8,128)(2,1)S(1)}, f32[32,2048]{1,0:T(8,128)S(1)}, f32[32,2048]{1,0:T(8,128)S(1)}, f32[32,2048]{1,0:T(8,128)S(1)}) custom-call(s32[6]{0:T(128)S(1)} %copy-done.3, s32[1]{0:T(128)} %bitcast.place_ref, f32[32,2048]{1,0:T(8,128)S(1)} %get-tuple-element.63.total_ref, ...), custom_call_target="tpu_custom_call" | custom-call | flops 800000000 | bytes 1048576 | tf_op jit(solution)/shard_map/round/pallas_call | solution.py:475
  36.5 1.6 %collective-permute-start.5 = (bf16[32,2048]{1,0:T(8,128)(2,1)S(1)}, bf16[32,2048]{1,0:T(8,128)(2,1)S(1)}, u32[]{:S(2)}, u32[]{:S(2)}) collective-permute-start(bf16[32,2048]{1,0:T(8,128)(2,1)S(1)} %get-tuple-element.74), channel_id=1, source_target_pairs={{0,8},{1,9},{2,10},{3,11},{4,12},{5,13},{6,14},{7,15},{8,0},{9,1},... | collective-permute-start | bytes 393224 | tf_op jit(solution)/shard_map/ppermute | solution.py:22
  38.1 2.4 %prepare.2 = (f32[32,16,2048]{2,1,0:T(8,128)S(1)}, f32[8,32,2048]{2,1,0:T(8,128)S(1)}, f32[8,32,2048]{2,1,0:T(8,128)S(1)}) custom-call(s32[6]{0:T(128)S(1)} %copy-done.3, s32[1]{0:T(128)} %bitcast.place_ref, f32[8,32,2048]{2,1,0:T(8,128)S(1)} %get-tuple-element.77.e_ref, f32[32,4096]{1,0:T(8,128)S(1)} %bitcast.13, f32[32,4096]{1,0:T(8,128)S(1)} %bitcast.17), custom_call_target="tpu_custom_call" | custom-call | flops 4000000000 | bytes 1048576 | tf_op jit(solution)/shard_map/prepare/pallas_call | solution.py:475
  40.6 2.5 %prepare.3 = (f32[32,16,2048]{2,1,0:T(8,128)S(1)}, f32[8,32,2048]{2,1,0:T(8,128)S(1)}, f32[8,32,2048]{2,1,0:T(8,128)S(1)}) custom-call(s32[6]{0:T(128)S(1)} %copy-done.3, s32[1]{0:T(128)} %bitcast.place_ref, f32[8,32,2048]{2,1,0:T(8,128)S(1)} %get-tuple-element.81.e_ref, f32[32,4096]{1,0:T(8,128)S(1)} %bitcast.14, f32[32,4096]{1,0:T(8,128)S(1)} %bitcast.18), custom_call_target="tpu_custom_call" | custom-call | flops 4000000000 | bytes 1048576 | tf_op jit(solution)/shard_map/prepare/pallas_call | solution.py:475
  43.0 2.0 %collective-permute-done.5.met_ref = bf16[32,2048]{1,0:T(8,128)(2,1)S(1)} collective-permute-done((bf16[32,2048]{1,0:T(8,128)(2,1)S(1)}, bf16[32,2048]{1,0:T(8,128)(2,1)S(1)}, u32[]{:S(2)}, u32[]{:S(2)}) %collective-permute-start.5) | collective-permute-done | bytes 131104 | tf_op jit(solution)/shard_map/ppermute | solution.py:22
  45.0 0.9 %round.5 = (f32[32,2048]{1,0:T(8,128)S(1)}, bf16[32,2048]{1,0:T(8,128)(2,1)S(1)}) custom-call(s32[6]{0:T(128)S(1)} %copy-done.3, s32[1]{0:T(128)} %bitcast.place_ref, f32[32,2048]{1,0:T(8,128)S(1)} %get-tuple-element.73.total_ref, bf16[32,2048]{1,0:T(8,128)(2,1)S(1)} %collective-permute-done.5.met_ref, f32[32,2048]{1,0:T(8,128)S(1)} %get-tuple-element.86.refs_0_, ...), custom_call_target="tpu_custom_call" | custom-call | flops 800000000 | bytes 1048576 | tf_op jit(solution)/shard_map/round/pallas_call | solution.py:475
  45.9 1.3 %collective-permute-start.6 = (bf16[32,2048]{1,0:T(8,128)(2,1)S(1)}, bf16[32,2048]{1,0:T(8,128)(2,1)S(1)}, u32[]{:S(2)}, u32[]{:S(2)}) collective-permute-start(bf16[32,2048]{1,0:T(8,128)(2,1)S(1)} %get-tuple-element.89), channel_id=1, source_target_pairs={{0,1},{1,0},{2,3},{3,2},{4,5},{5,4},{6,7},{7,6},{8,9},{9,8},{10,11... | collective-permute-start | bytes 393224 | tf_op jit(solution)/shard_map/ppermute | solution.py:22
  47.2 3.6 %back.2.refs_0_ = bf16[128,4096]{1,0:T(8,128)(2,1)} custom-call(s32[1]{0:T(128)} %bitcast.place_ref, f32[32,2048]{1,0:T(8,128)S(1)} %get-tuple-element.95.entry_ref, f32[32,16,2048]{2,1,0:T(8,128)S(1)} %get-tuple-element.96.table_ref, f32[8,32,2048]{2,1,0:T(8,128)S(1)} %get-tuple-element.97.local_ref, f32[8,32,2048]{2,1,0:T(8,128)S(1)} %get-tuple-element.98.reach_ref, ...), custom_call_target="tpu_custom_call" | custom-call | flops 3500000000 | bytes 1048576 | tf_op jit(solution)/shard_map/back/pallas_call | solution.py:533
  50.8 3.6 %back.3 = bf16[128,4096]{1,0:T(8,128)(2,1)} custom-call(s32[1]{0:T(128)} %bitcast.place_ref, bf16[32,2048]{1,0:T(8,128)(2,1)S(1)} %collective-permute-done.6.entry_ref, f32[32,16,2048]{2,1,0:T(8,128)S(1)} %get-tuple-element.90.table_ref, f32[8,32,2048]{2,1,0:T(8,128)S(1)} %get-tuple-element.91.local_ref, ...), custom_call_target="tpu_custom_call", output_to_operand_aliasing={{}: (7, {})} | custom-call | flops 3500000000 | bytes 1048576 | tf_op jit(solution)/shard_map/back/pallas_call | solution.py:533
  (14 shorter events, 0.0 us)
Async XLA Ops:
  0.0 8.3 %copy-start.3 = (s32[6]{0:T(128)S(1)}, s32[6]{0:T(128)}, u32[]{:S(2)}) copy-start(s32[6]{0:T(128)} %lengths_ref.19) | copy-start | bytes 76
  0.0 8.3 %copy-start.1 = (f32[3,3,4096]{2,1,0:T(4,128)S(1)}, f32[3,3,4096]{2,1,0:T(4,128)}, u32[]{:S(2)}) copy-start(f32[3,3,4096]{2,1,0:T(4,128)} %taps_ref.7) | copy-start | bytes 442372
  1.0 7.2 %collective-permute-start.1 = (bf16[3,2,4096]{2,1,0:T(2,128)(2,1)S(1)}, bf16[3,2,4096]{2,1,0:T(2,128)(2,1)S(1)}, u32[]{:S(2)}, u32[]{:S(2)}) collective-permute-start(bf16[3,2,4096]{2,1,0:T(2,128)(2,1)S(1)} %slice.3), channel_id=1, source_target_pairs={{1,2},{3,4},{5,6},{7,8},{9,10},{11,12},{13,14},{2,1},{4,3},{6,5},{... | collective-permute-start | bytes 147464 | tf_op jit(solution)/shard_map/ppermute | solution.py:456
  5.6 2.6 %collective-permute-start = (bf16[3,2,4096]{2,1,0:T(2,128)(2,1)S(1)}, bf16[3,2,4096]{2,1,0:T(2,128)(2,1)S(1)}, u32[]{:S(2)}, u32[]{:S(2)}) collective-permute-start(bf16[3,2,4096]{2,1,0:T(2,128)(2,1)S(1)} %slice.3), channel_id=1, source_target_pairs={{0,1},{1,0},{2,3},{3,2},{4,5},{5,4},{6,7},{7,6},{8,9},{9,8},{10,11... | collective-permute-start | bytes 147464 | tf_op jit(solution)/shard_map/ppermute | solution.py:22
  14.6 7.1 %collective-permute-start.2 = (bf16[32,2048]{1,0:T(8,128)(2,1)S(1)}, bf16[32,2048]{1,0:T(8,128)(2,1)S(1)}, u32[]{:S(2)}, u32[]{:S(2)}) collective-permute-start(bf16[32,2048]{1,0:T(8,128)(2,1)S(1)} %get-tuple-element.54), channel_id=1, source_target_pairs={{0,1},{1,0},{2,3},{3,2},{4,5},{5,4},{6,7},{7,6},{8,9},{9,8},{10,11... | collective-permute-start | bytes 393224 | tf_op jit(solution)/shard_map/ppermute | solution.py:22
  15.1 8.9 %copy-start = (bf16[3,128,4096]{2,1,0:T(8,128)(2,1)S(1)}, bf16[3,128,4096]{2,1,0:T(8,128)(2,1)}, u32[]{:S(2)}) copy-start(bf16[3,128,4096]{2,1,0:T(8,128)(2,1)} %features_ref.3) | copy-start | bytes 9437188
  21.7 2.4 %copy-start.2 = (f32[4096]{0:T(1024)S(1)}, f32[4096]{0:T(1024)}, u32[]{:S(2)}) copy-start(f32[4096]{0:T(1024)} %param.9) | copy-start | bytes 49156
  22.7 5.6 %collective-permute-start.3 = (bf16[32,2048]{1,0:T(8,128)(2,1)S(1)}, bf16[32,2048]{1,0:T(8,128)(2,1)S(1)}, u32[]{:S(2)}, u32[]{:S(2)}) collective-permute-start(bf16[32,2048]{1,0:T(8,128)(2,1)S(1)} %get-tuple-element.56), channel_id=1, source_target_pairs={{0,2},{1,3},{2,0},{3,1},{4,6},{5,7},{6,4},{7,5},{8,10},{9,11},{10,... | collective-permute-start | bytes 393224 | tf_op jit(solution)/shard_map/ppermute | solution.py:22
  29.2 6.4 %collective-permute-start.4 = (bf16[32,2048]{1,0:T(8,128)(2,1)S(1)}, bf16[32,2048]{1,0:T(8,128)(2,1)S(1)}, u32[]{:S(2)}, u32[]{:S(2)}) collective-permute-start(bf16[32,2048]{1,0:T(8,128)(2,1)S(1)} %get-tuple-element.64), channel_id=1, source_target_pairs={{0,4},{1,5},{2,6},{3,7},{4,0},{5,1},{6,2},{7,3},{8,12},{9,13},{10,... | collective-permute-start | bytes 393224 | tf_op jit(solution)/shard_map/ppermute | solution.py:22
  36.5 8.5 %collective-permute-start.5 = (bf16[32,2048]{1,0:T(8,128)(2,1)S(1)}, bf16[32,2048]{1,0:T(8,128)(2,1)S(1)}, u32[]{:S(2)}, u32[]{:S(2)}) collective-permute-start(bf16[32,2048]{1,0:T(8,128)(2,1)S(1)} %get-tuple-element.74), channel_id=1, source_target_pairs={{0,8},{1,9},{2,10},{3,11},{4,12},{5,13},{6,14},{7,15},{8,0},{9,1},... | collective-permute-start | bytes 393224 | tf_op jit(solution)/shard_map/ppermute | solution.py:22
  45.9 4.9 %collective-permute-start.6 = (bf16[32,2048]{1,0:T(8,128)(2,1)S(1)}, bf16[32,2048]{1,0:T(8,128)(2,1)S(1)}, u32[]{:S(2)}, u32[]{:S(2)}) collective-permute-start(bf16[32,2048]{1,0:T(8,128)(2,1)S(1)} %get-tuple-element.89), channel_id=1, source_target_pairs={{0,1},{1,0},{2,3},{3,2},{4,5},{5,4},{6,7},{7,6},{8,9},{9,8},{10,11... | collective-permute-start | bytes 393224 | tf_op jit(solution)/shard_map/ppermute | solution.py:22

commit v4 on v3

--- a/solution.py
+++ b/solution.py
@@ -12,7 +12,10 @@
 SUB = 8
 TILE = 512
 PITCH = 40
-ROOM = 49
+ROOM = 48
+PIECE = 256
+CHUNK = 512
+UNROLL = 2
 F32 = jnp.float32
 BF16 = jnp.bfloat16
 
@@ -115,44 +118,69 @@
     return pl.ds(pl.multiple_of(core * half + offset, LANE), size)
 
 
-def front_kernel(lengths_ref, place_ref, f0_ref, f2_ref, halo_ref, taps_ref, pole_ref,
-                 z_ref, e_ref, end_ref, last_s, shift_s, z_s):
-    tokens = z_ref.shape[0]
-    width = f0_ref.shape[2]
+def front_kernel(lengths_ref, place_ref, features_ref, halo_ref, taps_ref, pole_ref, z_ref, e_ref, end_ref, *refs, mine):
+    last_s, shift_s, z_s = refs[-3:]
+    tokens, half = z_ref.shape
     count = tokens // BLK
     modes = pole_ref.shape[0] // 2
     halves = modes // SUB
-    origin = pl.program_id(0) * width
-    wide = z_s.shape[0] * LANE
+    wide = TILE
+    tiles = half // wide
+    if mine:
+        streams_ref = features_ref
+    else:
+        next_ref, streams_ref, sems, next_sems = refs[:4]
+        for j in range(tiles):
+            for u, r in enumerate((0, 2)):
+                lanes = half_lanes(place_ref, mine, half, j * wide, wide)
+                here = pl.ds(j * wide, wide)
+                pltpu.make_async_copy(features_ref.at[r, :, lanes], streams_ref.at[u, :, here], sems.at[u, j]).start()
+        lanes = half_lanes(place_ref, True, half, 0, half)
+        ahead = [pltpu.make_async_copy(features_ref.at[r, :, lanes], next_ref.at[u], next_sems.at[u])
+                 for u, r in enumerate((0, 2))]
+        for copy in ahead:
+            copy.start()
     starts = starts_of(lengths_ref, place_ref[0] * tokens)
     edges = edge_flags(starts)
-
-    @pl.when(pl.program_id(0) == 0)
-    def _():
-        t = row_iota(tokens)
-        last = jnp.full((tokens, LANE), -1, jnp.int32)
-        for s in starts:
-            last = jnp.maximum(last, jnp.where(s <= (t | (BLK - 1)), s, -1))
-        last_s[...] = jnp.where(t >= last, 1.0, 0.0)
-        shift_s[...] = shift_matrix(starts, tokens)
-
-    @pl.loop(0, width // wide)
-    def _(part):
-        lanes = pl.ds(pl.multiple_of(part * wide, LANE), wide)
-        conv0, conv2 = (
-            short_filter(ref[0, :, lanes], halo_ref[r, :, lanes], taps_ref[r, :, lanes], shift_s, edges)
-            for r, ref in ((0, f0_ref), (2, f2_ref))
-        )
-        z = (conv0 * conv2).astype(BF16)
-        z_ref[:, pl.ds(pl.multiple_of(origin + part * wide, LANE), wide)] = z
-        for i in range(wide // LANE):
-            z_s[i] = z[:, i * LANE : (i + 1) * LANE].astype(F32) * last_s[...]
-        for i in range(wide // LANE):
+    t = row_iota(tokens)
+    last = jnp.full((tokens, LANE), -1, jnp.int32)
+    for s in starts:
+        last = jnp.maximum(last, jnp.where(s <= (t | (BLK - 1)), s, -1))
+    last_s[...] = jnp.where(t >= last, 1.0, 0.0)
+    shift_s[...] = shift_matrix(starts, tokens)
+    flags = {}
+    span = BLK
+    while span < tokens:
+        for first in range(span, tokens, 2 * span):
+            flags[first, span] = none_in(starts, first, first + span)
+        span *= 2
+
+    @pl.loop(0, tiles)
+    def _(j):
+        if not mine:
+            here = pl.ds(pl.multiple_of(j * wide, LANE), wide)
+            lanes = half_lanes(place_ref, mine, half, j * wide, wide)
+            for u, r in enumerate((0, 2)):
+                pltpu.make_async_copy(features_ref.at[r, :, lanes], streams_ref.at[u, :, here], sems.at[u, j]).wait()
+
+        def gated(i, size):
+            at = pl.ds(pl.multiple_of(j * wide + i * LANE, LANE), size)
+            lanes = half_lanes(place_ref, mine, half, j * wide + i * LANE, size)
+            conv0, conv2 = (
+                short_filter(streams_ref[u, :, at], halo_ref[r, :, lanes], taps_ref[r, :, lanes], shift_s, edges)
+                for u, r in enumerate((0, 2))
+            )
+            z = (conv0 * conv2).astype(BF16)
+            z_ref[:, at] = z
+            for v in range(size // LANE):
+                z_s[i + v] = z[:, v * LANE : (v + 1) * LANE].astype(F32) * last_s[...]
+
+        def states(i):
+            at = pl.ds(pl.multiple_of(j * wide + i * LANE, LANE), LANE)
+            lanes = half_lanes(place_ref, mine, half, j * wide + i * LANE, LANE)
             z_i = z_s.at[i]
-            from_lane = pl.ds(pl.multiple_of(part * wide + i * LANE, LANE), LANE)
-            to_lane = pl.ds(pl.multiple_of(origin + part * wide + i * LANE, LANE), LANE)
-            p_re = [rows_of(pole_ref, h, from_lane) for h in range(halves)]
-            p_im = [rows_of(pole_ref, halves + h, from_lane) for h in range(halves)]
+            p_re = [rows_of(pole_ref, h, lanes) for h in range(halves)]
+            p_im = [rows_of(pole_ref, halves + h, lanes) for h in range(halves)]
             pow_re, pow_im = list(p_re), list(p_im)
             e_re, e_im = [], []
             for b in range(count):
@@ -171,21 +199,32 @@
             for h in range(halves):
                 rows, rows_im = pl.ds(h * SUB, SUB), pl.ds(modes + h * SUB, SUB)
                 for b in range(count):
-                    e_ref[b, rows, to_lane] = e_re[b][h]
-                    e_ref[b, rows_im, to_lane] = e_im[b][h]
+                    e_ref[b, rows, at] = e_re[b][h]
+                    e_ref[b, rows_im, at] = e_im[b][h]
                 gate = cmul(pow_re[h], pow_im[h], p_re[h], p_im[h])
                 level = [(e_re[b][h], e_im[b][h]) for b in range(count)]
                 span = BLK
                 while len(level) > 1:
-                    joined = []
-                    for i in range(0, len(level), 2):
-                        flag = none_in(starts, (i + 1) * span, (i + 2) * span)
-                        joined.append(advance(gate, flag, level[i], level[i + 1]))
-                    level = joined
+                    level = [
+                        advance(gate, flags[(i + 1) * span, span], level[i], level[i + 1])
+                        for i in range(0, len(level), 2)
+                    ]
                     gate = cmul(*gate, *gate)
                     span *= 2
-                end_ref[rows, to_lane] = level[0][0].astype(BF16)
-                end_ref[rows_im, to_lane] = level[0][1].astype(BF16)
+                end_ref[rows, at] = level[0][0].astype(BF16)
+                end_ref[rows_im, at] = level[0][1].astype(BF16)
+
+        lane_tiles = wide // LANE
+        gated(0, PIECE)
+        for i in range(lane_tiles):
+            following = (i // (PIECE // LANE) + 1) * (PIECE // LANE)
+            if i % (PIECE // LANE) == 0 and following < lane_tiles:
+                gated(following, PIECE)
+            states(i)
+
+    if not mine:
+        for copy in ahead:
+            copy.wait()
 
 
 def middle_kernel(lengths_ref, place_ref, features_ref, halo_ref, taps_ref, z_ref, skip_ref, pole_ref,
@@ -341,11 +380,11 @@
     flag = none_in(starts, second * tokens, (second + 1) * tokens)
     half = kept_ref.shape[1]
 
-    @pl.loop(0, half // LANE)
-    def _(tile):
-        lanes = lane_tile(tile)
+    @pl.loop(0, half // CHUNK)
+    def _(part):
+        lanes = pl.ds(pl.multiple_of(part * CHUNK, LANE), CHUNK)
         kept, came = split(kept_ref, lanes), split(came_ref, lanes)
-        gate = split(pole_ref, half_lanes(place_ref, True, half, tile * LANE, LANE))
+        gate = split(pole_ref, half_lanes(place_ref, True, half, part * CHUNK, CHUNK))
         reach = 1
         while reach < tokens:
             gate = cmul(*gate, *gate)
@@ -369,9 +408,9 @@
     whole = none_in(starts, later * tokens, (later + distance) * tokens)
     flag = none_in(starts, even * tokens, (even + 1) * tokens)
 
-    @pl.loop(0, met_ref.shape[1] // LANE)
-    def _(tile):
-        lanes = lane_tile(tile)
+    @pl.loop(0, met_ref.shape[1] // CHUNK)
+    def _(part):
+        lanes = pl.ds(pl.multiple_of(part * CHUNK, LANE), CHUNK)
         rest = list(refs)
         met, total = split(met_ref, lanes), split(total_ref, lanes)
         power = split(rest.pop(0), lanes)
@@ -410,8 +449,7 @@
     halves = modes // SUB
     origin = pl.program_id(0) * width
 
-    @pl.loop(0, width // LANE)
-    def _(tile):
+    def one_tile(tile, state_s):
         lanes = lane_tile(tile)
         here = pl.ds(pl.multiple_of(origin + tile * LANE, LANE), LANE)
         entry = entry_ref[:, here].astype(F32)
@@ -438,6 +476,11 @@
             carried = jnp.concatenate(sums[b], axis=0)
             out_ref[rows, lanes] = (base_ref[rows, here] + gain_ref[rows, here] * carried).astype(BF16)
 
+    @pl.loop(0, width // LANE // state_s.shape[0])
+    def _(step):
+        for v in range(state_s.shape[0]):
+            one_tile(step * state_s.shape[0] + v, state_s.at[v])
+
 
 def per_device(features, kernel, skip, residues, decay, freq, lengths):
     tokens = features.shape[1]
@@ -451,10 +494,7 @@
     where = place.astype(jnp.int32)[None]
 
     rim = features[:, tokens - 2 :, :]
-    inner = exchange(rim, 1)
-    link = [(i, i + 1) for i in range(1, n - 1, 2)]
-    outer = lax.ppermute(rim, "seq", link + [(b, a) for a, b in link])
-    halo = jnp.where(core == 1, inner, outer)
+    halo = lax.ppermute(rim, "seq", [(i, (i + 1) % n) for i in range(n)])
 
     fade = jnp.exp(-decay)
     q = freq * freq
@@ -492,26 +532,25 @@
         core = w_ref[0] & 1
         return (core if mine else 1 - core) * tiles + i
 
-    def front(mine):
-        def columns(*lead):
-            return pl.BlockSpec((*lead, TILE), lambda i, n_ref, w_ref: (*(0,) * len(lead), tile_of(mine, i, w_ref)))
-
-        def stream(r):
-            return pl.BlockSpec((1, tokens, TILE), lambda i, n_ref, w_ref: (r, 0, tile_of(mine, i, w_ref)))
-
+    def front(mine, streams):
+        outs = [((tokens, half), BF16), blocks, sent]
+        scratch = [plane, shifts, pltpu.VMEM((TILE // LANE, tokens, LANE), F32)]
+        if not mine:
+            pair = (2, tokens, half)
+            outs = outs + [(pair, BF16)]
+            scratch = [pltpu.VMEM(pair, BF16), pltpu.SemaphoreType.DMA((2, half // TILE)),
+                       pltpu.SemaphoreType.DMA((2,))] + scratch
         return pl.pallas_call(
-            front_kernel,
+            functools.partial(front_kernel, mine=mine),
             grid_spec=pltpu.PrefetchScalarGridSpec(
-                num_scalar_prefetch=2, grid=(tiles,),
-                in_specs=[stream(0), stream(2), columns(3, 2), columns(3, 3), columns(packed)],
-                out_specs=[whole] * 3,
-                scratch_shapes=[plane, shifts, pltpu.VMEM((TILE // LANE, tokens, LANE), F32)],
+                num_scalar_prefetch=2, grid=(),
+                in_specs=[whole if mine else pl.BlockSpec(memory_space=pl.ANY)] + [whole] * 3,
+                out_specs=[whole] * len(outs), scratch_shapes=scratch,
             ),
-            out_shape=[jax.ShapeDtypeStruct((tokens, half), BF16), jax.ShapeDtypeStruct(*blocks),
-                       jax.ShapeDtypeStruct(*sent)],
-            compiler_params=roomy, name="front",
+            out_shape=[jax.ShapeDtypeStruct(*o) for o in outs],
+            compiler_params=params if mine else roomy, name="front",
             cost_estimate=pl.CostEstimate(flops=5_000_000_000, bytes_accessed=4 << 20, transcendentals=0),
-        )(lengths, where, features, features, halo, kernel, pole)
+        )(lengths, where, streams, halo, kernel, pole)
 
     def middle(mine, z):
         return call(
@@ -535,7 +574,7 @@
             grid_spec=pltpu.PrefetchScalarGridSpec(
                 num_scalar_prefetch=1, grid=(tiles,), in_specs=specs,
                 out_specs=pl.BlockSpec((tokens, TILE), lambda i, w_ref: (0, tile_of(mine, i, w_ref))),
-                scratch_shapes=[pltpu.VMEM((count * packed, LANE), F32)],
+                scratch_shapes=[pltpu.VMEM((UNROLL, count * packed, LANE), F32)],
             ),
             out_shape=jax.ShapeDtypeStruct((tokens, width), BF16),
             input_output_aliases={} if out is None else {len(args): 0},
@@ -543,9 +582,9 @@
             cost_estimate=pl.CostEstimate(flops=3_500_000_000, bytes_accessed=1 << 20, transcendentals=0),
         )(where, *args)
 
-    z_other, e_other, end_other = front(False)
+    z_other, e_other, end_other, streams = front(False, features)
     came = exchange(end_other, 1)
-    z_own, e_own, end_own = front(True)
+    z_own, e_own, end_own = front(True, streams)
     total, send, gate = call(
         functools.partial(first_kernel, tokens=tokens), (end_own, came, pole), (state, sent, state), "first"
     )

time: 54.6 us -> 49.5 us (0.907)
  starting transfers between devices: 11.4 us -> 8.32 us
  Pallas kernels: 37.2 us -> 35.9 us
    pallas_call x2, Pallas kernels: 12.8 us -> 10.6 us  [front(): pl.pallas_call(functools.partial(front_kernel, mine=mine), grid_spec=pltp...]
    ppermute x1, starting transfers between devices: 4.54 us -> 2.68 us  [per_device(): halo = lax.ppermute(rim, 'seq', [(i, (i + 1) % n) for i in range(n)])]
    ppermute x6 -> x5, starting transfers between devices: 6.88 us -> 5.64 us  [exchange(): return lax.ppermute(block, 'seq', [(i, i ^ distance) for i in devices])]
    pallas_call x8, Pallas kernels: 17.1 us -> 18.1 us  [call(): pl.pallas_call(body, grid_spec=pltpu.PrefetchScalarGridSpec(num_scalar_pr...]
    ppermute x6 -> x5, waiting for transfers between devices: 1.98 us -> 1.5 us  [exchange(): return lax.ppermute(block, 'seq', [(i, i ^ distance) for i in devices])]
  transfers between devices with their start and end apart: 7 -> 6, of which waited for: 1 -> 1; matrix products, arithmetic and copies ran while one was open for 5% -> 5% of each run, Pallas kernels for 44% -> 47%
where the time goes in v4:
time: 49.5 us
  Pallas kernels  35.9 us (73%)
  starting transfers between devices  8.32 us (17%)
  other arithmetic  2.53 us (5%)
  waiting for transfers between devices  1.5 us (3%)
  local copies, waits for them, and re-layouts  1.04 us (2%)
    pallas_call x8, Pallas kernels, call(): pl.pallas_call(body, grid_spec=pltpu.PrefetchScalarGridSpec(num_scalar_pr...  18.1 us
    pallas_call x2, Pallas kernels, front(): pl.pallas_call(functools.partial(front_kernel, mine=mine), grid_spec=pltp...  10.6 us
    pallas_call x2, Pallas kernels, back(): pl.pallas_call(back_kernel, grid_spec=pltpu.PrefetchScalarGridSpec(num_sc...  7.21 us
    ppermute x5, starting transfers between devices, exchange(): return lax.ppermute(block, 'seq', [(i, i ^ distance) for i in devices])  5.64 us
    ppermute x1, starting transfers between devices, per_device(): halo = lax.ppermute(rim, 'seq', [(i, (i + 1) % n) for i in range(n)])  2.68 us
    another operation x2, other arithmetic, per_device(): pole = jnp.stack([fade * cosine, fade * sine]).reshape(2 * modes, width)  2.53 us
    ppermute x5, waiting for transfers between devices, exchange(): return lax.ppermute(block, 'seq', [(i, i ^ distance) for i in devices])  1.5 us
    slice x1, local copies, waits for them, and re-layouts, per_device(): rim = features[:, tokens - 2:, :]  1.02 us
  transfers between devices with their start and end apart: 6, of which 1 were waited for; matrix products, arithmetic and copies ran while one was open for 5% of the time, Pallas kernels for 47%

profile of v4, /device:TPU:1, one launch (start us, length us, event | category | flops | bytes accessed | tf_op | source)
XLA Modules:
  0.0 49.5 jit_solution(516395934401775853)
XLA Ops:
  0.0 1.0 %slice.3 = bf16[3,2,4096]{2,1,0:T(2,128)(2,1)S(1)} slice(bf16[3,128,4096]{2,1,0:T(8,128)(2,1)} %features_ref.5), slice={[0:3], [126:128], [0:4096]} | slice | bytes 98304 | tf_op jit(solution)/shard_map/slice | solution.py:496
  1.0 2.7 %collective-permute-start = (bf16[3,2,4096]{2,1,0:T(2,128)(2,1)S(1)}, bf16[3,2,4096]{2,1,0:T(2,128)(2,1)S(1)}, u32[]{:S(2)}, u32[]{:S(2)}) collective-permute-start(bf16[3,2,4096]{2,1,0:T(2,128)(2,1)S(1)} %slice.3), channel_id=1, source_target_pairs={{0,1},{1,2},{2,3},{3,4},{4,5},{5,6},{6,7},{7,8},{8,9},{9,10},{10,1... | collective-permute-start | bytes 147464 | tf_op jit(solution)/shard_map/ppermute | solution.py:497
  3.7 1.4 %fusion.6 = (f32[1,16,4096]{2,1,0:T(8,128)S(1)}, f32[1,16,4096]{2,1,0:T(8,128)S(1)}, f32[16,4096]{1,0:T(8,128)S(1)}) fusion(f32[16,4096]{1,0:T(8,128)} %param.12, f32[16,4096]{1,0:T(8,128)} %param.11), kind=kLoop, calls=%fused_computation.17 | loop fusion | flops 2293760 | bytes 1310720 | tf_op jit(solution)/shard_map/stack | solution.py:505
  5.1 1.1 %pad_maximum_fusion = (f32[2,16,4096]{2,1,0:T(8,128)S(1)}, f32[2,16,4096]{2,1,0:T(8,128)S(1)}) fusion(f32[1,16,4096]{2,1,0:T(8,128)S(1)} %get-tuple-element.104, f32[1,16,4096]{2,1,0:T(8,128)S(1)} %get-tuple-element.103, f32[2,16,4096]{2,1,0:T(8,128)} %param.10, f32[16,4096]{1,0:T(8,128)S(1)} %get-tuple-element.105), kind=kLoop, calls=%fused_computation | loop fusion | flops 262144 | bytes 2359296 | tf_op jit(solution)/shard_map/stack | solution.py:505
  6.3 5.8 %front.2 = (bf16[128,2048]{1,0:T(8,128)(2,1)S(1)}, f32[8,32,2048]{2,1,0:T(8,128)S(1)}, bf16[32,2048]{1,0:T(8,128)(2,1)S(1)}, bf16[2,128,2048]{2,1,0:T(8,128)(2,1)S(1)}) custom-call(s32[6]{0:T(128)S(1)} %copy-done.3, s32[1]{0:T(128)} %bitcast.place_ref, bf16[3,128,4096]{2,1,0:T(8,128)(2,1)} %features_ref.5, ...), custom_call_target="tpu_custom_call" | custom-call | flops 5000000000 | bytes 4194304 | tf_op jit(solution)/shard_map/front/pallas_call | solution.py:543
  12.0 2.2 %collective-permute-start.1 = (bf16[32,2048]{1,0:T(8,128)(2,1)S(1)}, bf16[32,2048]{1,0:T(8,128)(2,1)S(1)}, u32[]{:S(2)}, u32[]{:S(2)}) collective-permute-start(bf16[32,2048]{1,0:T(8,128)(2,1)S(1)} %get-tuple-element.56), channel_id=1, source_target_pairs={{0,1},{1,0},{2,3},{3,2},{4,5},{5,4},{6,7},{7,6},{8,9},{9,8},{10,11... | collective-permute-start | bytes 393224 | tf_op jit(solution)/shard_map/ppermute | solution.py:25
  14.2 4.9 %front.3 = (bf16[128,2048]{1,0:T(8,128)(2,1)S(1)}, f32[8,32,2048]{2,1,0:T(8,128)S(1)}, bf16[32,2048]{1,0:T(8,128)(2,1)S(1)}) custom-call(s32[6]{0:T(128)S(1)} %copy-done.3, s32[1]{0:T(128)} %bitcast.place_ref, bf16[2,128,2048]{2,1,0:T(8,128)(2,1)S(1)} %get-tuple-element.54.features_ref, bf16[3,2,4096]{2,1,0:T(2,128)(2,1)S(1)} %collective-permute-done.halo_ref, ...), custom_call_target="tpu_custom_call" | custom-call | flops 5000000000 | bytes 4194304 | tf_op jit(solution)/shard_map/front/pallas_call | solution.py:543
  19.1 0.0 copy-start.2
  19.1 0.8 %first.1 = (f32[32,2048]{1,0:T(8,128)S(1)}, bf16[32,2048]{1,0:T(8,128)(2,1)S(1)}, f32[32,2048]{1,0:T(8,128)S(1)}) custom-call(s32[6]{0:T(128)S(1)} %copy-done.3, s32[1]{0:T(128)} %bitcast.place_ref, bf16[32,2048]{1,0:T(8,128)(2,1)S(1)} %get-tuple-element.55.kept_ref.refs_4_, bf16[32,2048]{1,0:T(8,128)(2,1)S(1)} %collective-permute-done.1.came_ref.refs_5_, ...), custom_call_target="tpu_custom_call" | custom-call | flops 800000000 | bytes 1048576 | tf_op jit(solution)/shard_map/first/pallas_call | solution.py:515
  19.9 0.1 collective-permute-start.2
  20.0 5.0 %middle.2 = (f32[128,2048]{1,0:T(8,128)S(1)}, f32[128,2048]{1,0:T(8,128)S(1)}) custom-call(s32[6]{0:T(128)S(1)} %copy-done.3, s32[1]{0:T(128)} %bitcast.place_ref, bf16[3,128,4096]{2,1,0:T(8,128)(2,1)S(1)} %copy-done, bf16[3,2,4096]{2,1,0:T(2,128)(2,1)S(1)} %collective-permute-done.halo_ref, f32[3,3,4096]{2,1,0:T(4,128)S(1)} %copy-done.1, ...), custom_call_target="tpu_custom_call" | custom-call | flops 5000000000 | bytes 1048576 | tf_op jit(solution)/shard_map/middle/pallas_call | solution.py:515
  25.1 0.0 collective-permute-done.2.met_ref
  25.1 0.7 %round.3 = (f32[32,2048]{1,0:T(8,128)S(1)}, bf16[32,2048]{1,0:T(8,128)(2,1)S(1)}, f32[32,2048]{1,0:T(8,128)S(1)}, f32[32,2048]{1,0:T(8,128)S(1)}, f32[32,2048]{1,0:T(8,128)S(1)}) custom-call(s32[6]{0:T(128)S(1)} %copy-done.3, s32[1]{0:T(128)} %bitcast.place_ref, f32[32,2048]{1,0:T(8,128)S(1)} %get-tuple-element.57.total_ref, ...), custom_call_target="tpu_custom_call" | custom-call | flops 800000000 | bytes 1048576 | tf_op jit(solution)/shard_map/round/pallas_call | solution.py:515
  25.8 0.1 collective-permute-start.3
  25.9 5.1 %middle.3 = (f32[128,2048]{1,0:T(8,128)S(1)}, f32[128,2048]{1,0:T(8,128)S(1)}) custom-call(s32[6]{0:T(128)S(1)} %copy-done.3, s32[1]{0:T(128)} %bitcast.place_ref, bf16[3,128,4096]{2,1,0:T(8,128)(2,1)S(1)} %copy-done, bf16[3,2,4096]{2,1,0:T(2,128)(2,1)S(1)} %collective-permute-done.halo_ref, f32[3,3,4096]{2,1,0:T(4,128)S(1)} %copy-done.1, ...), custom_call_target="tpu_custom_call" | custom-call | flops 5000000000 | bytes 1048576 | tf_op jit(solution)/shard_map/middle/pallas_call | solution.py:515
  31.0 0.8 %round.4 = (f32[32,2048]{1,0:T(8,128)S(1)}, bf16[32,2048]{1,0:T(8,128)(2,1)S(1)}, f32[32,2048]{1,0:T(8,128)S(1)}, f32[32,2048]{1,0:T(8,128)S(1)}, f32[32,2048]{1,0:T(8,128)S(1)}) custom-call(s32[6]{0:T(128)S(1)} %copy-done.3, s32[1]{0:T(128)} %bitcast.place_ref, f32[32,2048]{1,0:T(8,128)S(1)} %get-tuple-element.65.total_ref, ...), custom_call_target="tpu_custom_call" | custom-call | flops 800000000 | bytes 1048576 | tf_op jit(solution)/shard_map/round/pallas_call | solution.py:515
  31.8 2.3 %collective-permute-start.4 = (bf16[32,2048]{1,0:T(8,128)(2,1)S(1)}, bf16[32,2048]{1,0:T(8,128)(2,1)S(1)}, u32[]{:S(2)}, u32[]{:S(2)}) collective-permute-start(bf16[32,2048]{1,0:T(8,128)(2,1)S(1)} %get-tuple-element.76), channel_id=1, source_target_pairs={{0,8},{1,9},{2,10},{3,11},{4,12},{5,13},{6,14},{7,15},{8,0},{9,1},... | collective-permute-start | bytes 393224 | tf_op jit(solution)/shard_map/ppermute | solution.py:25
  34.1 2.5 %prepare.2 = (f32[32,16,2048]{2,1,0:T(8,128)S(1)}, f32[8,32,2048]{2,1,0:T(8,128)S(1)}, f32[8,32,2048]{2,1,0:T(8,128)S(1)}) custom-call(s32[6]{0:T(128)S(1)} %copy-done.3, s32[1]{0:T(128)} %bitcast.place_ref, f32[8,32,2048]{2,1,0:T(8,128)S(1)} %get-tuple-element.79.e_ref, f32[32,4096]{1,0:T(8,128)S(1)} %bitcast.13, f32[32,4096]{1,0:T(8,128)S(1)} %bitcast.17), custom_call_target="tpu_custom_call" | custom-call | flops 4000000000 | bytes 1048576 | tf_op jit(solution)/shard_map/prepare/pallas_call | solution.py:515
  36.5 2.5 %prepare.3 = (f32[32,16,2048]{2,1,0:T(8,128)S(1)}, f32[8,32,2048]{2,1,0:T(8,128)S(1)}, f32[8,32,2048]{2,1,0:T(8,128)S(1)}) custom-call(s32[6]{0:T(128)S(1)} %copy-done.3, s32[1]{0:T(128)} %bitcast.place_ref, f32[8,32,2048]{2,1,0:T(8,128)S(1)} %get-tuple-element.83.e_ref, f32[32,4096]{1,0:T(8,128)S(1)} %bitcast.14, f32[32,4096]{1,0:T(8,128)S(1)} %bitcast.18), custom_call_target="tpu_custom_call" | custom-call | flops 4000000000 | bytes 1048576 | tf_op jit(solution)/shard_map/prepare/pallas_call | solution.py:515
  39.0 1.5 %collective-permute-done.4.met_ref = bf16[32,2048]{1,0:T(8,128)(2,1)S(1)} collective-permute-done((bf16[32,2048]{1,0:T(8,128)(2,1)S(1)}, bf16[32,2048]{1,0:T(8,128)(2,1)S(1)}, u32[]{:S(2)}, u32[]{:S(2)}) %collective-permute-start.4) | collective-permute-done | bytes 131104 | tf_op jit(solution)/shard_map/ppermute | solution.py:25
  40.5 0.7 %round.5 = (f32[32,2048]{1,0:T(8,128)S(1)}, bf16[32,2048]{1,0:T(8,128)(2,1)S(1)}) custom-call(s32[6]{0:T(128)S(1)} %copy-done.3, s32[1]{0:T(128)} %bitcast.place_ref, f32[32,2048]{1,0:T(8,128)S(1)} %get-tuple-element.75.total_ref, bf16[32,2048]{1,0:T(8,128)(2,1)S(1)} %collective-permute-done.4.met_ref, f32[32,2048]{1,0:T(8,128)S(1)} %get-tuple-element.88.refs_0_, ...), custom_call_target="tpu_custom_call" | custom-call | flops 800000000 | bytes 1048576 | tf_op jit(solution)/shard_map/round/pallas_call | solution.py:515
  41.2 1.0 %collective-permute-start.5 = (bf16[32,2048]{1,0:T(8,128)(2,1)S(1)}, bf16[32,2048]{1,0:T(8,128)(2,1)S(1)}, u32[]{:S(2)}, u32[]{:S(2)}) collective-permute-start(bf16[32,2048]{1,0:T(8,128)(2,1)S(1)} %get-tuple-element.91), channel_id=1, source_target_pairs={{0,1},{1,0},{2,3},{3,2},{4,5},{5,4},{6,7},{7,6},{8,9},{9,8},{10,11... | collective-permute-start | bytes 393224 | tf_op jit(solution)/shard_map/ppermute | solution.py:25
  42.2 3.6 %back.2.refs_0_ = bf16[128,4096]{1,0:T(8,128)(2,1)} custom-call(s32[1]{0:T(128)} %bitcast.place_ref, f32[32,2048]{1,0:T(8,128)S(1)} %get-tuple-element.97.entry_ref, f32[32,16,2048]{2,1,0:T(8,128)S(1)} %get-tuple-element.98.table_ref, f32[8,32,2048]{2,1,0:T(8,128)S(1)} %get-tuple-element.99.local_ref, f32[8,32,2048]{2,1,0:T(8,128)S(1)} %get-tuple-element.100.reach_ref, ...), custom_call_target="tpu_custom_call" | custom-call | flops 3500000000 | bytes 1048576 | tf_op jit(solution)/shard_map/back/pallas_call | solution.py:572
  45.9 3.6 %back.3 = bf16[128,4096]{1,0:T(8,128)(2,1)} custom-call(s32[1]{0:T(128)} %bitcast.place_ref, bf16[32,2048]{1,0:T(8,128)(2,1)S(1)} %collective-permute-done.5.entry_ref, f32[32,16,2048]{2,1,0:T(8,128)S(1)} %get-tuple-element.92.table_ref, f32[8,32,2048]{2,1,0:T(8,128)S(1)} %get-tuple-element.93.local_ref, ...), custom_call_target="tpu_custom_call", output_to_operand_aliasing={{}: (7, {})} | custom-call | flops 3500000000 | bytes 1048576 | tf_op jit(solution)/shard_map/back/pallas_call | solution.py:572
  (11 shorter events, 0.0 us)
Async XLA Ops:
  0.0 6.3 %copy-start.3 = (s32[6]{0:T(128)S(1)}, s32[6]{0:T(128)}, u32[]{:S(2)}) copy-start(s32[6]{0:T(128)} %lengths_ref.19) | copy-start | bytes 76
  0.0 6.3 %copy-start.1 = (f32[3,3,4096]{2,1,0:T(4,128)S(1)}, f32[3,3,4096]{2,1,0:T(4,128)}, u32[]{:S(2)}) copy-start(f32[3,3,4096]{2,1,0:T(4,128)} %taps_ref.7) | copy-start | bytes 442372
  1.0 5.2 %collective-permute-start = (bf16[3,2,4096]{2,1,0:T(2,128)(2,1)S(1)}, bf16[3,2,4096]{2,1,0:T(2,128)(2,1)S(1)}, u32[]{:S(2)}, u32[]{:S(2)}) collective-permute-start(bf16[3,2,4096]{2,1,0:T(2,128)(2,1)S(1)} %slice.3), channel_id=1, source_target_pairs={{0,1},{1,2},{2,3},{3,4},{4,5},{5,6},{6,7},{7,8},{8,9},{9,10},{10,1... | collective-permute-start | bytes 147464 | tf_op jit(solution)/shard_map/ppermute | solution.py:497
  12.0 7.0 %collective-permute-start.1 = (bf16[32,2048]{1,0:T(8,128)(2,1)S(1)}, bf16[32,2048]{1,0:T(8,128)(2,1)S(1)}, u32[]{:S(2)}, u32[]{:S(2)}) collective-permute-start(bf16[32,2048]{1,0:T(8,128)(2,1)S(1)} %get-tuple-element.56), channel_id=1, source_target_pairs={{0,1},{1,0},{2,3},{3,2},{4,5},{5,4},{6,7},{7,6},{8,9},{9,8},{10,11... | collective-permute-start | bytes 393224 | tf_op jit(solution)/shard_map/ppermute | solution.py:25
  14.2 5.8 %copy-start = (bf16[3,128,4096]{2,1,0:T(8,128)(2,1)S(1)}, bf16[3,128,4096]{2,1,0:T(8,128)(2,1)}, u32[]{:S(2)}) copy-start(bf16[3,128,4096]{2,1,0:T(8,128)(2,1)} %features_ref.5) | copy-start | bytes 9437188
  19.1 0.9 %copy-start.2 = (f32[4096]{0:T(1024)S(1)}, f32[4096]{0:T(1024)}, u32[]{:S(2)}) copy-start(f32[4096]{0:T(1024)} %param.9) | copy-start | bytes 49156
  19.9 5.2 %collective-permute-start.2 = (bf16[32,2048]{1,0:T(8,128)(2,1)S(1)}, bf16[32,2048]{1,0:T(8,128)(2,1)S(1)}, u32[]{:S(2)}, u32[]{:S(2)}) collective-permute-start(bf16[32,2048]{1,0:T(8,128)(2,1)S(1)} %get-tuple-element.58), channel_id=1, source_target_pairs={{0,2},{1,3},{2,0},{3,1},{4,6},{5,7},{6,4},{7,5},{8,10},{9,11},{10,... | collective-permute-start | bytes 393224 | tf_op jit(solution)/shard_map/ppermute | solution.py:25
  25.8 5.2 %collective-permute-start.3 = (bf16[32,2048]{1,0:T(8,128)(2,1)S(1)}, bf16[32,2048]{1,0:T(8,128)(2,1)S(1)}, u32[]{:S(2)}, u32[]{:S(2)}) collective-permute-start(bf16[32,2048]{1,0:T(8,128)(2,1)S(1)} %get-tuple-element.66), channel_id=1, source_target_pairs={{0,4},{1,5},{2,6},{3,7},{4,0},{5,1},{6,2},{7,3},{8,12},{9,13},{10,... | collective-permute-start | bytes 393224 | tf_op jit(solution)/shard_map/ppermute | solution.py:25
  31.8 8.7 %collective-permute-start.4 = (bf16[32,2048]{1,0:T(8,128)(2,1)S(1)}, bf16[32,2048]{1,0:T(8,128)(2,1)S(1)}, u32[]{:S(2)}, u32[]{:S(2)}) collective-permute-start(bf16[32,2048]{1,0:T(8,128)(2,1)S(1)} %get-tuple-element.76), channel_id=1, source_target_pairs={{0,8},{1,9},{2,10},{3,11},{4,12},{5,13},{6,14},{7,15},{8,0},{9,1},... | collective-permute-start | bytes 393224 | tf_op jit(solution)/shard_map/ppermute | solution.py:25
  41.2 4.7 %collective-permute-start.5 = (bf16[32,2048]{1,0:T(8,128)(2,1)S(1)}, bf16[32,2048]{1,0:T(8,128)(2,1)S(1)}, u32[]{:S(2)}, u32[]{:S(2)}) collective-permute-start(bf16[32,2048]{1,0:T(8,128)(2,1)S(1)} %get-tuple-element.91), channel_id=1, source_target_pairs={{0,1},{1,0},{2,3},{3,2},{4,5},{5,4},{6,7},{7,6},{8,9},{9,8},{10,11... | collective-permute-start | bytes 393224 | tf_op jit(solution)/shard_map/ppermute | solution.py:25

commit v5 on v4

--- a/solution.py
+++ b/solution.py
@@ -12,7 +12,7 @@
 SUB = 8
 TILE = 512
 PITCH = 40
-ROOM = 48
+ROOM = 50
 PIECE = 256
 CHUNK = 512
 UNROLL = 2
@@ -112,62 +112,78 @@
     return ref[pl.ds(h * SUB, SUB), lanes]
 
 
-def half_lanes(place_ref, mine, half, offset, size):
-    core = place_ref[0] & 1
+def half_lanes(mine, half, offset, size):
+    core = lax.axis_index("seq") & 1
     core = core if mine else 1 - core
     return pl.ds(pl.multiple_of(core * half + offset, LANE), size)
 
 
-def front_kernel(lengths_ref, place_ref, features_ref, halo_ref, taps_ref, pole_ref, z_ref, e_ref, end_ref, *refs, mine):
-    last_s, shift_s, z_s = refs[-3:]
+def flag_rows(rounds):
+    names = ["odd", "second", "even", "edge0", "edge1", "edge2"] + [("tree", i) for i in range(16)]
+    names += [(kind, k) for k in range(1, rounds) for kind in ("upper", "enter", "whole")]
+    return {name: i for i, name in enumerate(names)}
+
+
+def prelude_kernel(lengths_ref, features_ref, streams_ref, shift_ref, last_ref, flags_ref, sems, *, rounds):
+    copies = [pltpu.make_async_copy(features_ref.at[r], streams_ref.at[u], sems.at[u]) for u, r in enumerate((0, 2))]
+    for copy in copies:
+        copy.start()
+    tokens = streams_ref.shape[1]
+    place = lax.axis_index("seq")
+    starts = starts_of(lengths_ref, place * tokens)
+    t = row_iota(tokens)
+    last = jnp.full((tokens, LANE), -1, jnp.int32)
+    for s in starts:
+        last = jnp.maximum(last, jnp.where(s <= (t | (BLK - 1)), s, -1))
+    last_ref[...] = jnp.where(t >= last, 1.0, 0.0)
+    shift_ref[...] = shift_matrix(starts, tokens)
+    values = dict(zip(("edge0", "edge1", "edge2"), edge_flags(starts)))
+    span, i = BLK, 0
+    while span < tokens:
+        for first in range(span, tokens, 2 * span):
+            values["tree", i] = none_in(starts, first, first + span)
+            i += 1
+        span *= 2
+    starts = starts_of(lengths_ref, 0)
+    even, second = place & -2, place | 1
+    values["odd"] = (place & 1).astype(F32)
+    values["even"] = none_in(starts, even * tokens, (even + 1) * tokens)
+    values["second"] = none_in(starts, second * tokens, (second + 1) * tokens)
+    for k in range(1, rounds):
+        distance = 1 << k
+        upper = ((place >> k) & 1).astype(F32)
+        group = (place >> k) << k
+        later = group | distance
+        values["upper", k] = upper
+        values["enter", k] = upper * none_in(starts, group * tokens, even * tokens)
+        values["whole", k] = none_in(starts, later * tokens, (later + distance) * tokens)
+    for name, row in flag_rows(rounds).items():
+        if name in values:
+            flags_ref[row : row + 1, :] = jnp.full((1, CHUNK), values[name], F32)
+    for copy in copies:
+        copy.wait()
+
+
+def front_kernel(streams_ref, halo_ref, taps_ref, pole_ref, shift_s, last_s, flags_ref, z_ref, e_ref, end_ref, z_s, *, mine):
     tokens, half = z_ref.shape
     count = tokens // BLK
     modes = pole_ref.shape[0] // 2
     halves = modes // SUB
     wide = TILE
-    tiles = half // wide
-    if mine:
-        streams_ref = features_ref
-    else:
-        next_ref, streams_ref, sems, next_sems = refs[:4]
-        for j in range(tiles):
-            for u, r in enumerate((0, 2)):
-                lanes = half_lanes(place_ref, mine, half, j * wide, wide)
-                here = pl.ds(j * wide, wide)
-                pltpu.make_async_copy(features_ref.at[r, :, lanes], streams_ref.at[u, :, here], sems.at[u, j]).start()
-        lanes = half_lanes(place_ref, True, half, 0, half)
-        ahead = [pltpu.make_async_copy(features_ref.at[r, :, lanes], next_ref.at[u], next_sems.at[u])
-                 for u, r in enumerate((0, 2))]
-        for copy in ahead:
-            copy.start()
-    starts = starts_of(lengths_ref, place_ref[0] * tokens)
-    edges = edge_flags(starts)
-    t = row_iota(tokens)
-    last = jnp.full((tokens, LANE), -1, jnp.int32)
-    for s in starts:
-        last = jnp.maximum(last, jnp.where(s <= (t | (BLK - 1)), s, -1))
-    last_s[...] = jnp.where(t >= last, 1.0, 0.0)
-    shift_s[...] = shift_matrix(starts, tokens)
-    flags = {}
-    span = BLK
-    while span < tokens:
-        for first in range(span, tokens, 2 * span):
-            flags[first, span] = none_in(starts, first, first + span)
-        span *= 2
-
-    @pl.loop(0, tiles)
+    rows_at = flag_rows(1)
+
+    def flag(name, size):
+        return flags_ref[rows_at[name] : rows_at[name] + 1, 0:size]
+
+    edges = [flag(name, PIECE) for name in ("edge0", "edge1", "edge2")]
+
+    @pl.loop(0, half // wide)
     def _(j):
-        if not mine:
-            here = pl.ds(pl.multiple_of(j * wide, LANE), wide)
-            lanes = half_lanes(place_ref, mine, half, j * wide, wide)
-            for u, r in enumerate((0, 2)):
-                pltpu.make_async_copy(features_ref.at[r, :, lanes], streams_ref.at[u, :, here], sems.at[u, j]).wait()
-
         def gated(i, size):
             at = pl.ds(pl.multiple_of(j * wide + i * LANE, LANE), size)
-            lanes = half_lanes(place_ref, mine, half, j * wide + i * LANE, size)
+            lanes = half_lanes(mine, half, j * wide + i * LANE, size)
             conv0, conv2 = (
-                short_filter(streams_ref[u, :, at], halo_ref[r, :, lanes], taps_ref[r, :, lanes], shift_s, edges)
+                short_filter(streams_ref[u, :, lanes], halo_ref[r, :, lanes], taps_ref[r, :, lanes], shift_s, edges)
                 for u, r in enumerate((0, 2))
             )
             z = (conv0 * conv2).astype(BF16)
@@ -177,7 +193,7 @@
 
         def states(i):
             at = pl.ds(pl.multiple_of(j * wide + i * LANE, LANE), LANE)
-            lanes = half_lanes(place_ref, mine, half, j * wide + i * LANE, LANE)
+            lanes = half_lanes(mine, half, j * wide + i * LANE, LANE)
             z_i = z_s.at[i]
             p_re = [rows_of(pole_ref, h, lanes) for h in range(halves)]
             p_im = [rows_of(pole_ref, halves + h, lanes) for h in range(halves)]
@@ -203,14 +219,14 @@
                     e_ref[b, rows_im, at] = e_im[b][h]
                 gate = cmul(pow_re[h], pow_im[h], p_re[h], p_im[h])
                 level = [(e_re[b][h], e_im[b][h]) for b in range(count)]
-                span = BLK
+                step = 0
                 while len(level) > 1:
+                    pairs = range(0, len(level), 2)
                     level = [
-                        advance(gate, flags[(i + 1) * span, span], level[i], level[i + 1])
-                        for i in range(0, len(level), 2)
+                        advance(gate, flag(("tree", step + i // 2), LANE), level[i], level[i + 1]) for i in pairs
                     ]
+                    step += len(pairs)
                     gate = cmul(*gate, *gate)
-                    span *= 2
                 end_ref[rows, at] = level[0][0].astype(BF16)
                 end_ref[rows_im, at] = level[0][1].astype(BF16)
 
@@ -222,18 +238,14 @@
                 gated(following, PIECE)
             states(i)
 
-    if not mine:
-        for copy in ahead:
-            copy.wait()
-
-
-def middle_kernel(lengths_ref, place_ref, features_ref, halo_ref, taps_ref, z_ref, skip_ref, pole_ref,
+
+def middle_kernel(lengths_ref, features_ref, halo_ref, taps_ref, z_ref, skip_ref, pole_ref,
                   coef_ref, base_ref, gain_ref, first_s, part_s, z_s, filt_s, acc_s, shift_s, piece_s, *, mine):
     tokens, half = z_ref.shape
     count = tokens // BLK
     modes = pole_ref.shape[0] // 2
     halves = modes // SUB
-    starts = starts_of(lengths_ref, place_ref[0] * tokens)
+    starts = starts_of(lengths_ref, lax.axis_index("seq") * tokens)
     edges = edge_flags(starts)
     t = row_iota(tokens)
     t0 = t & (-BLK)
@@ -257,7 +269,7 @@
     @pl.loop(0, half // wide)
     def _(part):
         here = pl.ds(pl.multiple_of(part * wide, LANE), wide)
-        lanes = half_lanes(place_ref, mine, half, part * wide, wide)
+        lanes = half_lanes(mine, half, part * wide, wide)
         conv1 = short_filter(features_ref[1, :, lanes], halo_ref[1, :, lanes], taps_ref[1, :, lanes], shift_s, edges)
         base_ref[:, here] = conv1
         for i in range(wide // LANE):
@@ -267,7 +279,7 @@
     @pl.loop(0, half // LANE)
     def _(tile):
         here = lane_tile(tile)
-        lanes = half_lanes(place_ref, mine, half, tile * LANE, LANE)
+        lanes = half_lanes(mine, half, tile * LANE, LANE)
         p_re = [rows_of(pole_ref, h, lanes) for h in range(halves)]
         p_im = [rows_of(pole_ref, halves + h, lanes) for h in range(halves)]
         q_re = [rows_of(coef_ref, h, lanes) for h in range(halves)]
@@ -315,18 +327,18 @@
         base_ref[:, here] = base_ref[:, here] * acc_s[...]
 
 
-def prepare_kernel(lengths_ref, place_ref, e_ref, pole_ref, coef_ref, table_ref, local_ref, reach_ref, turn_s, *, mine):
+def prepare_kernel(lengths_ref, e_ref, pole_ref, coef_ref, table_ref, local_ref, reach_ref, turn_s, *, mine):
     count, packed, half = e_ref.shape
     modes = packed // 2
     halves = modes // SUB
-    starts = starts_of(lengths_ref, place_ref[0] * count * BLK)
+    starts = starts_of(lengths_ref, lax.axis_index("seq") * count * BLK)
     flags = block_flags(starts, count)
     pitch = turn_s.shape[0] // BLK
 
     @pl.loop(0, half // LANE)
     def _(tile):
         here = lane_tile(tile)
-        lanes = half_lanes(place_ref, mine, half, tile * LANE, LANE)
+        lanes = half_lanes(mine, half, tile * LANE, LANE)
         for h in range(halves):
             rows, rows_im = pl.ds(h * SUB, SUB), pl.ds(modes + h * SUB, SUB)
             p = pole_ref[rows, lanes], pole_ref[rows_im, lanes]
@@ -372,57 +384,54 @@
     return tuple(jnp.where(flag, x, y) for x, y in zip(a, b))
 
 
-def first_kernel(lengths_ref, place_ref, kept_ref, came_ref, pole_ref, total_ref, send_ref, gate_ref, *, tokens):
-    starts = starts_of(lengths_ref, 0)
-    place = place_ref[0]
-    odd = (place & 1) == 1
-    second = place | 1
-    flag = none_in(starts, second * tokens, (second + 1) * tokens)
+def first_kernel(kept_ref, came_ref, pole_ref, flags_ref, total_ref, send_ref, gate_ref, *, tokens):
     half = kept_ref.shape[1]
+    rows_at = flag_rows(1)
+    shape = kept_ref.shape[0] // 2, CHUNK
 
     @pl.loop(0, half // CHUNK)
     def _(part):
+        def flag(name):
+            return jnp.broadcast_to(flags_ref[rows_at[name] : rows_at[name] + 1, :], shape)
+
         lanes = pl.ds(pl.multiple_of(part * CHUNK, LANE), CHUNK)
         kept, came = split(kept_ref, lanes), split(came_ref, lanes)
-        gate = split(pole_ref, half_lanes(place_ref, True, half, part * CHUNK, CHUNK))
+        gate = split(pole_ref, half_lanes(True, half, part * CHUNK, CHUNK))
+        odd = flag("odd") > 0.5
         reach = 1
         while reach < tokens:
             gate = cmul(*gate, *gate)
             reach *= 2
-        total = advance(gate, flag, choose(odd, came, kept), choose(odd, kept, came))
+        total = advance(gate, flag("second"), choose(odd, came, kept), choose(odd, kept, came))
         store(total_ref, lanes, total)
         store(send_ref, lanes, total)
         store(gate_ref, lanes, gate)
 
 
-def round_kernel(lengths_ref, place_ref, total_ref, met_ref, *refs, tokens, k, last):
-    starts = starts_of(lengths_ref, 0)
-    place = place_ref[0]
-    distance = 1 << k
-    upper = (place & distance) != 0
-    group = (place >> k) << k
-    even = (place >> 1) << 1
-    later = group | distance
-    enter = none_in(starts, group * tokens, even * tokens)
-    enter = jnp.where(upper, enter, 0.0)
-    whole = none_in(starts, later * tokens, (later + distance) * tokens)
-    flag = none_in(starts, even * tokens, (even + 1) * tokens)
+def round_kernel(total_ref, met_ref, flags_ref, *refs, k, rounds):
+    rows_at = flag_rows(rounds)
+    shape = met_ref.shape[0] // 2, CHUNK
 
     @pl.loop(0, met_ref.shape[1] // CHUNK)
     def _(part):
+        def flag(name):
+            return jnp.broadcast_to(flags_ref[rows_at[name] : rows_at[name] + 1, :], shape)
+
         lanes = pl.ds(pl.multiple_of(part * CHUNK, LANE), CHUNK)
         rest = list(refs)
         met, total = split(met_ref, lanes), split(total_ref, lanes)
         power = split(rest.pop(0), lanes)
+        enter = flag(("enter", k))
         if k == 1:
             prefix = tuple(enter * x for x in met)
         else:
             before, prefix = split(rest.pop(0), lanes), split(rest.pop(0), lanes)
             prefix = advance(before, enter, met, prefix)
-        if not last:
+        if k < rounds - 1:
             total_out, send_ref, power_out, before_out, prefix_out = rest
+            upper = flag(("upper", k)) > 0.5
             power = cmul(*power, *power)
-            total = advance(power, whole, choose(upper, met, total), choose(upper, total, met))
+            total = advance(power, flag(("whole", k)), choose(upper, met, total), choose(upper, total, met))
             store(total_out, lanes, total)
             store(send_ref, lanes, total)
             store(prefix_out, lanes, prefix)
@@ -434,24 +443,22 @@
             store(before_out, lanes, before)
         else:
             gate_ref, kept_ref, came_ref, own_ref, send_ref = rest
-            odd = (place & 1) == 1
+            odd = flag("odd") > 0.5
             kept, came = split(kept_ref, lanes), split(came_ref, lanes)
-            beyond = advance(split(gate_ref, lanes), flag, prefix, choose(odd, came, kept))
+            beyond = advance(split(gate_ref, lanes), flag("even"), prefix, choose(odd, came, kept))
             store(own_ref, lanes, choose(odd, beyond, prefix))
             store(send_ref, lanes, choose(odd, prefix, beyond))
 
 
-def back_kernel(place_ref, entry_ref, table_ref, local_ref, reach_ref, base_ref, gain_ref, *refs):
-    out_ref, state_s = refs[-2:]
-    tokens, width = out_ref.shape
+def back_kernel(entry_ref, table_ref, local_ref, reach_ref, base_ref, gain_ref, *refs, mine):
+    out_hbm, out_ref, state_s, sems = refs[-4:]
+    tokens, half = out_ref.shape
+    width = TILE
     count, packed, _ = local_ref.shape
     modes = packed // 2
     halves = modes // SUB
-    origin = pl.program_id(0) * width
-
     def one_tile(tile, state_s):
-        lanes = lane_tile(tile)
-        here = pl.ds(pl.multiple_of(origin + tile * LANE, LANE), LANE)
+        lanes = here = lane_tile(tile)
         entry = entry_ref[:, here].astype(F32)
         for h in range(halves):
             rows, rows_im = pl.ds(h * SUB, SUB), pl.ds(modes + h * SUB, SUB)
@@ -476,10 +483,22 @@
             carried = jnp.concatenate(sums[b], axis=0)
             out_ref[rows, lanes] = (base_ref[rows, here] + gain_ref[rows, here] * carried).astype(BF16)
 
-    @pl.loop(0, width // LANE // state_s.shape[0])
-    def _(step):
-        for v in range(state_s.shape[0]):
-            one_tile(step * state_s.shape[0] + v, state_s.at[v])
+    def leaving(j):
+        lanes = half_lanes(mine, half, j * width, width)
+        here = pl.ds(pl.multiple_of(j * width, LANE), width)
+        return pltpu.make_async_copy(out_ref.at[:, here], out_hbm.at[:, lanes], sems.at[j])
+
+    @pl.loop(0, half // width)
+    def _(j):
+        @pl.loop(0, width // LANE // state_s.shape[0])
+        def _(step):
+            for v in range(state_s.shape[0]):
+                one_tile(j * (width // LANE) + step * state_s.shape[0] + v, state_s.at[v])
+
+        leaving(j).start()
+
+    for j in range(half // width):
+        leaving(j).wait()
 
 
 def per_device(features, kernel, skip, residues, decay, freq, lengths):
@@ -491,7 +510,6 @@
     place = lax.axis_index("seq")
     core = place % 2
     rounds = n.bit_length() - 1
-    where = place.astype(jnp.int32)[None]
 
     rim = features[:, tokens - 2 :, :]
     halo = lax.ppermute(rim, "seq", [(i, (i + 1) % n) for i in range(n)])
@@ -502,7 +520,8 @@
     cosine = 1 + q * (-1 / 2 + q * (1 / 24 + q * (-1 / 720 + q * (1 / 40320 - q * (1 / 3628800)))))
     d = 2 * decay
     scale = jnp.sqrt(d * (1 - d * (1 / 2 - d * (1 / 6 - d * (1 / 24 - d * (1 / 120 - d * (1 / 720)))))))
-    pole = jnp.stack([fade * cosine, fade * sine]).reshape(2 * modes, width)
+    part = lax.broadcasted_iota(jnp.int32, (2, modes, width), 0)
+    pole = (fade * jnp.where(part == 0, cosine, sine)).reshape(2 * modes, width)
     coef = (residues * scale[None]).reshape(2 * modes, width)
 
     params = pltpu.CompilerParams(vmem_limit_bytes=16 * 1024 * 1024)
@@ -511,57 +530,46 @@
     shifts = pltpu.VMEM((2 * tokens, tokens), BF16)
     whole = pl.BlockSpec(memory_space=pltpu.VMEM)
 
-    def call(body, args, outs, name, scratch=(), cost=0.8e9):
+    def call(body, args, outs, name, scratch=(), cost=0.8e9, ragged=False, spec=whole, limit=params):
         return pl.pallas_call(
             body,
             grid_spec=pltpu.PrefetchScalarGridSpec(
-                num_scalar_prefetch=2, grid=(), in_specs=[whole] * len(args), out_specs=[whole] * len(outs),
+                num_scalar_prefetch=int(ragged), grid=(), in_specs=[spec] * len(args), out_specs=[whole] * len(outs),
                 scratch_shapes=scratch,
             ),
             out_shape=[jax.ShapeDtypeStruct(*o) for o in outs],
-            compiler_params=params, name=name,
+            compiler_params=limit, name=name,
             cost_estimate=pl.CostEstimate(flops=int(cost), bytes_accessed=1 << 20, transcendentals=0),
-        )(lengths, where, *args)
+        )(*((lengths,) if ragged else ()), *args)
 
     packed = 2 * modes
-    tiles = half // TILE
     state, sent = ((packed, half), F32), ((packed, half), BF16)
     blocks, plain = ((count, packed, half), F32), ((tokens, half), F32)
 
-    def tile_of(mine, i, w_ref):
-        core = w_ref[0] & 1
-        return (core if mine else 1 - core) * tiles + i
-
-    def front(mine, streams):
-        outs = [((tokens, half), BF16), blocks, sent]
-        scratch = [plane, shifts, pltpu.VMEM((TILE // LANE, tokens, LANE), F32)]
-        if not mine:
-            pair = (2, tokens, half)
-            outs = outs + [(pair, BF16)]
-            scratch = [pltpu.VMEM(pair, BF16), pltpu.SemaphoreType.DMA((2, half // TILE)),
-                       pltpu.SemaphoreType.DMA((2,))] + scratch
-        return pl.pallas_call(
-            functools.partial(front_kernel, mine=mine),
-            grid_spec=pltpu.PrefetchScalarGridSpec(
-                num_scalar_prefetch=2, grid=(),
-                in_specs=[whole if mine else pl.BlockSpec(memory_space=pl.ANY)] + [whole] * 3,
-                out_specs=[whole] * len(outs), scratch_shapes=scratch,
-            ),
-            out_shape=[jax.ShapeDtypeStruct(*o) for o in outs],
-            compiler_params=params if mine else roomy, name="front",
-            cost_estimate=pl.CostEstimate(flops=5_000_000_000, bytes_accessed=4 << 20, transcendentals=0),
-        )(lengths, where, streams, halo, kernel, pole)
+    flag_count = -(-len(flag_rows(rounds)) // SUB) * SUB
+    streams, shift, last_mask, flags = call(
+        functools.partial(prelude_kernel, rounds=rounds), (features,),
+        (((2, tokens, width), BF16), ((2 * tokens, tokens), BF16), ((tokens, LANE), F32), ((flag_count, CHUNK), F32)),
+        "prelude", [pltpu.SemaphoreType.DMA((2,))], ragged=True, spec=pl.BlockSpec(memory_space=pl.ANY), limit=roomy,
+        cost=1.2e9,
+    )
+
+    def front(mine):
+        return call(
+            functools.partial(front_kernel, mine=mine), (streams, halo, kernel, pole, shift, last_mask, flags),
+            (((tokens, half), BF16), blocks, sent), "front", [pltpu.VMEM((TILE // LANE, tokens, LANE), F32)], cost=5e9,
+        )
 
     def middle(mine, z):
         return call(
             functools.partial(middle_kernel, mine=mine), (features, halo, kernel, z, skip[None], pole, coef),
-            (plain, plain), "middle", [plane, plane, plane, pltpu.VMEM((2 * BLK, LANE), F32), plane, shifts, pltpu.VMEM((BLK, LANE), F32)], cost=5e9,
+            (plain, plain), "middle", [plane, plane, plane, pltpu.VMEM((2 * BLK, LANE), F32), plane, shifts, pltpu.VMEM((BLK, LANE), F32)], cost=5e9, ragged=True,
         )
 
     def prepare(mine, e):
         return call(
             functools.partial(prepare_kernel, mine=mine), (e, pole, coef),
-            (((packed, BLK, half), F32), blocks, blocks), "prepare", [pltpu.VMEM((BLK * PITCH, LANE), F32)], cost=4e9,
+            (((packed, BLK, half), F32), blocks, blocks), "prepare", [pltpu.VMEM((BLK * PITCH, LANE), F32)], cost=2.5e9, ragged=True,
         )
 
     def back(mine, args, out):
@@ -570,23 +578,21 @@
             args, specs = args + (out,), specs + [pl.BlockSpec(memory_space=pl.ANY)]
 
         return pl.pallas_call(
-            back_kernel,
-            grid_spec=pltpu.PrefetchScalarGridSpec(
-                num_scalar_prefetch=1, grid=(tiles,), in_specs=specs,
-                out_specs=pl.BlockSpec((tokens, TILE), lambda i, w_ref: (0, tile_of(mine, i, w_ref))),
-                scratch_shapes=[pltpu.VMEM((UNROLL, count * packed, LANE), F32)],
-            ),
+            functools.partial(back_kernel, mine=mine),
+            in_specs=specs, out_specs=pl.BlockSpec(memory_space=pl.ANY),
             out_shape=jax.ShapeDtypeStruct((tokens, width), BF16),
-            input_output_aliases={} if out is None else {len(args): 0},
+            scratch_shapes=[pltpu.VMEM((tokens, half), BF16), pltpu.VMEM((UNROLL, count * packed, LANE), F32),
+                            pltpu.SemaphoreType.DMA((half // TILE,))],
+            input_output_aliases={} if out is None else {len(args) - 1: 0},
             compiler_params=params, name="back",
             cost_estimate=pl.CostEstimate(flops=3_500_000_000, bytes_accessed=1 << 20, transcendentals=0),
-        )(where, *args)
-
-    z_other, e_other, end_other, streams = front(False, features)
+        )(*args)
+
+    z_other, e_other, end_other = front(False)
     came = exchange(end_other, 1)
-    z_own, e_own, end_own = front(True, streams)
+    z_own, e_own, end_own = front(True)
     total, send, gate = call(
-        functools.partial(first_kernel, tokens=tokens), (end_own, came, pole), (state, sent, state), "first"
+        functools.partial(first_kernel, tokens=tokens), (end_own, came, pole, flags), (state, sent, state), "first"
     )
     power, carry = gate, ()
     jobs = [lambda z: middle(True, z), lambda z: middle(False, z), lambda es: (*prepare(True, es[0]), *prepare(False, es[1]))]
@@ -599,8 +605,8 @@
             operand, send = lax.optimization_barrier((operand, send))
             met, done = lax.optimization_barrier((met, job(operand)))
             ready.append(done)
-        body = functools.partial(round_kernel, tokens=tokens, k=k, last=last)
-        args = (total, met, power, *carry)
+        body = functools.partial(round_kernel, k=k, rounds=rounds)
+        args = (total, met, flags, power, *carry)
         if last:
             own, send = call(body, args + (gate, end_own, came), (state, sent), "round")
         else:

time: 49.5 us -> 47.5 us (0.960)
  Pallas kernels: 35.9 us -> 31.7 us
  waiting for transfers between devices: 1.5 us -> 3.18 us
  local copies, waits for them, and re-layouts: 1.04 us -> 1.83 us
    pallas_call x4 -> x2, Pallas kernels: 17.8 us -> 7.23 us  [back(): pl.pallas_call(functools.partial(back_kernel, mine=mine), in_specs=specs,...]
    pallas_call x8 -> x11, Pallas kernels: 18.1 us -> 24.5 us  [call(): pl.pallas_call(body, grid_spec=pltpu.PrefetchScalarGridSpec(num_scalar_pr...]
    another operation x2 -> x0, other arithmetic: 2.53 us -> none  [per_device(): pole = jnp.stack([fade * cosine, fade * sine]).reshape(2 * modes, width)]
    ppermute x5, waiting for transfers between devices: 1.5 us -> 3.18 us  [exchange(): return lax.ppermute(block, 'seq', [(i, i ^ distance) for i in devices])]
    mul x0 -> x2, other arithmetic: none -> 1.19 us  [the longest x1 1.14 us: per_device(): pole = (fade * jnp.where(part == 0, cosine, sine)).reshape(2 * modes, width)]
    sqrt x0 -> x1, other arithmetic: none -> 1.14 us  [per_device(): jnp.sqrt(d * (1 - d * (1 / 2 - d * (1 / 6 - d * (1 / 24 - d * (1 / 120 -...]
    unnamed x8 -> x16, local copies, waits for them, and re-layouts: 0.02 us -> 0.69 us
  transfers between devices with their start and end apart: 6 -> 6, of which waited for: 1 -> 1; matrix products, arithmetic and copies ran while one was open for 5% -> 5% of each run, Pallas kernels for 47% -> 49%
where the time goes in v5:
time: 47.5 us; the launch traced here: 47.3 us
  Pallas kernels  31.7 us (67%)
  starting transfers between devices  7.98 us (17%)
  waiting for transfers between devices  3.18 us (7%)
  other arithmetic  2.34 us (5%)
  local copies, waits for them, and re-layouts  1.83 us (4%)
    pallas_call x11, Pallas kernels, call(): pl.pallas_call(body, grid_spec=pltpu.PrefetchScalarGridSpec(num_scalar_pr...  24.5 us
    pallas_call x2, Pallas kernels, back(): pl.pallas_call(functools.partial(back_kernel, mine=mine), in_specs=specs,...  7.23 us
    ppermute x5, starting transfers between devices, exchange(): return lax.ppermute(block, 'seq', [(i, i ^ distance) for i in devices])  5.3 us
    ppermute x5, waiting for transfers between devices, exchange(): return lax.ppermute(block, 'seq', [(i, i ^ distance) for i in devices])  3.18 us
    ppermute x1, starting transfers between devices, per_device(): halo = lax.ppermute(rim, 'seq', [(i, (i + 1) % n) for i in range(n)])  2.68 us
    mul x1, other arithmetic, per_device(): pole = (fade * jnp.where(part == 0, cosine, sine)).reshape(2 * modes, width)  1.14 us
    sqrt x1, other arithmetic, per_device(): jnp.sqrt(d * (1 - d * (1 / 2 - d * (1 / 6 - d * (1 / 24 - d * (1 / 120 -...  1.14 us
    slice x1, local copies, waits for them, and re-layouts, per_device(): rim = features[:, tokens - 2:, :]  0.98 us
  transfers between devices with their start and end apart: 6, of which 1 were waited for; matrix products, arithmetic and copies ran while one was open for 5% of the time, Pallas kernels for 49%

profile of v5, /device:TPU:1, one launch (start us, length us, event | category | flops | bytes accessed | tf_op | source)
XLA Modules:
  0.0 47.3 jit_solution(18157264023787191528)
XLA Ops:
  0.0 1.0 %slice.3 = bf16[3,2,4096]{2,1,0:T(2,128)(2,1)S(1)} slice(bf16[3,128,4096]{2,1,0:T(8,128)(2,1)} %features_ref.5), slice={[0:3], [126:128], [0:4096]} | slice | bytes 98304 | tf_op jit(solution)/shard_map/slice | solution.py:514
  1.0 2.7 %collective-permute-start = (bf16[3,2,4096]{2,1,0:T(2,128)(2,1)S(1)}, bf16[3,2,4096]{2,1,0:T(2,128)(2,1)S(1)}, u32[]{:S(2)}, u32[]{:S(2)}) collective-permute-start(bf16[3,2,4096]{2,1,0:T(2,128)(2,1)S(1)} %slice.3), channel_id=1, source_target_pairs={{0,1},{1,2},{2,3},{3,4},{4,5},{5,6},{6,7},{7,8},{8,9},{9,10},{10,1... | collective-permute-start | bytes 147464 | tf_op jit(solution)/shard_map/ppermute | solution.py:515
  3.7 0.7 %copy-done.3 = s32[6]{0:T(128)S(1)} copy-done((s32[6]{0:T(128)S(1)}, s32[6]{0:T(128)}, u32[]{:S(2)}) %copy-start.3) | copy-done | bytes 48
  4.3 2.1 %prelude.1 = (bf16[2,128,4096]{2,1,0:T(8,128)(2,1)S(1)}, bf16[256,128]{1,0:T(8,128)(2,1)S(1)}, f32[128,128]{1,0:T(8,128)S(1)}, f32[32,512]{1,0:T(8,128)S(1)}) custom-call(s32[6]{0:T(128)S(1)} %copy-done.3, bf16[3,128,4096]{2,1,0:T(8,128)(2,1)} %features_ref.5), custom_call_target="tpu_custom_call" | custom-call | flops 1200000000 | bytes 1048576 | tf_op jit(solution)/shard_map/prelude/pallas_call | solution.py:534
  6.5 1.1 %multiply_sqrt_fusion = (f32[16,4096]{1,0:T(8,128)S(1)}, f32[16,4096]{1,0:T(8,128)S(1)}, f32[16,4096]{1,0:T(8,128)}, f32[16,4096]{1,0:T(8,128)}) fusion(f32[16,4096]{1,0:T(8,128)S(1)} %copy-done.6, f32[16,4096]{1,0:T(8,128)S(1)} %copy-done.7), kind=kLoop, calls=%fused_computation.3 | loop fusion | flops 2162688 | bytes 1572864 | tf_op jit(solution)/shard_map/sqrt | solution.py:522
  7.7 0.1 iota.12
  7.8 1.1 %fusion.pole_ref = f32[32,4096]{1,0:T(8,128)S(1)} fusion(f32[16,4096]{1,0:T(8,128)} %get-tuple-element.113, f32[16,4096]{1,0:T(8,128)} %get-tuple-element.114, f32[16,4096]{1,0:T(8,128)S(1)} %get-tuple-element.110, pred[32]{0:T(512)(128)(4,1)S(1)} %iota.12), kind=kLoop, calls=%fused_computation.1 | loop fusion | flops 262144 | bytes 1310752 | tf_op jit(solution)/shard_map/mul | solution.py:524
  9.0 4.2 %front.3 = (bf16[128,2048]{1,0:T(8,128)(2,1)S(1)}, f32[8,32,2048]{2,1,0:T(8,128)S(1)}, bf16[32,2048]{1,0:T(8,128)(2,1)S(1)}) custom-call(bf16[2,128,4096]{2,1,0:T(8,128)(2,1)S(1)} %get-tuple-element.57.streams_ref, bf16[3,2,4096]{2,1,0:T(2,128)(2,1)S(1)} %collective-permute-done.halo_ref, f32[3,3,4096]{2,1,0:T(4,128)S(1)} %copy-done.1, ...), custom_call_target="tpu_custom_call" | custom-call | flops 5000000000 | bytes 1048576 | tf_op jit(solution)/shard_map/front/pallas_call | solution.py:534
  13.3 4.2 %front.2 = (bf16[128,2048]{1,0:T(8,128)(2,1)S(1)}, f32[8,32,2048]{2,1,0:T(8,128)S(1)}, bf16[32,2048]{1,0:T(8,128)(2,1)S(1)}) custom-call(bf16[2,128,4096]{2,1,0:T(8,128)(2,1)S(1)} %get-tuple-element.57.streams_ref, bf16[3,2,4096]{2,1,0:T(2,128)(2,1)S(1)} %collective-permute-done.halo_ref, f32[3,3,4096]{2,1,0:T(4,128)S(1)} %copy-done.1, ...), custom_call_target="tpu_custom_call" | custom-call | flops 5000000000 | bytes 1048576 | tf_op jit(solution)/shard_map/front/pallas_call | solution.py:534
  17.6 0.3 first.1
  17.9 1.3 %collective-permute-start.2 = (bf16[32,2048]{1,0:T(8,128)(2,1)S(1)}, bf16[32,2048]{1,0:T(8,128)(2,1)S(1)}, u32[]{:S(2)}, u32[]{:S(2)}) collective-permute-start(bf16[32,2048]{1,0:T(8,128)(2,1)S(1)} %get-tuple-element.64), channel_id=1, source_target_pairs={{0,2},{1,3},{2,0},{3,1},{4,6},{5,7},{6,4},{7,5},{8,10},{9,11},{10,... | collective-permute-start | bytes 393224 | tf_op jit(solution)/shard_map/ppermute | solution.py:25
  19.1 4.2 %middle.2 = (f32[128,2048]{1,0:T(8,128)S(1)}, f32[128,2048]{1,0:T(8,128)S(1)}) custom-call(s32[6]{0:T(128)S(1)} %copy-done.4, bf16[3,128,4096]{2,1,0:T(8,128)(2,1)S(1)} %copy-done, bf16[3,2,4096]{2,1,0:T(2,128)(2,1)S(1)} %collective-permute-done.halo_ref, f32[3,3,4096]{2,1,0:T(4,128)S(1)} %copy-done.1, bf16[128,2048]{1,0:T(8,128)(2,1)S(1)} %get-tuple-element.66.z_ref, ...), custom_call_target="tpu_custom_call" | custom-call | flops 5000000000 | bytes 1048576 | tf_op jit(solution)/shard_map/middle/pallas_call | solution.py:534
  23.4 0.2 round.3
  23.6 2.1 %collective-permute-start.3 = (bf16[32,2048]{1,0:T(8,128)(2,1)S(1)}, bf16[32,2048]{1,0:T(8,128)(2,1)S(1)}, u32[]{:S(2)}, u32[]{:S(2)}) collective-permute-start(bf16[32,2048]{1,0:T(8,128)(2,1)S(1)} %get-tuple-element.72), channel_id=1, source_target_pairs={{0,4},{1,5},{2,6},{3,7},{4,0},{5,1},{6,2},{7,3},{8,12},{9,13},{10,... | collective-permute-start | bytes 393224 | tf_op jit(solution)/shard_map/ppermute | solution.py:25
  25.7 4.2 %middle.3 = (f32[128,2048]{1,0:T(8,128)S(1)}, f32[128,2048]{1,0:T(8,128)S(1)}) custom-call(s32[6]{0:T(128)S(1)} %copy-done.4, bf16[3,128,4096]{2,1,0:T(8,128)(2,1)S(1)} %copy-done, bf16[3,2,4096]{2,1,0:T(2,128)(2,1)S(1)} %collective-permute-done.halo_ref, f32[3,3,4096]{2,1,0:T(4,128)S(1)} %copy-done.1, bf16[128,2048]{1,0:T(8,128)(2,1)S(1)} %get-tuple-element.74.z_ref, ...), custom_call_target="tpu_custom_call" | custom-call | flops 5000000000 | bytes 1048576 | tf_op jit(solution)/shard_map/middle/pallas_call | solution.py:534
  29.9 0.2 round.4
  30.1 0.8 %collective-permute-start.4 = (bf16[32,2048]{1,0:T(8,128)(2,1)S(1)}, bf16[32,2048]{1,0:T(8,128)(2,1)S(1)}, u32[]{:S(2)}, u32[]{:S(2)}) collective-permute-start(bf16[32,2048]{1,0:T(8,128)(2,1)S(1)} %get-tuple-element.82), channel_id=1, source_target_pairs={{0,8},{1,9},{2,10},{3,11},{4,12},{5,13},{6,14},{7,15},{8,0},{9,1},... | collective-permute-start | bytes 393224 | tf_op jit(solution)/shard_map/ppermute | solution.py:25
  30.9 2.4 %prepare.2 = (f32[32,16,2048]{2,1,0:T(8,128)S(1)}, f32[8,32,2048]{2,1,0:T(8,128)S(1)}, f32[8,32,2048]{2,1,0:T(8,128)S(1)}) custom-call(s32[6]{0:T(128)S(1)} %copy-done.4, f32[8,32,2048]{2,1,0:T(8,128)S(1)} %get-tuple-element.85.e_ref, f32[32,4096]{1,0:T(8,128)S(1)} %fusion.pole_ref, f32[32,4096]{1,0:T(8,128)S(1)} %bitcast.12), custom_call_target="tpu_custom_call" | custom-call | flops 2500000000 | bytes 1048576 | tf_op jit(solution)/shard_map/prepare/pallas_call | solution.py:534
  33.3 2.3 %prepare.3 = (f32[32,16,2048]{2,1,0:T(8,128)S(1)}, f32[8,32,2048]{2,1,0:T(8,128)S(1)}, f32[8,32,2048]{2,1,0:T(8,128)S(1)}) custom-call(s32[6]{0:T(128)S(1)} %copy-done.4, f32[8,32,2048]{2,1,0:T(8,128)S(1)} %get-tuple-element.89.e_ref, f32[32,4096]{1,0:T(8,128)S(1)} %fusion.pole_ref, f32[32,4096]{1,0:T(8,128)S(1)} %bitcast.13), custom_call_target="tpu_custom_call" | custom-call | flops 2500000000 | bytes 1048576 | tf_op jit(solution)/shard_map/prepare/pallas_call | solution.py:534
  35.6 3.2 %collective-permute-done.4.met_ref = bf16[32,2048]{1,0:T(8,128)(2,1)S(1)} collective-permute-done((bf16[32,2048]{1,0:T(8,128)(2,1)S(1)}, bf16[32,2048]{1,0:T(8,128)(2,1)S(1)}, u32[]{:S(2)}, u32[]{:S(2)}) %collective-permute-start.4) | collective-permute-done | bytes 131104 | tf_op jit(solution)/shard_map/ppermute | solution.py:25
  38.8 0.2 round.5
  39.0 1.1 %collective-permute-start.5 = (bf16[32,2048]{1,0:T(8,128)(2,1)S(1)}, bf16[32,2048]{1,0:T(8,128)(2,1)S(1)}, u32[]{:S(2)}, u32[]{:S(2)}) collective-permute-start(bf16[32,2048]{1,0:T(8,128)(2,1)S(1)} %get-tuple-element.97), channel_id=1, source_target_pairs={{0,1},{1,0},{2,3},{3,2},{4,5},{5,4},{6,7},{7,6},{8,9},{9,8},{10,11... | collective-permute-start | bytes 393224 | tf_op jit(solution)/shard_map/ppermute | solution.py:25
  40.0 3.6 %back.2.refs_0_ = bf16[128,4096]{1,0:T(8,128)(2,1)} custom-call(f32[32,2048]{1,0:T(8,128)S(1)} %get-tuple-element.103.entry_ref, f32[32,16,2048]{2,1,0:T(8,128)S(1)} %get-tuple-element.104.table_ref, f32[8,32,2048]{2,1,0:T(8,128)S(1)} %get-tuple-element.105.local_ref, f32[8,32,2048]{2,1,0:T(8,128)S(1)} %get-tuple-element.106.reach_ref, ...), custom_call_target="tpu_custom_call" | custom-call | flops 3500000000 | bytes 1048576 | tf_op jit(solution)/shard_map/back/pallas_call | solution.py:580
  43.7 3.6 %back.3 = bf16[128,4096]{1,0:T(8,128)(2,1)} custom-call(bf16[32,2048]{1,0:T(8,128)(2,1)S(1)} %collective-permute-done.5.entry_ref, f32[32,16,2048]{2,1,0:T(8,128)S(1)} %get-tuple-element.98.table_ref, f32[8,32,2048]{2,1,0:T(8,128)S(1)} %get-tuple-element.99.local_ref, ...), custom_call_target="tpu_custom_call", output_to_operand_aliasing={{}: (6, {})} | custom-call | flops 3500000000 | bytes 1048576 | tf_op jit(solution)/shard_map/back/pallas_call | solution.py:580
  (24 shorter events, 0.3 us)
Async XLA Ops:
  1.0 8.0 %collective-permute-start = (bf16[3,2,4096]{2,1,0:T(2,128)(2,1)S(1)}, bf16[3,2,4096]{2,1,0:T(2,128)(2,1)S(1)}, u32[]{:S(2)}, u32[]{:S(2)}) collective-permute-start(bf16[3,2,4096]{2,1,0:T(2,128)(2,1)S(1)} %slice.3), channel_id=1, source_target_pairs={{0,1},{1,2},{2,3},{3,4},{4,5},{5,6},{6,7},{7,8},{8,9},{9,10},{10,1... | collective-permute-start | bytes 147464 | tf_op jit(solution)/shard_map/ppermute | solution.py:515
  3.7 0.7 %copy-start.3 = (s32[6]{0:T(128)S(1)}, s32[6]{0:T(128)}, u32[]{:S(2)}) copy-start(s32[6]{0:T(128)} %lengths_ref.9) | copy-start | bytes 76
  4.3 2.1 %copy-start.6 = (f32[16,4096]{1,0:T(8,128)S(1)}, f32[16,4096]{1,0:T(8,128)}, u32[]{:S(2)}) copy-start(f32[16,4096]{1,0:T(8,128)} %param.11) | copy-start | bytes 786436
  4.3 2.1 %copy-start.7 = (f32[16,4096]{1,0:T(8,128)S(1)}, f32[16,4096]{1,0:T(8,128)}, u32[]{:S(2)}) copy-start(f32[16,4096]{1,0:T(8,128)} %param.12) | copy-start | bytes 786436
  4.3 3.3 %copy-start.5 = (f32[2,16,4096]{2,1,0:T(8,128)S(1)}, f32[2,16,4096]{2,1,0:T(8,128)}, u32[]{:S(2)}) copy-start(f32[2,16,4096]{2,1,0:T(8,128)} %param.10) | copy-start | bytes 1572868
  6.5 2.5 %copy-start.1 = (f32[3,3,4096]{2,1,0:T(4,128)S(1)}, f32[3,3,4096]{2,1,0:T(4,128)}, u32[]{:S(2)}) copy-start(f32[3,3,4096]{2,1,0:T(4,128)} %taps_ref.7) | copy-start | bytes 442372
  13.2 4.3 %collective-permute-start.1 = (bf16[32,2048]{1,0:T(8,128)(2,1)S(1)}, bf16[32,2048]{1,0:T(8,128)(2,1)S(1)}, u32[]{:S(2)}, u32[]{:S(2)}) collective-permute-start(bf16[32,2048]{1,0:T(8,128)(2,1)S(1)} %get-tuple-element.62), channel_id=1, source_target_pairs={{0,1},{1,0},{2,3},{3,2},{4,5},{5,4},{6,7},{7,6},{8,9},{9,8},{10,11... | collective-permute-start | bytes 393224 | tf_op jit(solution)/shard_map/ppermute | solution.py:25
  13.3 5.8 %copy-start = (bf16[3,128,4096]{2,1,0:T(8,128)(2,1)S(1)}, bf16[3,128,4096]{2,1,0:T(8,128)(2,1)}, u32[]{:S(2)}) copy-start(bf16[3,128,4096]{2,1,0:T(8,128)(2,1)} %features_ref.5) | copy-start | bytes 9437188
  17.5 1.6 %copy-start.2 = (f32[4096]{0:T(1024)S(1)}, f32[4096]{0:T(1024)}, u32[]{:S(2)}) copy-start(f32[4096]{0:T(1024)} %param.9) | copy-start | bytes 49156
  17.6 1.6 %copy-start.4 = (s32[6]{0:T(128)S(1)}, s32[6]{0:T(128)}, u32[]{:S(2)}) copy-start(s32[6]{0:T(128)} %lengths_ref.9) | copy-start | bytes 76
  17.9 5.5 %collective-permute-start.2 = (bf16[32,2048]{1,0:T(8,128)(2,1)S(1)}, bf16[32,2048]{1,0:T(8,128)(2,1)S(1)}, u32[]{:S(2)}, u32[]{:S(2)}) collective-permute-start(bf16[32,2048]{1,0:T(8,128)(2,1)S(1)} %get-tuple-element.64), channel_id=1, source_target_pairs={{0,2},{1,3},{2,0},{3,1},{4,6},{5,7},{6,4},{7,5},{8,10},{9,11},{10,... | collective-permute-start | bytes 393224 | tf_op jit(solution)/shard_map/ppermute | solution.py:25
  23.6 6.3 %collective-permute-start.3 = (bf16[32,2048]{1,0:T(8,128)(2,1)S(1)}, bf16[32,2048]{1,0:T(8,128)(2,1)S(1)}, u32[]{:S(2)}, u32[]{:S(2)}) collective-permute-start(bf16[32,2048]{1,0:T(8,128)(2,1)S(1)} %get-tuple-element.72), channel_id=1, source_target_pairs={{0,4},{1,5},{2,6},{3,7},{4,0},{5,1},{6,2},{7,3},{8,12},{9,13},{10,... | collective-permute-start | bytes 393224 | tf_op jit(solution)/shard_map/ppermute | solution.py:25
  30.1 8.7 %collective-permute-start.4 = (bf16[32,2048]{1,0:T(8,128)(2,1)S(1)}, bf16[32,2048]{1,0:T(8,128)(2,1)S(1)}, u32[]{:S(2)}, u32[]{:S(2)}) collective-permute-start(bf16[32,2048]{1,0:T(8,128)(2,1)S(1)} %get-tuple-element.82), channel_id=1, source_target_pairs={{0,8},{1,9},{2,10},{3,11},{4,12},{5,13},{6,14},{7,15},{8,0},{9,1},... | collective-permute-start | bytes 393224 | tf_op jit(solution)/shard_map/ppermute | solution.py:25
  39.0 4.7 %collective-permute-start.5 = (bf16[32,2048]{1,0:T(8,128)(2,1)S(1)}, bf16[32,2048]{1,0:T(8,128)(2,1)S(1)}, u32[]{:S(2)}, u32[]{:S(2)}) collective-permute-start(bf16[32,2048]{1,0:T(8,128)(2,1)S(1)} %get-tuple-element.97), channel_id=1, source_target_pairs={{0,1},{1,0},{2,3},{3,2},{4,5},{5,4},{6,7},{7,6},{8,9},{9,8},{10,11... | collective-permute-start | bytes 393224 | tf_op jit(solution)/shard_map/ppermute | solution.py:25
